TPU v7x, 32 devices: a whole 2x2x4 slice. The times are simulated.
32 devices in a mesh: pair: 8 (over z, core), aux: 4 (over y, x).
Axes of the slice: x: 2, y: 2, z: 4, core: 2. Of those that a mesh axis runs over, the one named last changes fastest.
Arguments:
- factors: bfloat16 [384, 16, 64, 128], P('aux', 'pair'), may hold values from -1.75 to 1.75
- pairs: int32 [80, 2], replicated, may hold values from 0 to 15, as said below
- shared: int32 [80, 4], P(None, 'aux'), may hold values 0 or 1
- owners: int32 [80], replicated, may hold values from 0 to 7, as said below
Outputs:
- exchange_matrix: float32 [16, 128, 2048], P('pair', 'aux')
- pair_tiles: float32 [8, 40, 128, 128], P('pair', None, 'aux')
Inputs may be any that keep to these rules, and one draw needn't show every extreme that they name: Distinct pairs (a, b) with a <= b. `owners`: each device owns at most 40 pairs and one device owns exactly 40.
All inputs are finite; a program needn't handle non-finite values. No bound on the sum of `shared` on one device may be relied on, other than what follows from the above.
Results may differ from a plain program's by a relative error of at most 0.0003.
Values may be sent and summed in bfloat16 or wider, within the bound.
No kernel may reach another device: no remote copies, remote signals or barrier semaphores. Data moves between devices by JAX's collectives and lax.ppermute only.
A program may use at most 128 MiB of HBM per device.

v0:
```python
import jax
import jax.numpy as jnp
from jax import lax
from jax.sharding import PartitionSpec as P


def body(factors, pairs, shared, owners):
    aux_rows, tiles_here, orbitals, tile_width = factors.shape
    owner_count = lax.axis_size("pair")
    tile_count = tiles_here * owner_count
    basis_count = tile_count * tile_width
    pair_count = pairs.shape[0]
    shard_rows = tile_width // lax.axis_size("aux")
    myself = lax.axis_index("pair")
    column = lax.axis_index("aux")
    slot_count = 4 * (pair_count // owner_count)
    pair_ids = jnp.arange(pair_count, dtype=jnp.int32)
    same_owner = owners[:, None] == owners[None, :]
    owner_rank = jnp.sum(
        (same_owner & (pair_ids[None, :] < pair_ids[:, None])).astype(jnp.int32), axis=1
    )
    slot_ids = jnp.arange(slot_count, dtype=jnp.int32)
    matches = (owners[None, :] == myself) & (owner_rank[None, :] == slot_ids[:, None])
    picked = jnp.sum(jnp.where(matches, pair_ids[None, :], 0), axis=1)
    live_slot = jnp.any(matches, axis=1).astype(jnp.float32)
    left_ids = pairs[picked, 0]
    right_ids = pairs[picked, 1]
    weights = live_slot * shared[picked, 0].astype(jnp.float32)
    gathered = lax.all_gather(factors, "pair", axis=1, tiled=True)

    def contract(slot_item):
        left_id, right_id, slot_scale = slot_item
        left_block = lax.dynamic_index_in_dim(gathered, left_id, 1, keepdims=False).reshape(
            aux_rows * orbitals, tile_width
        )
        right_block = lax.dynamic_index_in_dim(gathered, right_id, 1, keepdims=False).reshape(
            aux_rows * orbitals, tile_width
        )
        product = lax.dot_general(
            left_block, right_block, (((0,), (0,)), ((), ())), preferred_element_type=jnp.float32
        )
        return product * slot_scale

    partial_tiles = lax.map(contract, (left_ids, right_ids, weights))
    summed = lax.psum(partial_tiles, "aux")
    direct = lax.dynamic_slice_in_dim(summed, column * shard_rows, shard_rows, 1)
    mirror = lax.dynamic_slice_in_dim(
        jnp.swapaxes(summed, 1, 2), column * shard_rows, shard_rows, 1
    )
    tile_ids = jnp.arange(tile_count, dtype=jnp.int32)
    off_diagonal = live_slot * (left_ids != right_ids).astype(jnp.float32)
    left_hot = (left_ids[:, None] == tile_ids[None, :]).astype(jnp.float32)
    right_hot = (right_ids[:, None] == tile_ids[None, :]).astype(jnp.float32)
    upper_part = jnp.einsum(
        "jt,jc,jrm->trcm",
        left_hot * live_slot[:, None],
        right_hot,
        direct,
        precision=lax.Precision.HIGHEST,
    )
    lower_part = jnp.einsum(
        "jt,jc,jrm->trcm",
        right_hot * off_diagonal[:, None],
        left_hot,
        mirror,
        precision=lax.Precision.HIGHEST,
    )
    contribution = (upper_part + lower_part).reshape(tile_count, shard_rows, basis_count)
    matrix_rows = lax.psum_scatter(contribution, "pair", scatter_dimension=0, tiled=True)
    owned_tiles = direct[None]
    return (matrix_rows, owned_tiles)


def solution(mesh):
    placed = (P("aux", "pair", None, None), P(), P(None, "aux"), P())
    return jax.shard_map(
        body,
        mesh=mesh,
        in_specs=placed,
        out_specs=(P("pair", "aux", None), P("pair", None, "aux", None)),
        check_vma=False,
    )
```

profile of v0, /device:TPU:0, one launch (start us, length us, event | category | flops | bytes accessed | tf_op | source)
XLA Modules:
  0.0 886.6 jit_solution(12804275647070934509)
XLA Ops:
  7.2 4.4 copy.20
  15.7 218.7 %all-gather.2.cloned.1.call-done = bf16[96,16,64,128]{3,2,0,1:T(8,128)(2,1)} async-done(((bf16[96,2,64,128]{3,2,0,1:T(8,128)(2,1)}), bf16[96,16,64,128]{3,2,0,1:T(8,128)(2,1)}) %all-gather.2.cloned.1.call-update) | async-done | bytes 25165840 | tf_op jit(solution)/shard_map/all_gather | solution.py:29
  234.4 26.9 %copy.21 = bf16[96,16,64,128]{3,0,2,1:T(8,128)(2,1)} copy(bf16[96,16,64,128]{3,2,0,1:T(8,128)(2,1)} %all-gather.2.cloned.1.call-done) | data formatting | bytes 50331648 | tf_op jit(solution)/shard_map/while | solution.py:44
  261.3 470.7 %while.10 = (s32[]{:T(128)}, f32[40,128,128]{2,0,1:T(8,128)}, s32[40]{0:T(128)S(1)}, bf16[96,16,64,128]{3,0,2,1:T(8,128)(2,1)}, s32[40]{0:T(128)S(1)}, /*index=5*/f32[40]{0:T(128)S(1)}, s32[]{:T(128)}, s32[]{:T(128)}, s32[]{:T(128)}) while((s32[]{:T(128)}, f32[40,128,128]{2,0,1:T(8,128)}, s32[40]{0:T(128)S(1)}, ...), condition=%wide.region_4.5_spmd, body=%wide.region_3.4_spmd.sunk | while | flops 201342976 | bytes 3343057 | solution.py:44
  266.9 3.1 fusion.42
  278.7 3.1 fusion.42
  290.4 3.2 fusion.42
  302.2 3.1 fusion.42
  314.0 3.1 fusion.42
  325.7 3.1 fusion.42
  337.5 3.1 fusion.42
  349.3 3.1 fusion.42
  361.0 3.1 fusion.42
  372.8 3.1 fusion.42
  384.6 3.1 fusion.42
  396.4 3.1 fusion.42
  408.2 3.1 fusion.42
  420.0 3.1 fusion.42
  431.8 3.1 fusion.42
  443.6 3.1 fusion.42
  455.4 3.1 fusion.42
  467.1 3.1 fusion.42
  478.9 3.1 fusion.42
  490.7 3.1 fusion.42
  502.4 3.1 fusion.42
  514.2 3.1 fusion.42
  525.9 3.1 fusion.42
  537.7 3.1 fusion.42
  549.4 3.1 fusion.42
  561.2 3.1 fusion.42
  572.9 3.1 fusion.42
  584.7 3.1 fusion.42
  596.4 3.1 fusion.42
  608.1 3.1 fusion.42
  619.9 3.1 fusion.42
  631.6 3.1 fusion.42
  643.4 3.1 fusion.42
  666.9 3.1 fusion.42
  678.7 3.1 fusion.42
  690.5 3.1 fusion.42
  714.1 3.1 fusion.42
  725.9 3.1 fusion.42
  732.3 76.5 %all-reduce.4.cloned.1.call-done = f32[40,128,128]{2,0,1:T(8,128)} async-done(((f32[40,128,128]{2,0,1:T(8,128)}), f32[40,128,128]{2,0,1:T(8,128)}) %all-reduce.4.cloned.1.call-update) | async-done | bytes 2621456 | tf_op jit(solution)/shard_map/psum | solution.py:45
  813.6 3.4 fusion.17
  817.0 3.6 add_bitcast_fusion
  820.6 4.4 copy.24
  825.0 4.9 reshape.48
  830.9 49.2 %reduce-scatter.2.cloned.1.call-done = f32[2,32,2048]{2,1,0:T(8,128)} async-done(((f32[16,32,2048]{2,1,0:T(8,128)}), f32[2,32,2048]{2,1,0:T(8,128)}) %reduce-scatter.2.cloned.1.call-update) | async-done | bytes 524304 | tf_op jit(solution)/shard_map/reduce_scatter | solution.py:69
  (195 shorter events, 205.7 us)
Async XLA Ops:
  7.2 5.4 copy-start
  7.2 227.2 %all-gather.2.cloned.1.call-start = ((), (), s32[]{:S(2)}) async-start(), calls=%async_computation.1 | async-start | bytes 28311552 | tf_op jit(solution)/shard_map/all_gather | solution.py:29
  11.6 0.7 copy-start.3
  11.6 3.1 copy-start.2
  11.6 797.1 %all-reduce.4.cloned.1.call-start = ((), (), s32[]{:S(2)}) async-start(), calls=%async_computation.2 | async-start | bytes 5242880 | tf_op jit(solution)/shard_map/psum | solution.py:45
  732.0 148.1 %reduce-scatter.2.cloned.1.call-start = ((), (), s32[]{:S(2)}) async-start(), calls=%async_computation.3 | async-start | bytes 4718592 | tf_op jit(solution)/shard_map/reduce_scatter | solution.py:69
  825.0 55.1 %copy-start.1 = (s32[80,2]{0,1:T(2,128)S(1)}, s32[80,2]{0,1:T(2,128)}, u32[]{:S(2)}) copy-start(s32[80,2]{0,1:T(2,128)} %param.7) | copy-start | bytes 1924
Sparse Core Ops, SparseCore 0:
  11.8 222.5 all-gather.1
  732.1 76.6 all-reduce.3
  830.1 49.9 reduce-scatter.1
where the time goes:
time: 891 us; the launch traced here: 887 us
  waiting for transfers between devices  344 us (39%)
  local copies, waits for them, and re-layouts  239 us (27%)
  loops' own time  156 us (18%)
  matrix products  133 us (15%)
  between operations  13.9 us (2%)
    all_gather x1, waiting for transfers between devices, body(): gathered = lax.all_gather(factors, 'pair', axis=1, tiled=True)  219 us
    another operation x1, loops' own time, body(): partial_tiles = lax.map(contract, (left_ids, right_ids, weights))  156 us
    dot_general x40, matrix products, contract(): lax.dot_general(left_block, right_block, (((0,), (0,)), ((), ())), prefer...  126 us
    dynamic_update_slice x40, local copies, waits for them, and re-layouts, body(): partial_tiles = lax.map(contract, (left_ids, right_ids, weights))  119 us
    psum x1, waiting for transfers between devices, body(): summed = lax.psum(partial_tiles, 'aux')  76.5 us
    dynamic_slice x120, local copies, waits for them, and re-layouts, body(): partial_tiles = lax.map(contract, (left_ids, right_ids, weights))  70.4 us
    reduce_scatter x1, waiting for transfers between devices, body(): lax.psum_scatter(contribution, 'pair', scatter_dimension=0, tiled=True)  49.2 us
    while x1, local copies, waits for them, and re-layouts, body(): partial_tiles = lax.map(contract, (left_ids, right_ids, weights))  26.9 us
  transfers between devices with their start and end apart: 3, of which 3 were waited for; matrix products, arithmetic and copies ran while one was open for 0% of the time, Pallas kernels for 0%

commit v1 on v0

v1 whole, which is shorter than its diff:
```python
import jax
import jax.numpy as jnp
from jax import lax
from jax.experimental import pallas as pl
from jax.experimental.pallas import tpu as pltpu
from jax.sharding import PartitionSpec as P

VMEM_LIMIT = 48 << 20


def swap(value, axis, size, step):
    return lax.ppermute(value, axis, [(i, i ^ step) for i in range(size)])


def contract_kernel(left, right, weight, *refs):
    *parts, out, plain, turned = refs
    count = out.shape[0]
    depth, here, orbitals, width = parts[0].shape
    for step, part in enumerate(parts):
        for tile in range(here):
            block = part[:, tile].reshape(depth * orbitals, width)
            plain[step * here + tile] = block
            turned[step * here + tile] = block.T

    def one(index, carry):
        @pl.when(weight[index] != 0)
        def _():
            out[index] = jnp.dot(
                turned[left[index]], plain[right[index]], preferred_element_type=jnp.float32
            )

        @pl.when(weight[index] == 0)
        def _():
            out[index] = jnp.zeros((width, width), jnp.float32)

        return carry

    lax.fori_loop(0, count, one, 0)


def contract(parts, left, right, weight):
    depth, here, orbitals, width = parts[0].shape
    tiles = len(parts) * here
    count = left.shape[0]
    return pl.pallas_call(
        contract_kernel,
        out_shape=jax.ShapeDtypeStruct((count, width, width), jnp.float32),
        grid_spec=pltpu.PrefetchScalarGridSpec(
            num_scalar_prefetch=3,
            grid=(),
            in_specs=[pl.BlockSpec(memory_space=pltpu.VMEM)] * len(parts),
            out_specs=pl.BlockSpec(memory_space=pltpu.VMEM),
            scratch_shapes=[
                pltpu.VMEM((tiles, depth * orbitals, width), jnp.bfloat16),
                pltpu.VMEM((tiles, width, depth * orbitals), jnp.bfloat16),
            ],
        ),
        compiler_params=pltpu.CompilerParams(vmem_limit_bytes=VMEM_LIMIT),
    )(left, right, weight, *parts)


def turn_kernel(source, out):
    for group in range(source.shape[0]):
        out[group] = source[group].T


def turn(source):
    return pl.pallas_call(
        turn_kernel,
        out_shape=jax.ShapeDtypeStruct(source.shape, source.dtype),
        in_specs=[pl.BlockSpec(memory_space=pltpu.VMEM)],
        out_specs=pl.BlockSpec(memory_space=pltpu.VMEM),
        compiler_params=pltpu.CompilerParams(vmem_limit_bytes=VMEM_LIMIT),
    )(source)


def place_kernel(columns, kinds, sources, slots, direct, mirror, matrix, tiles):
    here, rows, _ = matrix.shape
    width = direct.shape[-1]
    columns_here = mirror.shape[0]
    pack = width // rows
    tile_count = matrix.shape[2] // width
    lane = lax.broadcasted_iota(jnp.int32, (rows, width), 1) // rows
    for tile in range(here):

        def one(other, carry):
            spot = tile * tile_count + other
            kind = kinds[spot]
            source = sources[spot]
            target = pl.ds(pl.multiple_of(other * width, width), width)

            @pl.when(kind == 0)
            def _():
                matrix[tile, :, target] = jnp.zeros((rows, width), jnp.float32)

            @pl.when(kind == 1)
            def _():
                matrix[tile, :, target] = direct[source]

            @pl.when(kind == 2)
            def _():
                group = source // pack
                place = source - group * pack
                total = jnp.zeros((rows, width), jnp.float32)
                for step in range(columns_here):
                    column = columns[step]
                    shift = ((column - place + pack) % pack) * rows
                    moved = pltpu.roll(mirror[step, group], shift, 1)
                    total = jnp.where(lane == column, moved, total)
                matrix[tile, :, target] = total

            return carry

        lax.fori_loop(0, tile_count, one, 0)

    def fill(slot, carry):
        source = slots[slot]

        @pl.when(source < 0)
        def _():
            tiles[0, slot] = jnp.zeros((rows, width), jnp.float32)

        @pl.when(source >= 0)
        def _():
            tiles[0, slot] = direct[source]

        return carry

    lax.fori_loop(0, tiles.shape[1], fill, 0)


def place(columns, kinds, sources, slots, direct, mirror, here, tile_count):
    _, rows, width = direct.shape
    return pl.pallas_call(
        place_kernel,
        out_shape=(
            jax.ShapeDtypeStruct((here, rows, tile_count * width), jnp.float32),
            jax.ShapeDtypeStruct((1, slots.shape[0], rows, width), jnp.float32),
        ),
        grid_spec=pltpu.PrefetchScalarGridSpec(
            num_scalar_prefetch=4,
            grid=(),
            in_specs=[pl.BlockSpec(memory_space=pltpu.VMEM)] * 2,
            out_specs=[pl.BlockSpec(memory_space=pltpu.VMEM)] * 2,
        ),
        compiler_params=pltpu.CompilerParams(vmem_limit_bytes=VMEM_LIMIT),
    )(columns, kinds, sources, slots, direct, mirror)


def take(value, index):
    return lax.dynamic_index_in_dim(value, index, 0, keepdims=False)


def body(factors, pairs, shared, owners):
    aux_rows, here, orbitals, width = factors.shape
    pair_size = lax.axis_size("pair")
    aux_size = lax.axis_size("aux")
    chips = pair_size // 2
    tile_count = here * pair_size
    pair_count = pairs.shape[0]
    rows = width // aux_size
    slot_count = 4 * (pair_count // pair_size)
    me = lax.axis_index("pair")
    core = me % 2
    chip = me // 2
    column = lax.axis_index("aux")
    depth = aux_rows // pair_size
    pack = aux_size
    unit = max(pack, chips)
    half = -(-(-(-pair_count // 2)) // unit) * unit
    share = half // chips
    padded = 2 * half

    pair_ids = jnp.arange(pair_count, dtype=jnp.int32)
    lefts, rights = pairs[:, 0], pairs[:, 1]
    same_owner = owners[:, None] == owners[None, :]
    rank = jnp.sum(
        (same_owner & (pair_ids[None, :] < pair_ids[:, None])).astype(jnp.int32), axis=1
    )
    left_slots = ((lefts // here) ^ me) * here + lefts % here
    right_slots = ((rights // here) ^ me) * here + rights % here
    weights = shared[:, 0]
    tables = jnp.pad(
        jnp.stack([left_slots, right_slots, weights]), ((0, 0), (0, padded - pair_count))
    ).reshape(3, 2, half)
    mine = lax.dynamic_index_in_dim(tables, core, 1, keepdims=False)
    theirs = lax.dynamic_index_in_dim(tables, 1 - core, 1, keepdims=False)

    local = pair_ids % half
    part_core = pair_ids // half
    final_pos = (part_core ^ core) * half + ((local // share) ^ chip) * share + local % share
    my_rows = me * here + jnp.arange(here, dtype=jnp.int32)
    others = jnp.arange(tile_count, dtype=jnp.int32)
    is_direct = (lefts == my_rows[:, None, None]) & (rights == others[None, :, None])
    is_mirror = (rights == my_rows[:, None, None]) & (lefts == others[None, :, None])
    any_direct = jnp.any(is_direct, axis=-1)
    any_mirror = jnp.any(is_mirror, axis=-1)
    kinds = jnp.where(any_direct, 1, jnp.where(any_mirror, 2, 0)).astype(jnp.int32).reshape(-1)
    chosen = jnp.where(any_direct[..., None], is_direct, is_mirror)
    sources = jnp.sum(jnp.where(chosen, final_pos, 0), axis=-1).astype(jnp.int32).reshape(-1)
    slot_ids = jnp.arange(slot_count, dtype=jnp.int32)
    matches = (owners[None, :] == me) & (rank[None, :] == slot_ids[:, None])
    slots = jnp.sum(jnp.where(matches, final_pos + 1, 0), axis=1).astype(jnp.int32) - 1
    columns = column ^ jnp.arange(aux_size, dtype=jnp.int32)

    pieces = factors.reshape(pair_size, depth, here, orbitals, width)
    parts = [take(pieces, me)]
    for step in range(1, pair_size):
        parts.append(swap(take(pieces, me ^ step), "pair", pair_size, step))

    given = contract(parts, *theirs)
    kept = contract(parts, *mine)
    chip_sum = kept + swap(given, "pair", pair_size, 1)

    by_column = chip_sum.reshape(half, aux_size, rows, width)

    def column_rows(step):
        return lax.dynamic_index_in_dim(by_column, column ^ step, 1, keepdims=False)

    summed = column_rows(0)
    arrived = [swap(column_rows(step), "aux", aux_size, step) for step in range(1, aux_size)]
    for value in arrived:
        summed = summed + value

    by_chip = summed.reshape(chips, share, rows, width)
    arrived = [
        swap(take(by_chip, chip ^ step), "pair", pair_size, 2 * step) for step in range(1, chips)
    ]
    total = take(by_chip, chip)
    for value in arrived:
        total = total + value

    line = [total] + [swap(total, "pair", pair_size, 2 * step) for step in range(1, chips)]
    own_direct = jnp.concatenate(line, axis=0)
    other_direct = swap(own_direct, "pair", pair_size, 1)

    turned = turn(own_direct.reshape(half // pack, pack * rows, width))
    turned = turned.reshape(half // pack, aux_size, rows, width)

    def turned_rows(step):
        return lax.dynamic_index_in_dim(turned, column ^ step, 1, keepdims=False)

    own_mirror = jnp.stack(
        [turned_rows(0)]
        + [swap(turned_rows(step), "aux", aux_size, step) for step in range(1, aux_size)]
    )
    other_mirror = swap(own_mirror, "pair", pair_size, 1)
    direct = jnp.concatenate([own_direct, other_direct], axis=0)
    mirror = jnp.concatenate([own_mirror, other_mirror], axis=1)
    return place(columns, kinds, sources, slots, direct, mirror, here, tile_count)


def solution(mesh):
    placed = (P("aux", "pair", None, None), P(), P(None, "aux"), P())
    return jax.shard_map(
        body,
        mesh=mesh,
        in_specs=placed,
        out_specs=(P("pair", "aux", None), P("pair", None, "aux", None)),
        check_vma=False,
    )
```

time: 891 us -> 187 us (0.21)
  waiting for transfers between devices: 344 us -> 97.2 us
  local copies, waits for them, and re-layouts: 239 us -> 18.8 us
  loops' own time: 156 us -> 0 us
  matrix products: 133 us -> 0 us
  starting transfers between devices: 0.3 us -> 43.2 us
  Pallas kernels: 0 us -> 20 us
  between operations: 13.9 us -> 0.96 us
    all_gather x1 -> x0, waiting for transfers between devices: 219 us -> none  [body(): gathered = lax.all_gather(factors, 'pair', axis=1, tiled=True)]
    another operation x1 -> x0, loops' own time: 156 us -> none  [body(): partial_tiles = lax.map(contract, (left_ids, right_ids, weights))]
    dot_general x42 -> x0, matrix products: 133 us -> none  [the longest x40 126 us: contract(): lax.dot_general(left_block, right_block, (((0,), (0,)), ((), ())), prefer...]
    dynamic_update_slice x40 -> x0, local copies, waits for them, and re-layouts: 119 us -> none  [body(): partial_tiles = lax.map(contract, (left_ids, right_ids, weights))]
    ppermute x0 -> x22, waiting for transfers between devices: none -> 97.2 us  [swap(): return lax.ppermute(value, axis, [(i, i ^ step) for i in range(size)])]
    psum x1 -> x0, waiting for transfers between devices: 76.5 us -> none  [body(): summed = lax.psum(partial_tiles, 'aux')]
    dynamic_slice x124 -> x0, local copies, waits for them, and re-layouts: 76.1 us -> none  [the longest x120 70.4 us: body(): partial_tiles = lax.map(contract, (left_ids, right_ids, weights))]
    reduce_scatter x1 -> x0, waiting for transfers between devices: 49.2 us -> none  [body(): lax.psum_scatter(contribution, 'pair', scatter_dimension=0, tiled=True)]
  transfers between devices with their start and end apart: 3 -> 22, of which waited for: 3 -> 12; matrix products, arithmetic and copies ran while one was open for 0% -> 1% of each run, Pallas kernels for 0% -> 5%
where the time goes in v1:
time: 187 us; the launch traced here: 185 us
  waiting for transfers between devices  97.2 us (52%)
  starting transfers between devices  43.2 us (23%)
  Pallas kernels  20 us (11%)
  local copies, waits for them, and re-layouts  18.8 us (10%)
  other arithmetic  4.3 us (2%)
    ppermute x22, waiting for transfers between devices, swap(): return lax.ppermute(value, axis, [(i, i ^ step) for i in range(size)])  97.2 us
    ppermute x22, starting transfers between devices, swap(): return lax.ppermute(value, axis, [(i, i ^ step) for i in range(size)])  43.2 us
    pallas_call x2, Pallas kernels, contract(): pl.pallas_call(contract_kernel, out_shape=jax.ShapeDtypeStruct((count, wi...  16.7 us
    unnamed x42, local copies, waits for them, and re-layouts  13.8 us
  transfers between devices with their start and end apart: 22, of which 12 were waited for; matrix products, arithmetic and copies ran while one was open for 1% of the time, Pallas kernels for 5%

profile of v1, /device:TPU:0, one launch (start us, length us, event | category | flops | bytes accessed | tf_op | source)
XLA Modules:
  0.0 184.6 jit_solution(5373701582117586971)
XLA Ops:
  0.7 3.6 %dynamic-slice_bitcast_fusion.3 = (bf16[12,2,64,128]{3,2,1,0:T(8,128)(2,1)S(1)}, bf16[12,2,64,128]{3,2,1,0:T(8,128)(2,1)S(1)}, bf16[12,2,64,128]{3,2,1,0:T(8,128...) fusion(bf16[8,12,2,64,128]{4,3,2,1,0:T(8,128)(2,1)} %bitcast.86, ...), kind=kLoop, calls=%fused_computation.9 | loop fusion | bytes 6291488 | tf_op jit(solution)/shard_map/jit(dynamic_index_in_dim)/squeeze | solution.py:151
  4.8 2.6 %collective-permute-start.1 = (bf16[12,2,64,128]{3,2,1,0:T(8,128)(2,1)}, bf16[12,2,64,128]{3,2,1,0:T(8,128)(2,1)S(1)}, u32[]{:S(2)}, u32[]{:S(2)}) collective-permute-start(bf16[12,2,64,128]{3,2,1,0:T(8,128)(2,1)} %get-tuple-element.13), channel_id=1, source_target_pairs={{0,8},{4,12},{8,0},{12,4},{16,24},{20,28},{24,16},{28,20},{1,9},{5... | collective-permute-start | bytes 1179656 | tf_op jit(solution)/shard_map/ppermute | solution.py:12
  7.5 2.7 %collective-permute-start.3 = (bf16[12,2,64,128]{3,2,1,0:T(8,128)(2,1)}, bf16[12,2,64,128]{3,2,1,0:T(8,128)(2,1)S(1)}, u32[]{:S(2)}, u32[]{:S(2)}) collective-permute-start(bf16[12,2,64,128]{3,2,1,0:T(8,128)(2,1)} %get-tuple-element.11), channel_id=1, source_target_pairs={{0,16},{4,20},{8,24},{12,28},{16,0},{20,4},{24,8},{28,12},{1,17},{... | collective-permute-start | bytes 1179656 | tf_op jit(solution)/shard_map/ppermute | solution.py:12
  10.2 0.6 broadcast.321
  10.8 0.7 reduce.11
  11.8 3.5 %collective-permute-start.5 = (bf16[12,2,64,128]{3,2,1,0:T(8,128)(2,1)S(1)}, bf16[12,2,64,128]{3,2,1,0:T(8,128)(2,1)S(1)}, u32[]{:S(2)}, u32[]{:S(2)}) collective-permute-start(bf16[12,2,64,128]{3,2,1,0:T(8,128)(2,1)S(1)} %get-tuple-element.9), channel_id=1, source_target_pairs={{0,24},{4,28},{8,16},{12,20},{16,8},{20,12},{24,0},{28,4},{1,25},{... | collective-permute-start | bytes 1179656 | tf_op jit(solution)/shard_map/ppermute | solution.py:12
  15.3 18.6 %collective-permute-done.1.refs_2_ = bf16[12,2,64,128]{3,2,1,0:T(8,128)(2,1)S(1)} collective-permute-done((bf16[12,2,64,128]{3,2,1,0:T(8,128)(2,1)}, bf16[12,2,64,128]{3,2,1,0:T(8,128)(2,1)S(1)}, u32[]{:S(2)}, u32[]{:S(2)}) %collective-permute-start.1) | collective-permute-done | bytes 393248 | tf_op jit(solution)/shard_map/ppermute | solution.py:12
  33.9 0.8 copy-done
  34.7 0.7 collective-permute-start.6
  35.4 6.5 %collective-permute-done.2.refs_3_ = bf16[12,2,64,128]{3,2,1,0:T(8,128)(2,1)S(1)} collective-permute-done((bf16[12,2,64,128]{3,2,1,0:T(8,128)(2,1)}, bf16[12,2,64,128]{3,2,1,0:T(8,128)(2,1)S(1)}, u32[]{:S(2)}, u32[]{:S(2)}) %collective-permute-start.2) | collective-permute-done | bytes 393248 | tf_op jit(solution)/shard_map/ppermute | solution.py:12
  42.0 0.8 copy-done.3
  42.7 0.7 copy-done.6
  43.5 0.7 copy-done.9
  44.2 9.5 %collective-permute-done.5.refs_6_ = bf16[12,2,64,128]{3,2,1,0:T(8,128)(2,1)S(1)} collective-permute-done((bf16[12,2,64,128]{3,2,1,0:T(8,128)(2,1)S(1)}, bf16[12,2,64,128]{3,2,1,0:T(8,128)(2,1)S(1)}, u32[]{:S(2)}, u32[]{:S(2)}) %collective-permute-start.5) | collective-permute-done | bytes 393248 | tf_op jit(solution)/shard_map/ppermute | solution.py:12
  53.7 7.7 %collective-permute-done.6.refs_7_ = bf16[12,2,64,128]{3,2,1,0:T(8,128)(2,1)S(1)} collective-permute-done((bf16[12,2,64,128]{3,2,1,0:T(8,128)(2,1)S(1)}, bf16[12,2,64,128]{3,2,1,0:T(8,128)(2,1)S(1)}, u32[]{:S(2)}, u32[]{:S(2)}) %collective-permute-start.6) | collective-permute-done | bytes 393248 | tf_op jit(solution)/shard_map/ppermute | solution.py:12
  61.4 1.1 copy-done.1
  62.5 1.0 copy-done.4
  63.5 1.0 copy-done.7
  64.5 1.0 copy-done.10
  65.5 8.0 %shard_map.60 = f32[40,128,128]{2,1,0:T(8,128)S(1)} custom-call(s32[40]{0:T(128)S(1)} %get-tuple-element.28.left, s32[40]{0:T(128)S(1)} %get-tuple-element.27.right, s32[40]{0:T(128)S(1)} %get-tuple-element.26.weight, bf16[12,2,64,128]{3,2,1,0:T(8,128)(2,1)S(1)} %get-tuple-element.15.refs_0_, bf16[12,2,64,128]{3,2,1,0:T(8,128)(2,1)S(1)} %collective-permute-done.refs_1_, ...), custom_call_target="tpu_custom_call" | custom-call | tf_op jit(solution)/shard_map/pallas_call | solution.py:45
  73.6 2.7 %collective-permute-start.7 = (f32[40,128,128]{2,1,0:T(8,128)S(1)}, f32[40,128,128]{2,1,0:T(8,128)}, u32[]{:S(2)}, u32[]{:S(2)}) collective-permute-start(f32[40,128,128]{2,1,0:T(8,128)S(1)} %shard_map.60), channel_id=1, source_target_pairs={{0,4},{4,0},{8,12},{12,8},{16,20},{20,16},{24,28},{28,24},{1,5},{5... | collective-permute-start | bytes 7864328 | tf_op jit(solution)/shard_map/ppermute | solution.py:12
  76.3 1.0 copy-done.2
  77.3 1.0 copy-done.5
  78.3 1.0 copy-done.8
  79.3 1.0 copy-done.11
  80.3 1.0 copy-done.13
  81.3 1.0 copy-done.15
  82.3 8.7 %shard_map.59 = f32[40,128,128]{2,1,0:T(8,128)S(1)} custom-call(s32[40]{0:T(128)S(1)} %get-tuple-element.30.left, s32[40]{0:T(128)S(1)} %get-tuple-element.29.right, s32[40]{0:T(128)S(1)} %get-tuple-element.31.weight, bf16[12,2,64,128]{3,2,1,0:T(8,128)(2,1)S(1)} %get-tuple-element.15.refs_0_, bf16[12,2,64,128]{3,2,1,0:T(8,128)(2,1)S(1)} %collective-permute-done.refs_1_, ...), custom_call_target="tpu_custom_call" | custom-call | tf_op jit(solution)/shard_map/pallas_call | solution.py:45
  91.0 2.2 %add.211 = f32[40,128,128]{2,1,0:T(8,128)S(1)} add(f32[40,128,128]{2,1,0:T(8,128)S(1)} %shard_map.59, f32[40,128,128]{2,1,0:T(8,128)} %collective-permute-done.7) | non-fusion elementwise | flops 655360 | bytes 7864320 | tf_op jit(solution)/shard_map/add | solution.py:213
  93.4 3.1 %collective-permute-start.9 = (f32[40,32,128]{2,1,0:T(8,128)S(1)}, f32[40,32,128]{2,1,0:T(8,128)S(1)}, u32[]{:S(2)}, u32[]{:S(2)}) collective-permute-start(f32[40,32,128]{2,1,0:T(8,128)S(1)} %get-tuple-element.18), channel_id=1, source_target_pairs={{0,2},{1,3},{2,0},{3,1},{4,6},{5,7},{6,4},{7,5},{8,10},{9,11},{10,... | collective-permute-start | bytes 1966088 | tf_op jit(solution)/shard_map/ppermute | solution.py:12
  97.3 14.8 %collective-permute-done.10 = f32[40,32,128]{2,1,0:T(8,128)S(1)} collective-permute-done((f32[40,32,128]{2,1,0:T(8,128)S(1)}, f32[40,32,128]{2,1,0:T(8,128)S(1)}, u32[]{:S(2)}, u32[]{:S(2)}) %collective-permute-start.10) | collective-permute-done | bytes 655392 | tf_op jit(solution)/shard_map/ppermute | solution.py:12
  112.0 12.5 %collective-permute-done.9 = f32[40,32,128]{2,1,0:T(8,128)S(1)} collective-permute-done((f32[40,32,128]{2,1,0:T(8,128)S(1)}, f32[40,32,128]{2,1,0:T(8,128)S(1)}, u32[]{:S(2)}, u32[]{:S(2)}) %collective-permute-start.9) | collective-permute-done | bytes 655392 | tf_op jit(solution)/shard_map/ppermute | solution.py:12
  124.9 3.8 %collective-permute-start.13 = (f32[10,32,128]{2,1,0:T(8,128)S(1)}, f32[10,32,128]{2,1,0:T(8,128)S(1)}, u32[]{:S(2)}, u32[]{:S(2)}) collective-permute-start(f32[10,32,128]{2,1,0:T(8,128)S(1)} %get-tuple-element.24), channel_id=1, source_target_pairs={{0,24},{4,28},{8,16},{12,20},{16,8},{20,12},{24,0},{28,4},{1,25},{... | collective-permute-start | bytes 491528 | tf_op jit(solution)/shard_map/ppermute | solution.py:12
  128.7 14.5 %collective-permute-start.12 = (f32[10,32,128]{2,1,0:T(8,128)S(1)}, f32[10,32,128]{2,1,0:T(8,128)S(1)}, u32[]{:S(2)}, u32[]{:S(2)}) collective-permute-start(f32[10,32,128]{2,1,0:T(8,128)S(1)} %get-tuple-element.25), channel_id=1, source_target_pairs={{0,16},{4,20},{8,24},{12,28},{16,0},{20,4},{24,8},{28,12},{1,17},{... | collective-permute-start | bytes 491528 | tf_op jit(solution)/shard_map/ppermute | solution.py:12
  143.2 0.5 collective-permute-start.11
  143.8 10.7 %collective-permute-done.12 = f32[10,32,128]{2,1,0:T(8,128)S(1)} collective-permute-done((f32[10,32,128]{2,1,0:T(8,128)S(1)}, f32[10,32,128]{2,1,0:T(8,128)S(1)}, u32[]{:S(2)}, u32[]{:S(2)}) %collective-permute-start.12) | collective-permute-done | bytes 163872 | tf_op jit(solution)/shard_map/ppermute | solution.py:12
  154.7 3.2 %collective-permute-start.15 = (f32[10,32,128]{2,1,0:T(8,128)S(1)}, f32[10,32,128]{2,1,0:T(8,128)S(1)}, u32[]{:S(2)}, u32[]{:S(2)}) collective-permute-start(f32[10,32,128]{2,1,0:T(8,128)S(1)} %get-tuple-element.5), channel_id=1, source_target_pairs={{0,16},{4,20},{8,24},{12,28},{16,0},{20,4},{24,8},{28,12},{1,17},{... | collective-permute-start | bytes 491528 | tf_op jit(solution)/shard_map/ppermute | solution.py:12
  157.9 1.2 collective-permute-start.16
  159.3 3.6 %collective-permute-done.14 = f32[10,32,128]{2,1,0:T(8,128)S(1)} collective-permute-done((f32[10,32,128]{2,1,0:T(8,128)S(1)}, f32[10,32,128]{2,1,0:T(8,128)S(1)}, u32[]{:S(2)}, u32[]{:S(2)}) %collective-permute-start.14) | collective-permute-done | bytes 163872 | tf_op jit(solution)/shard_map/ppermute | solution.py:12
  162.9 7.2 %collective-permute-done.15 = f32[10,32,128]{2,1,0:T(8,128)S(1)} collective-permute-done((f32[10,32,128]{2,1,0:T(8,128)S(1)}, f32[10,32,128]{2,1,0:T(8,128)S(1)}, u32[]{:S(2)}, u32[]{:S(2)}) %collective-permute-start.15) | collective-permute-done | bytes 163872 | tf_op jit(solution)/shard_map/ppermute | solution.py:12
  170.3 0.7 dynamic-slice_bitcast_fusion.14
  171.0 1.0 collective-permute-start.20
  172.1 0.8 collective-permute-start.19
  172.9 1.7 collective-permute-start.18
  174.9 2.7 %collective-permute-done.20 = f32[10,32,128]{2,1,0:T(8,128)S(1)} collective-permute-done((f32[10,32,128]{2,1,0:T(8,128)}, f32[10,32,128]{2,1,0:T(8,128)S(1)}, u32[]{:S(2)}, u32[]{:S(2)}) %collective-permute-start.20) | collective-permute-done | bytes 163872 | tf_op jit(solution)/shard_map/ppermute | solution.py:12
  177.6 1.6 collective-permute-done.19
  179.4 1.9 %collective-permute-done.21 = f32[4,10,32,128]{3,2,1,0:T(8,128)S(1)} collective-permute-done((f32[4,10,32,128]{3,2,1,0:T(8,128)S(1)}, f32[4,10,32,128]{3,2,1,0:T(8,128)S(1)}, u32[]{:S(2)}, u32[]{:S(2)}) %collective-permute-start.21) | collective-permute-done | bytes 655392 | tf_op jit(solution)/shard_map/ppermute | solution.py:12
  181.5 3.1 %shard_map.62 = (f32[2,32,2048]{2,1,0:T(8,128)}, f32[1,40,32,128]{3,2,1,0:T(8,128)}) custom-call(s32[4]{0:T(128)S(1)} %iota_xor_fusion.columns, s32[32]{0:T(128)S(1)} %select_n.168.kinds, s32[32]{0:T(128)S(1)} %reshape.384.sources, s32[40]{0:T(128)S(1)} %broadcast_add_fusion.slots, f32[80,32,128]{2,1,0:T(8,128)S(1)} %constant_dynamic-update-slice_fusion.direct, ...), custom_call_target="tpu_custom_call" | custom-call | tf_op jit(solution)/shard_map/pallas_call | solution.py:134
  (76 shorter events, 3.7 us)
Async XLA Ops:
  0.7 10.1 %copy-start.17 = (s32[80,1]{0,1:T(1,128)S(1)}, s32[80,1]{0,1:T(1,128)}, u32[]{:S(2)}) copy-start(s32[80,1]{0,1:T(1,128)} %param.6) | copy-start | bytes 964
  0.7 10.9 %copy-start.16 = (s32[80,2]{0,1:T(2,128)S(1)}, s32[80,2]{0,1:T(2,128)}, u32[]{:S(2)}) copy-start(s32[80,2]{0,1:T(2,128)} %param.5) | copy-start | bytes 1924
  4.3 7.5 %collective-permute-start = (bf16[12,2,64,128]{3,2,1,0:T(8,128)(2,1)}, bf16[12,2,64,128]{3,2,1,0:T(8,128)(2,1)S(1)}, u32[]{:S(2)}, u32[]{:S(2)}) collective-permute-start(bf16[12,2,64,128]{3,2,1,0:T(8,128)(2,1)} %get-tuple-element.14), channel_id=1, source_target_pairs={{0,4},{4,0},{8,12},{12,8},{16,20},{20,16},{24,28},{28,24},{1,5},{5... | collective-permute-start | bytes 1179656 | tf_op jit(solution)/shard_map/ppermute | solution.py:12
  4.8 29.1 %collective-permute-start.1 = (bf16[12,2,64,128]{3,2,1,0:T(8,128)(2,1)}, bf16[12,2,64,128]{3,2,1,0:T(8,128)(2,1)S(1)}, u32[]{:S(2)}, u32[]{:S(2)}) collective-permute-start(bf16[12,2,64,128]{3,2,1,0:T(8,128)(2,1)} %get-tuple-element.13), channel_id=1, source_target_pairs={{0,8},{4,12},{8,0},{12,4},{16,24},{20,28},{24,16},{28,20},{1,9},{5... | collective-permute-start | bytes 1179656 | tf_op jit(solution)/shard_map/ppermute | solution.py:12
  7.3 34.6 %collective-permute-start.2 = (bf16[12,2,64,128]{3,2,1,0:T(8,128)(2,1)}, bf16[12,2,64,128]{3,2,1,0:T(8,128)(2,1)S(1)}, u32[]{:S(2)}, u32[]{:S(2)}) collective-permute-start(bf16[12,2,64,128]{3,2,1,0:T(8,128)(2,1)} %get-tuple-element.12), channel_id=1, source_target_pairs={{0,12},{4,8},{8,4},{12,0},{16,28},{20,24},{24,20},{28,16},{1,13},{... | collective-permute-start | bytes 1179656 | tf_op jit(solution)/shard_map/ppermute | solution.py:12
  7.5 35.2 %collective-permute-start.3 = (bf16[12,2,64,128]{3,2,1,0:T(8,128)(2,1)}, bf16[12,2,64,128]{3,2,1,0:T(8,128)(2,1)S(1)}, u32[]{:S(2)}, u32[]{:S(2)}) collective-permute-start(bf16[12,2,64,128]{3,2,1,0:T(8,128)(2,1)} %get-tuple-element.11), channel_id=1, source_target_pairs={{0,16},{4,20},{8,24},{12,28},{16,0},{20,4},{24,8},{28,12},{1,17},{... | collective-permute-start | bytes 1179656 | tf_op jit(solution)/shard_map/ppermute | solution.py:12
  10.2 33.3 %collective-permute-start.4 = (bf16[12,2,64,128]{3,2,1,0:T(8,128)(2,1)}, bf16[12,2,64,128]{3,2,1,0:T(8,128)(2,1)S(1)}, u32[]{:S(2)}, u32[]{:S(2)}) collective-permute-start(bf16[12,2,64,128]{3,2,1,0:T(8,128)(2,1)} %get-tuple-element.10), channel_id=1, source_target_pairs={{0,20},{4,16},{8,28},{12,24},{16,4},{20,0},{24,12},{28,8},{1,21},{... | collective-permute-start | bytes 1179656 | tf_op jit(solution)/shard_map/ppermute | solution.py:12
  11.8 41.9 %collective-permute-start.5 = (bf16[12,2,64,128]{3,2,1,0:T(8,128)(2,1)S(1)}, bf16[12,2,64,128]{3,2,1,0:T(8,128)(2,1)S(1)}, u32[]{:S(2)}, u32[]{:S(2)}) collective-permute-start(bf16[12,2,64,128]{3,2,1,0:T(8,128)(2,1)S(1)} %get-tuple-element.9), channel_id=1, source_target_pairs={{0,24},{4,28},{8,16},{12,20},{16,8},{20,12},{24,0},{28,4},{1,25},{... | collective-permute-start | bytes 1179656 | tf_op jit(solution)/shard_map/ppermute | solution.py:12
  33.9 0.8 copy-start
  34.7 26.7 %collective-permute-start.6 = (bf16[12,2,64,128]{3,2,1,0:T(8,128)(2,1)S(1)}, bf16[12,2,64,128]{3,2,1,0:T(8,128)(2,1)S(1)}, u32[]{:S(2)}, u32[]{:S(2)}) collective-permute-start(bf16[12,2,64,128]{3,2,1,0:T(8,128)(2,1)S(1)} %get-tuple-element.8), channel_id=1, source_target_pairs={{0,28},{4,24},{8,20},{12,16},{16,12},{20,8},{24,4},{28,0},{1,29},{... | collective-permute-start | bytes 1179656 | tf_op jit(solution)/shard_map/ppermute | solution.py:12
  42.0 0.8 copy-start.3
  42.7 0.7 copy-start.6
  43.5 0.7 copy-start.9
  53.7 19.8 %copy-start.12 = (bf16[12,2,64,128]{3,2,1,0:T(8,128)(2,1)}, bf16[12,2,64,128]{3,2,1,0:T(8,128)(2,1)S(1)}, u32[]{:S(2)}) copy-start(bf16[12,2,64,128]{3,2,1,0:T(8,128)(2,1)S(1)} %collective-permute-done.5.refs_6_) | copy-start | bytes 1179652
  61.4 12.2 %copy-start.14 = (bf16[12,2,64,128]{3,2,1,0:T(8,128)(2,1)}, bf16[12,2,64,128]{3,2,1,0:T(8,128)(2,1)S(1)}, u32[]{:S(2)}) copy-start(bf16[12,2,64,128]{3,2,1,0:T(8,128)(2,1)S(1)} %collective-permute-done.6.refs_7_) | copy-start | bytes 1179652
  61.4 1.1 copy-start.1
  62.5 1.0 copy-start.4
  63.5 1.0 copy-start.7
  64.5 1.0 copy-start.10
  73.6 17.4 %collective-permute-start.7 = (f32[40,128,128]{2,1,0:T(8,128)S(1)}, f32[40,128,128]{2,1,0:T(8,128)}, u32[]{:S(2)}, u32[]{:S(2)}) collective-permute-start(f32[40,128,128]{2,1,0:T(8,128)S(1)} %shard_map.60), channel_id=1, source_target_pairs={{0,4},{4,0},{8,12},{12,8},{16,20},{20,16},{24,28},{28,24},{1,5},{5... | collective-permute-start | bytes 7864328 | tf_op jit(solution)/shard_map/ppermute | solution.py:12
  76.3 1.0 copy-start.2
  77.3 1.0 copy-start.5
  78.3 1.0 copy-start.8
  79.3 1.0 copy-start.11
  80.3 1.0 copy-start.13
  81.3 1.0 copy-start.15
  93.4 18.7 %collective-permute-start.10 = (f32[40,32,128]{2,1,0:T(8,128)S(1)}, f32[40,32,128]{2,1,0:T(8,128)S(1)}, u32[]{:S(2)}, u32[]{:S(2)}) collective-permute-start(f32[40,32,128]{2,1,0:T(8,128)S(1)} %get-tuple-element.17), channel_id=1, source_target_pairs={{0,3},{1,2},{2,1},{3,0},{4,7},{5,6},{6,5},{7,4},{8,11},{9,10},{10,... | collective-permute-start | bytes 1966088 | tf_op jit(solution)/shard_map/ppermute | solution.py:12
  93.4 31.1 %collective-permute-start.9 = (f32[40,32,128]{2,1,0:T(8,128)S(1)}, f32[40,32,128]{2,1,0:T(8,128)S(1)}, u32[]{:S(2)}, u32[]{:S(2)}) collective-permute-start(f32[40,32,128]{2,1,0:T(8,128)S(1)} %get-tuple-element.18), channel_id=1, source_target_pairs={{0,2},{1,3},{2,0},{3,1},{4,6},{5,7},{6,4},{7,5},{8,10},{9,11},{10,... | collective-permute-start | bytes 1966088 | tf_op jit(solution)/shard_map/ppermute | solution.py:12
  96.5 28.0 %collective-permute-start.8 = (f32[40,32,128]{2,1,0:T(8,128)S(1)}, f32[40,32,128]{2,1,0:T(8,128)S(1)}, u32[]{:S(2)}, u32[]{:S(2)}) collective-permute-start(f32[40,32,128]{2,1,0:T(8,128)S(1)} %get-tuple-element.16), channel_id=1, source_target_pairs={{0,1},{1,0},{2,3},{3,2},{4,5},{5,4},{6,7},{7,6},{8,9},{9,8},{10,11... | collective-permute-start | bytes 1966088 | tf_op jit(solution)/shard_map/ppermute | solution.py:12
  97.2 46.4 %copy-start.18 = (s32[80]{0:T(128)S(1)}, s32[80]{0:T(128)}, u32[]{:S(2)}) copy-start(s32[80]{0:T(128)} %param.7) | copy-start | bytes 964
  124.9 19.0 %collective-permute-start.13 = (f32[10,32,128]{2,1,0:T(8,128)S(1)}, f32[10,32,128]{2,1,0:T(8,128)S(1)}, u32[]{:S(2)}, u32[]{:S(2)}) collective-permute-start(f32[10,32,128]{2,1,0:T(8,128)S(1)} %get-tuple-element.24), channel_id=1, source_target_pairs={{0,24},{4,28},{8,16},{12,20},{16,8},{20,12},{24,0},{28,4},{1,25},{... | collective-permute-start | bytes 491528 | tf_op jit(solution)/shard_map/ppermute | solution.py:12
  128.7 25.9 %collective-permute-start.12 = (f32[10,32,128]{2,1,0:T(8,128)S(1)}, f32[10,32,128]{2,1,0:T(8,128)S(1)}, u32[]{:S(2)}, u32[]{:S(2)}) collective-permute-start(f32[10,32,128]{2,1,0:T(8,128)S(1)} %get-tuple-element.25), channel_id=1, source_target_pairs={{0,16},{4,20},{8,24},{12,28},{16,0},{20,4},{24,8},{28,12},{1,17},{... | collective-permute-start | bytes 491528 | tf_op jit(solution)/shard_map/ppermute | solution.py:12
  143.2 11.4 %collective-permute-start.11 = (f32[10,32,128]{2,1,0:T(8,128)S(1)}, f32[10,32,128]{2,1,0:T(8,128)S(1)}, u32[]{:S(2)}, u32[]{:S(2)}) collective-permute-start(f32[10,32,128]{2,1,0:T(8,128)S(1)} %get-tuple-element.23), channel_id=1, source_target_pairs={{0,8},{4,12},{8,0},{12,4},{16,24},{20,28},{24,16},{28,20},{1,9},{5... | collective-permute-start | bytes 491528 | tf_op jit(solution)/shard_map/ppermute | solution.py:12
  154.6 8.2 %collective-permute-start.14 = (f32[10,32,128]{2,1,0:T(8,128)S(1)}, f32[10,32,128]{2,1,0:T(8,128)S(1)}, u32[]{:S(2)}, u32[]{:S(2)}) collective-permute-start(f32[10,32,128]{2,1,0:T(8,128)S(1)} %get-tuple-element.5), channel_id=1, source_target_pairs={{0,8},{4,12},{8,0},{12,4},{16,24},{20,28},{24,16},{28,20},{1,9},{5... | collective-permute-start | bytes 491528 | tf_op jit(solution)/shard_map/ppermute | solution.py:12
  154.7 15.3 %collective-permute-start.15 = (f32[10,32,128]{2,1,0:T(8,128)S(1)}, f32[10,32,128]{2,1,0:T(8,128)S(1)}, u32[]{:S(2)}, u32[]{:S(2)}) collective-permute-start(f32[10,32,128]{2,1,0:T(8,128)S(1)} %get-tuple-element.5), channel_id=1, source_target_pairs={{0,16},{4,20},{8,24},{12,28},{16,0},{20,4},{24,8},{28,12},{1,17},{... | collective-permute-start | bytes 491528 | tf_op jit(solution)/shard_map/ppermute | solution.py:12
  157.9 12.1 %collective-permute-start.16 = (f32[10,32,128]{2,1,0:T(8,128)S(1)}, f32[10,32,128]{2,1,0:T(8,128)S(1)}, u32[]{:S(2)}, u32[]{:S(2)}) collective-permute-start(f32[10,32,128]{2,1,0:T(8,128)S(1)} %get-tuple-element.5), channel_id=1, source_target_pairs={{0,24},{4,28},{8,16},{12,20},{16,8},{20,12},{24,0},{28,4},{1,25},{... | collective-permute-start | bytes 491528 | tf_op jit(solution)/shard_map/ppermute | solution.py:12
  171.0 6.5 %collective-permute-start.20 = (f32[10,32,128]{2,1,0:T(8,128)}, f32[10,32,128]{2,1,0:T(8,128)S(1)}, u32[]{:S(2)}, u32[]{:S(2)}) collective-permute-start(f32[10,32,128]{2,1,0:T(8,128)} %get-tuple-element.22), channel_id=1, source_target_pairs={{0,3},{1,2},{2,1},{3,0},{4,7},{5,6},{6,5},{7,4},{8,11},{9,10},{10,... | collective-permute-start | bytes 491528 | tf_op jit(solution)/shard_map/ppermute | solution.py:12
  172.1 7.1 %collective-permute-start.19 = (f32[10,32,128]{2,1,0:T(8,128)S(1)}, f32[10,32,128]{2,1,0:T(8,128)S(1)}, u32[]{:S(2)}, u32[]{:S(2)}) collective-permute-start(f32[10,32,128]{2,1,0:T(8,128)S(1)} %get-tuple-element.20), channel_id=1, source_target_pairs={{0,2},{1,3},{2,0},{3,1},{4,6},{5,7},{6,4},{7,5},{8,10},{9,11},{10,... | collective-permute-start | bytes 491528 | tf_op jit(solution)/shard_map/ppermute | solution.py:12
  172.9 6.3 %collective-permute-start.18 = (f32[10,32,128]{2,1,0:T(8,128)S(1)}, f32[10,32,128]{2,1,0:T(8,128)S(1)}, u32[]{:S(2)}, u32[]{:S(2)}) collective-permute-start(f32[10,32,128]{2,1,0:T(8,128)S(1)} %get-tuple-element.21), channel_id=1, source_target_pairs={{0,1},{1,0},{2,3},{3,2},{4,5},{5,4},{6,7},{7,6},{8,9},{9,8},{10,11... | collective-permute-start | bytes 491528 | tf_op jit(solution)/shard_map/ppermute | solution.py:12
  174.8 4.6 %collective-permute-start.17 = (f32[40,32,128]{2,1,0:T(8,128)S(1)}, f32[40,32,128]{2,1,0:T(8,128)S(1)}, u32[]{:S(2)}, u32[]{:S(2)}) collective-permute-start(f32[40,32,128]{2,1,0:T(8,128)S(1)} %pad_maximum_fusion.1), channel_id=1, source_target_pairs={{0,4},{4,0},{8,12},{12,8},{16,20},{20,16},{24,28},{28,24},{1,5},{5... | collective-permute-start | bytes 1966088 | tf_op jit(solution)/shard_map/ppermute | solution.py:12
  179.2 2.2 %collective-permute-start.21 = (f32[4,10,32,128]{3,2,1,0:T(8,128)S(1)}, f32[4,10,32,128]{3,2,1,0:T(8,128)S(1)}, u32[]{:S(2)}, u32[]{:S(2)}) collective-permute-start(f32[4,10,32,128]{3,2,1,0:T(8,128)S(1)} %pad_maximum_fusion.2), channel_id=1, source_target_pairs={{0,4},{4,0},{8,12},{12,8},{16,20},{20,16},{24,28},{28,24},{1,5},{5... | collective-permute-start | bytes 1966088 | tf_op jit(solution)/shard_map/ppermute | solution.py:12

commit v2 on v1

--- a/solution.py
+++ b/solution.py
@@ -5,58 +5,79 @@
 from jax.experimental.pallas import tpu as pltpu
 from jax.sharding import PartitionSpec as P
 
-VMEM_LIMIT = 48 << 20
+VMEM_LIMIT = 24 << 20
 
 
 def swap(value, axis, size, step):
     return lax.ppermute(value, axis, [(i, i ^ step) for i in range(size)])
 
 
-def contract_kernel(left, right, weight, *refs):
-    *parts, out, plain, turned = refs
-    count = out.shape[0]
-    depth, here, orbitals, width = parts[0].shape
-    for step, part in enumerate(parts):
-        for tile in range(here):
-            block = part[:, tile].reshape(depth * orbitals, width)
-            plain[step * here + tile] = block
-            turned[step * here + tile] = block.T
+def contract_kernel(left, right, weight, column, tiles, out):
+    count = out.shape[1]
+    rows = out.shape[2]
 
     def one(index, carry):
-        @pl.when(weight[index] != 0)
-        def _():
-            out[index] = jnp.dot(
-                turned[left[index]], plain[right[index]], preferred_element_type=jnp.float32
-            )
-
-        @pl.when(weight[index] == 0)
-        def _():
-            out[index] = jnp.zeros((width, width), jnp.float32)
-
+        block = lax.dot_general(
+            tiles[left[index]],
+            tiles[right[index]],
+            (((0,), (0,)), ((), ())),
+            preferred_element_type=jnp.float32,
+        ) * weight[index].astype(jnp.float32)
+        for step in range(out.shape[0]):
+            out[column[0] ^ step, index] = block[step * rows : (step + 1) * rows]
         return carry
 
-    lax.fori_loop(0, count, one, 0)
-
-
-def contract(parts, left, right, weight):
-    depth, here, orbitals, width = parts[0].shape
-    tiles = len(parts) * here
-    count = left.shape[0]
+    lax.fori_loop(0, count, one, 0, unroll=4)
+
+
+def contract(tiles, table, column, aux_size):
+    width = tiles.shape[-1]
+    count = table.shape[1]
     return pl.pallas_call(
         contract_kernel,
-        out_shape=jax.ShapeDtypeStruct((count, width, width), jnp.float32),
+        out_shape=jax.ShapeDtypeStruct((aux_size, count, width // aux_size, width), jnp.float32),
         grid_spec=pltpu.PrefetchScalarGridSpec(
-            num_scalar_prefetch=3,
+            num_scalar_prefetch=4,
             grid=(),
-            in_specs=[pl.BlockSpec(memory_space=pltpu.VMEM)] * len(parts),
+            in_specs=[pl.BlockSpec(memory_space=pltpu.VMEM)],
             out_specs=pl.BlockSpec(memory_space=pltpu.VMEM),
-            scratch_shapes=[
-                pltpu.VMEM((tiles, depth * orbitals, width), jnp.bfloat16),
-                pltpu.VMEM((tiles, width, depth * orbitals), jnp.bfloat16),
-            ],
         ),
         compiler_params=pltpu.CompilerParams(vmem_limit_bytes=VMEM_LIMIT),
-    )(left, right, weight, *parts)
+    )(table[0], table[1], table[2], column.reshape(1), tiles)
+
+
+def gather_kernel(targets, *refs):
+    *groups, out = refs
+    base = 0
+    per_group = len(groups) // 3
+    for part in range(3):
+        first, *rest = groups[part * per_group : (part + 1) * per_group]
+
+        def one(index, carry, first=first, rest=rest, base=base):
+            total = first[0, index]
+            for ref in rest:
+                total = total + ref[index]
+            out[targets[base + index]] = total
+            return carry
+
+        lax.fori_loop(0, first.shape[1], one, 0, unroll=4)
+        base += first.shape[1]
+
+
+def gather_sums(targets, groups):
+    flat = [value for group in groups for value in group]
+    _, _, rows, width = flat[0].shape
+    return pl.pallas_call(
+        gather_kernel,
+        out_shape=jax.ShapeDtypeStruct((targets.shape[0], rows, width), jnp.float32),
+        grid_spec=pltpu.PrefetchScalarGridSpec(
+            num_scalar_prefetch=1,
+            grid=(),
+            in_specs=[pl.BlockSpec(memory_space=pltpu.VMEM)] * len(flat),
+            out_specs=pl.BlockSpec(memory_space=pltpu.VMEM),
+        ),
+        compiler_params=pltpu.CompilerParams(vmem_limit_bytes=VMEM_LIMIT),
+    )(targets, *flat)
 
 
 def turn_kernel(source, out):
@@ -151,6 +172,16 @@
     return lax.dynamic_index_in_dim(value, index, 0, keepdims=False)
 
 
+def arrival_order(chips, here):
+    far = [step for step in range(1, chips)]
+    if chips == 4:
+        far = [2, 1, 3]
+    order = [(step, inner) for step in far[:2] for inner in range(here)]
+    if len(far) > 1:
+        order = [(step, inner) for inner in range(here) for step in far[:2]]
+    return order + [(step, inner) for step in far[2:] for inner in range(here)]
+
+
 def body(factors, pairs, shared, owners):
     aux_rows, here, orbitals, width = factors.shape
     pair_size = lax.axis_size("pair")
@@ -164,7 +195,7 @@
     core = me % 2
     chip = me // 2
     column = lax.axis_index("aux")
-    depth = aux_rows // pair_size
+    depth = aux_rows // chips
     pack = aux_size
     unit = max(pack, chips)
     half = -(-(-(-pair_count // 2)) // unit) * unit
@@ -177,14 +208,42 @@
     rank = jnp.sum(
         (same_owner & (pair_ids[None, :] < pair_ids[:, None])).astype(jnp.int32), axis=1
     )
-    left_slots = ((lefts // here) ^ me) * here + lefts % here
-    right_slots = ((rights // here) ^ me) * here + rights % here
-    weights = shared[:, 0]
-    tables = jnp.pad(
-        jnp.stack([left_slots, right_slots, weights]), ((0, 0), (0, padded - pair_count))
-    ).reshape(3, 2, half)
-    mine = lax.dynamic_index_in_dim(tables, core, 1, keepdims=False)
-    theirs = lax.dynamic_index_in_dim(tables, 1 - core, 1, keepdims=False)
+    order = arrival_order(chips, here)
+    tile_ids = jnp.arange(tile_count, dtype=jnp.int32)
+    tile_chip = tile_ids // (2 * here) ^ chip
+    tile_core = (tile_ids // here) % 2
+    tile_spot = tile_ids % here
+    arrival = jnp.where(tile_chip == 0, tile_spot * 2 + (tile_core ^ core), 0)
+    rank_of = jnp.zeros_like(arrival)
+    for spot, (step, inner) in enumerate(order):
+        hit = (tile_chip == step) & (tile_spot == inner)
+        last = spot == len(order) - 1
+        lane = tile_core if last else tile_core ^ core
+        arrival = jnp.where(hit, 2 * here + 2 * spot + lane, arrival)
+        rank_of = jnp.where(hit, 1 + spot + (tile_core if last else 0), rank_of)
+    left_slots = jnp.sum(jnp.where(lefts[:, None] == tile_ids, arrival, 0), axis=1)
+    right_slots = jnp.sum(jnp.where(rights[:, None] == tile_ids, arrival, 0), axis=1)
+    left_rank = jnp.sum(jnp.where(lefts[:, None] == tile_ids, rank_of, 0), axis=1)
+    right_rank = jnp.sum(jnp.where(rights[:, None] == tile_ids, rank_of, 0), axis=1)
+    ready = jnp.maximum(left_rank, right_rank)
+    values = jnp.stack([left_slots, right_slots, shared[:, 0], ready])
+    values = jnp.pad(values, ((0, 0), (0, padded - pair_count)))
+    values = values.at[3, pair_count:].set(64) if padded > pair_count else values
+    values = lax.dynamic_index_in_dim(values.reshape(4, 2, half), core, 1, keepdims=False)
+    local_ids = jnp.arange(half, dtype=jnp.int32)
+    key = values[3] * half + local_ids
+    spot_of = jnp.sum((key[None, :] < key[:, None]).astype(jnp.int32), axis=1)
+    sorter = spot_of[None, :] == local_ids[:, None]
+    target_of = ((local_ids // share) ^ chip) * share + local_ids % share
+    fields = jnp.concatenate([values[:3], target_of[None]])
+    fields = jnp.sum(jnp.where(sorter[None], fields[:, None, :], 0), axis=2).astype(jnp.int32)
+    real_half = -(-pair_count // 2)
+    all_pairs = tile_count * (tile_count + 1) // 2
+    bounds = [0]
+    for missing in (2, 1):
+        known = tile_count - missing
+        bounds.append(max(1, real_half - (all_pairs - known * (known + 1) // 2)))
+    bounds.append(half)
 
     local = pair_ids % half
     part_core = pair_ids // half
@@ -203,30 +262,43 @@
     slots = jnp.sum(jnp.where(matches, final_pos + 1, 0), axis=1).astype(jnp.int32) - 1
     columns = column ^ jnp.arange(aux_size, dtype=jnp.int32)
 
-    pieces = factors.reshape(pair_size, depth, here, orbitals, width)
-    parts = [take(pieces, me)]
-    for step in range(1, pair_size):
-        parts.append(swap(take(pieces, me ^ step), "pair", pair_size, step))
-
-    given = contract(parts, *theirs)
-    kept = contract(parts, *mine)
-    chip_sum = kept + swap(given, "pair", pair_size, 1)
-
-    by_column = chip_sum.reshape(half, aux_size, rows, width)
-
-    def column_rows(step):
-        return lax.dynamic_index_in_dim(by_column, column ^ step, 1, keepdims=False)
-
-    summed = column_rows(0)
-    arrived = [swap(column_rows(step), "aux", aux_size, step) for step in range(1, aux_size)]
-    for value in arrived:
-        summed = summed + value
+    pieces = factors.reshape(chips, depth, here, orbitals, width)
+
+    def outgoing(step, inner):
+        return take(pieces[:, :, inner], chip ^ step).reshape(depth * orbitals, width)
+
+    tiles = []
+    for inner in range(here):
+        block = outgoing(0, inner)
+        tiles += [block, swap(block, "pair", pair_size, 1)]
+    for step, inner in order[:-1]:
+        block = swap(outgoing(step, inner), "pair", pair_size, 2 * step)
+        tiles += [block, swap(block, "pair", pair_size, 1)]
+    step, inner = order[-1]
+    last_block = outgoing(step, inner)
+    late = []
+    for lane in range(2):
+        there = [(2 * i + lane, 2 * (i ^ step) + lane) for i in range(chips)]
+        block = lax.ppermute(last_block, "pair", there)
+        across = lax.ppermute(block, "pair", [(2 * i + lane, 2 * i + 1 - lane) for i in range(chips)])
+        late.append(jnp.where(core == lane, block, across))
+
+    store = jnp.stack(tiles + [jnp.zeros_like(tiles[0])] * 2)
+    groups = []
+    for part in range(3):
+        if part:
+            store = lax.dynamic_update_index_in_dim(
+                store, late[part - 1], tile_count - 3 + part, 0
+            )
+        blocks = contract(store, fields[:3, bounds[part] : bounds[part + 1]], column, aux_size)
+        groups.append(
+            [blocks] + [swap(blocks[step], "aux", aux_size, step) for step in range(1, aux_size)]
+        )
+    summed = gather_sums(fields[3], groups)
 
     by_chip = summed.reshape(chips, share, rows, width)
-    arrived = [
-        swap(take(by_chip, chip ^ step), "pair", pair_size, 2 * step) for step in range(1, chips)
-    ]
-    total = take(by_chip, chip)
+    arrived = [swap(by_chip[step], "pair", pair_size, 2 * step) for step in range(1, chips)]
+    total = by_chip[0]
     for value in arrived:
         total = total + value
 

time: 187 us -> 180 us (0.963)
  waiting for transfers between devices: 97.2 us -> 110 us
  local copies, waits for them, and re-layouts: 18.8 us -> 8.64 us
  Pallas kernels: 20 us -> 12.4 us
  other arithmetic: 4.3 us -> 2.39 us
    ppermute x22 -> x32, waiting for transfers between devices: 97.2 us -> 110 us  [swap(): return lax.ppermute(value, axis, [(i, i ^ step) for i in range(size)])]
    unnamed x42 -> x25, local copies, waits for them, and re-layouts: 13.8 us -> 2.25 us
    ppermute x0 -> x4, starting transfers between devices: none -> 11.3 us  [the longest x2 7.63 us: body(): block = lax.ppermute(last_block, 'pair', there)]
    ppermute x22 -> x32, starting transfers between devices: 43.2 us -> 32.1 us  [swap(): return lax.ppermute(value, axis, [(i, i ^ step) for i in range(size)])]
    pallas_call x2 -> x4, Pallas kernels: 16.7 us -> 9.15 us  [the longest x3 8.43 us: contract(): pl.pallas_call(contract_kernel, out_shape=jax.ShapeDtypeStruct((aux_size,...]
    squeeze x5 -> x7, local copies, waits for them, and re-layouts: 4 us -> 0.29 us  [the longest x3 0.15 us: contract(): table[2]]
    slice x1 -> x3, local copies, waits for them, and re-layouts: 0.02 us -> 3.12 us  [the longest x1 3.08 us: outgoing(): pieces[:, :, inner]]
    add x3 -> x2, other arithmetic: 2.5 us -> 0.02 us  [the longest x1 0.01 us: body(): target_of = (local_ids // share ^ chip) * share + local_ids % share]
  transfers between devices with their start and end apart: 22 -> 36, of which waited for: 12 -> 14; matrix products, arithmetic and copies ran while one was open for 1% -> 3% of each run, Pallas kernels for 5% -> 5%
where the time goes in v2:
time: 180 us; the launch traced here: 178 us
  waiting for transfers between devices  110 us (61%)
  starting transfers between devices  43.4 us (24%)
  Pallas kernels  12.4 us (7%)
  local copies, waits for them, and re-layouts  8.64 us (5%)
  other arithmetic  2.39 us (1%)
    ppermute x32, waiting for transfers between devices, swap(): return lax.ppermute(value, axis, [(i, i ^ step) for i in range(size)])  110 us
    ppermute x32, starting transfers between devices, swap(): return lax.ppermute(value, axis, [(i, i ^ step) for i in range(size)])  32.1 us
    pallas_call x3, Pallas kernels, contract(): pl.pallas_call(contract_kernel, out_shape=jax.ShapeDtypeStruct((aux_size,...  8.43 us
    ppermute x2, starting transfers between devices, body(): block = lax.ppermute(last_block, 'pair', there)  7.63 us
    ppermute x2, starting transfers between devices, body(): lax.ppermute(block, 'pair', [(2 * i + lane, 2 * i + 1 - lane) for i in ra...  3.65 us
  transfers between devices with their start and end apart: 36, of which 14 were waited for; matrix products, arithmetic and copies ran while one was open for 3% of the time, Pallas kernels for 5%

profile of v2, /device:TPU:0, one launch (start us, length us, event | category | flops | bytes accessed | tf_op | source)
XLA Modules:
  0.0 177.9 jit_solution(6318631826990290302)
XLA Ops:
  0.7 3.1 %fusion.23 = (bf16[4,24,1,64,128]{4,3,2,1,0:T(8,128)(2,1)S(1)}, bf16[4,24,1,64,128]{4,3,2,1,0:T(8,128)(2,1)S(1)}) fusion(bf16[4,24,2,64,128]{4,3,2,1,0:T(8,128)(2,1)} %bitcast.133), kind=kLoop, calls=%fused_computation.147 | loop fusion | bytes 6291456 | tf_op jit(solution)/shard_map/slice | solution.py:268
  3.8 1.6 constant_dynamic-slice_fusion.1
  5.4 6.9 %collective-permute-start.15 = (bf16[1536,128]{1,0:T(8,128)(2,1)}, bf16[1536,128]{1,0:T(8,128)(2,1)S(1)}, u32[]{:S(2)}, u32[]{:S(2)}) collective-permute-start(bf16[1536,128]{1,0:T(8,128)(2,1)} %bitcast.36), channel_id=1, source_target_pairs={{0,24},{8,16},{16,8},{24,0},{1,25},{9,17},{17,9},{25,1},{2,26},{10... | collective-permute-start | bytes 1179656 | tf_op jit(solution)/shard_map/ppermute | solution.py:282
  12.3 0.7 collective-permute-start.20
  13.1 0.5 collective-permute-start.1
  14.0 0.5 broadcast.273
  14.5 0.6 reduce.3
  16.0 1.0 constant_dynamic-update-slice_fusion.1
  17.1 0.6 collective-permute-start.4
  17.8 2.4 %collective-permute-start.6 = (bf16[1536,128]{1,0:T(8,128)(2,1)}, bf16[1536,128]{1,0:T(8,128)(2,1)S(1)}, u32[]{:S(2)}, u32[]{:S(2)}) collective-permute-start(bf16[1536,128]{1,0:T(8,128)(2,1)} %bitcast.144), channel_id=1, source_target_pairs={{0,16},{4,20},{8,24},{12,28},{16,0},{20,4},{24,8},{28,12},{1,17},{... | collective-permute-start | bytes 1179656 | tf_op jit(solution)/shard_map/ppermute | solution.py:12
  20.3 35.3 %collective-permute-done.2 = bf16[1536,128]{1,0:T(8,128)(2,1)S(1)} collective-permute-done((bf16[1536,128]{1,0:T(8,128)(2,1)}, bf16[1536,128]{1,0:T(8,128)(2,1)S(1)}, u32[]{:S(2)}, u32[]{:S(2)}) %collective-permute-start.2) | collective-permute-done | bytes 393248 | tf_op jit(solution)/shard_map/ppermute | solution.py:12
  55.7 1.6 collective-permute-done.3
  57.3 2.5 %collective-permute-start.10 = (bf16[1536,128]{1,0:T(8,128)(2,1)}, bf16[1536,128]{1,0:T(8,128)(2,1)S(1)}, u32[]{:S(2)}, u32[]{:S(2)}) collective-permute-start(bf16[1536,128]{1,0:T(8,128)(2,1)} %bitcast.142), channel_id=1, source_target_pairs={{0,24},{4,28},{8,16},{12,20},{16,8},{20,12},{24,0},{28,4},{1,25},{... | collective-permute-start | bytes 1179656 | tf_op jit(solution)/shard_map/ppermute | solution.py:12
  59.9 4.1 %collective-permute-done.6 = bf16[1536,128]{1,0:T(8,128)(2,1)S(1)} collective-permute-done((bf16[1536,128]{1,0:T(8,128)(2,1)}, bf16[1536,128]{1,0:T(8,128)(2,1)S(1)}, u32[]{:S(2)}, u32[]{:S(2)}) %collective-permute-start.6) | collective-permute-done | bytes 393248 | tf_op jit(solution)/shard_map/ppermute | solution.py:12
  64.1 16.4 %collective-permute-done.8 = bf16[1536,128]{1,0:T(8,128)(2,1)S(1)} collective-permute-done((bf16[1536,128]{1,0:T(8,128)(2,1)}, bf16[1536,128]{1,0:T(8,128)(2,1)S(1)}, u32[]{:S(2)}, u32[]{:S(2)}) %collective-permute-start.8) | collective-permute-done | bytes 393248 | tf_op jit(solution)/shard_map/ppermute | solution.py:12
  81.1 2.4 %collective-permute-start.16 = (bf16[1536,128]{1,0:T(8,128)(2,1)S(1)}, bf16[1536,128]{1,0:T(8,128)(2,1)S(1)}, u32[]{:S(2)}, u32[]{:S(2)}) collective-permute-start(bf16[1536,128]{1,0:T(8,128)(2,1)S(1)} %collective-permute-done.15), channel_id=1, source_target_pairs={{0,4},{8,12},{16,20},{24,28},{1,5},{9,13},{17,21},{25,29},{2,6},{1... | collective-permute-start | bytes 1179656 | tf_op jit(solution)/shard_map/ppermute | solution.py:283
  83.4 1.3 collective-permute-start.21
  85.3 2.1 %shard_map.59.refs_0_ = f32[4,9,32,128]{3,2,1,0:T(8,128)S(1)} custom-call(s32[9]{0:T(128)S(1)} %get-tuple-element.44.left, s32[9]{0:T(128)S(1)} %get-tuple-element.43.right, s32[9]{0:T(128)S(1)} %get-tuple-element.42.weight, s32[1]{0:T(128)} %bitcast.7.column, bf16[16,1536,128]{2,1,0:T(8,128)(2,1)S(1)} %broadcast_dynamic-update-slice_fusion.tiles), custom_call_target="tpu_custom_call" | custom-call | tf_op jit(solution)/shard_map/pallas_call | solution.py:36
  87.6 3.3 %shard_map.60.refs_4_ = f32[4,15,32,128]{3,2,1,0:T(8,128)S(1)} custom-call(s32[15]{0:T(128)S(1)} %get-tuple-element.41.left, s32[15]{0:T(128)S(1)} %get-tuple-element.40.right, s32[15]{0:T(128)S(1)} %get-tuple-element.39.weight, s32[1]{0:T(128)} %bitcast.7.column, bf16[16,1536,128]{2,1,0:T(8,128)(2,1)S(1)} %bitcast_dynamic-update-slice_fusion.1.tiles), custom_call_target="tpu_custom_call" | custom-call | tf_op jit(solution)/shard_map/pallas_call | solution.py:36
  90.9 1.6 collective-permute-start.17
  92.5 0.6 collective-permute-start.12
  93.1 1.5 collective-permute-start.13
  94.7 1.4 collective-permute-start.14
  96.2 3.0 %shard_map.61.refs_8_ = f32[4,16,32,128]{3,2,1,0:T(8,128)S(1)} custom-call(s32[16]{0:T(128)S(1)} %get-tuple-element.38.left, s32[16]{0:T(128)S(1)} %get-tuple-element.37.right, s32[16]{0:T(128)S(1)} %get-tuple-element.36.weight, s32[1]{0:T(128)} %bitcast.7.column, bf16[16,1536,128]{2,1,0:T(8,128)(2,1)S(1)} %bitcast_dynamic-update-slice_fusion.tiles), custom_call_target="tpu_custom_call" | custom-call | tf_op jit(solution)/shard_map/pallas_call | solution.py:36
  99.3 0.6 collective-permute-start.22
  99.9 2.9 %collective-permute-done.12.refs_1_ = f32[9,32,128]{2,1,0:T(8,128)S(1)} collective-permute-done((f32[9,32,128]{2,1,0:T(8,128)S(1)}, f32[9,32,128]{2,1,0:T(8,128)S(1)}, u32[]{:S(2)}, u32[]{:S(2)}) %collective-permute-start.12) | collective-permute-done | bytes 147488 | tf_op jit(solution)/shard_map/ppermute | solution.py:12
  102.8 1.5 collective-permute-start.23
  104.3 1.4 collective-permute-start.24
  105.8 1.3 collective-permute-done.14.refs_3_
  107.5 2.5 %collective-permute-start.19 = (f32[15,32,128]{2,1,0:T(8,128)S(1)}, f32[15,32,128]{2,1,0:T(8,128)S(1)}, u32[]{:S(2)}, u32[]{:S(2)}) collective-permute-start(f32[15,32,128]{2,1,0:T(8,128)S(1)} %get-tuple-element.23), channel_id=1, source_target_pairs={{0,3},{1,2},{2,1},{3,0},{4,7},{5,6},{6,5},{7,4},{8,11},{9,10},{10,... | collective-permute-start | bytes 737288 | tf_op jit(solution)/shard_map/ppermute | solution.py:12
  110.0 18.9 %collective-permute-done.18.refs_6_ = f32[15,32,128]{2,1,0:T(8,128)S(1)} collective-permute-done((f32[15,32,128]{2,1,0:T(8,128)S(1)}, f32[15,32,128]{2,1,0:T(8,128)S(1)}, u32[]{:S(2)}, u32[]{:S(2)}) %collective-permute-start.18) | collective-permute-done | bytes 245792 | tf_op jit(solution)/shard_map/ppermute | solution.py:12
  128.9 0.7 shard_map.62
  129.9 2.9 %collective-permute-start.26 = (f32[10,32,128]{2,1,0:T(8,128)S(1)}, f32[10,32,128]{2,1,0:T(8,128)S(1)}, u32[]{:S(2)}, u32[]{:S(2)}) collective-permute-start(f32[10,32,128]{2,1,0:T(8,128)S(1)} %get-tuple-element.32), channel_id=1, source_target_pairs={{0,16},{4,20},{8,24},{12,28},{16,0},{20,4},{24,8},{28,12},{1,17},{... | collective-permute-start | bytes 491528 | tf_op jit(solution)/shard_map/ppermute | solution.py:12
  132.8 1.3 collective-permute-start.27
  134.3 4.5 %collective-permute-done.25 = f32[10,32,128]{2,1,0:T(8,128)S(1)} collective-permute-done((f32[10,32,128]{2,1,0:T(8,128)S(1)}, f32[10,32,128]{2,1,0:T(8,128)S(1)}, u32[]{:S(2)}, u32[]{:S(2)}) %collective-permute-start.25) | collective-permute-done | bytes 163872 | tf_op jit(solution)/shard_map/ppermute | solution.py:12
  138.8 6.1 %collective-permute-done.26 = f32[10,32,128]{2,1,0:T(8,128)S(1)} collective-permute-done((f32[10,32,128]{2,1,0:T(8,128)S(1)}, f32[10,32,128]{2,1,0:T(8,128)S(1)}, u32[]{:S(2)}, u32[]{:S(2)}) %collective-permute-start.26) | collective-permute-done | bytes 163872 | tf_op jit(solution)/shard_map/ppermute | solution.py:12
  144.9 3.2 %collective-permute-start.28 = (f32[10,32,128]{2,1,0:T(8,128)S(1)}, f32[10,32,128]{2,1,0:T(8,128)S(1)}, u32[]{:S(2)}, u32[]{:S(2)}) collective-permute-start(f32[10,32,128]{2,1,0:T(8,128)S(1)} %get-tuple-element.7), channel_id=1, source_target_pairs={{0,8},{4,12},{8,0},{12,4},{16,24},{20,28},{24,16},{28,20},{1,9},{5... | collective-permute-start | bytes 491528 | tf_op jit(solution)/shard_map/ppermute | solution.py:12
  148.2 1.1 collective-permute-start.29
  149.2 1.4 collective-permute-start.30
  150.8 2.9 %collective-permute-done.28 = f32[10,32,128]{2,1,0:T(8,128)S(1)} collective-permute-done((f32[10,32,128]{2,1,0:T(8,128)S(1)}, f32[10,32,128]{2,1,0:T(8,128)S(1)}, u32[]{:S(2)}, u32[]{:S(2)}) %collective-permute-start.28) | collective-permute-done | bytes 163872 | tf_op jit(solution)/shard_map/ppermute | solution.py:12
  153.7 9.2 %collective-permute-done.29 = f32[10,32,128]{2,1,0:T(8,128)S(1)} collective-permute-done((f32[10,32,128]{2,1,0:T(8,128)S(1)}, f32[10,32,128]{2,1,0:T(8,128)S(1)}, u32[]{:S(2)}, u32[]{:S(2)}) %collective-permute-start.29) | collective-permute-done | bytes 163872 | tf_op jit(solution)/shard_map/ppermute | solution.py:12
  163.2 0.7 dynamic-slice_bitcast_fusion.3
  163.9 1.5 collective-permute-start.32
  165.5 1.9 %collective-permute-start.34 = (f32[10,32,128]{2,1,0:T(8,128)S(1)}, f32[10,32,128]{2,1,0:T(8,128)S(1)}, u32[]{:S(2)}, u32[]{:S(2)}) collective-permute-start(f32[10,32,128]{2,1,0:T(8,128)S(1)} %get-tuple-element.29), channel_id=1, source_target_pairs={{0,3},{1,2},{2,1},{3,0},{4,7},{5,6},{6,5},{7,4},{8,11},{9,10},{10,... | collective-permute-start | bytes 491528 | tf_op jit(solution)/shard_map/ppermute | solution.py:12
  167.8 1.7 collective-permute-done.32
  169.5 3.0 %collective-permute-done.33 = f32[10,32,128]{2,1,0:T(8,128)S(1)} collective-permute-done((f32[10,32,128]{2,1,0:T(8,128)S(1)}, f32[10,32,128]{2,1,0:T(8,128)S(1)}, u32[]{:S(2)}, u32[]{:S(2)}) %collective-permute-start.33) | collective-permute-done | bytes 163872 | tf_op jit(solution)/shard_map/ppermute | solution.py:12
  172.8 1.9 %collective-permute-done.35 = f32[4,10,32,128]{3,2,1,0:T(8,128)S(1)} collective-permute-done((f32[4,10,32,128]{3,2,1,0:T(8,128)S(1)}, f32[4,10,32,128]{3,2,1,0:T(8,128)S(1)}, u32[]{:S(2)}, u32[]{:S(2)}) %collective-permute-start.35) | collective-permute-done | bytes 655392 | tf_op jit(solution)/shard_map/ppermute | solution.py:12
  174.8 3.1 %shard_map.64 = (f32[2,32,2048]{2,1,0:T(8,128)}, f32[1,40,32,128]{3,2,1,0:T(8,128)}) custom-call(s32[4]{0:T(128)S(1)} %iota_xor_fusion.columns, s32[32]{0:T(128)S(1)} %select_n.231.kinds, s32[32]{0:T(128)S(1)} %reshape.343.sources, s32[40]{0:T(128)S(1)} %broadcast_add_fusion.slots, f32[80,32,128]{2,1,0:T(8,128)S(1)} %constant_dynamic-update-slice_fusion.2.direct, ...), custom_call_target="tpu_custom_call" | custom-call | tf_op jit(solution)/shard_map/pallas_call | solution.py:155
  (106 shorter events, 5.3 us)
Async XLA Ops:
  0.7 13.0 %copy-start = (s32[80,2]{0,1:T(2,128)S(1)}, s32[80,2]{0,1:T(2,128)}, u32[]{:S(2)}) copy-start(s32[80,2]{0,1:T(2,128)} %param.5) | copy-start | bytes 1924
  0.7 13.8 %copy-start.1 = (s32[80,1]{0,1:T(1,128)S(1)}, s32[80,1]{0,1:T(1,128)}, u32[]{:S(2)}) copy-start(s32[80,1]{0,1:T(1,128)} %param.6) | copy-start | bytes 964
  5.4 75.6 %collective-permute-start.15 = (bf16[1536,128]{1,0:T(8,128)(2,1)}, bf16[1536,128]{1,0:T(8,128)(2,1)S(1)}, u32[]{:S(2)}, u32[]{:S(2)}) collective-permute-start(bf16[1536,128]{1,0:T(8,128)(2,1)} %bitcast.36), channel_id=1, source_target_pairs={{0,24},{8,16},{16,8},{24,0},{1,25},{9,17},{17,9},{25,1},{2,26},{10... | collective-permute-start | bytes 1179656 | tf_op jit(solution)/shard_map/ppermute | solution.py:282
  12.3 68.7 %collective-permute-start.20 = (bf16[1536,128]{1,0:T(8,128)(2,1)}, bf16[1536,128]{1,0:T(8,128)(2,1)S(1)}, u32[]{:S(2)}, u32[]{:S(2)}) collective-permute-start(bf16[1536,128]{1,0:T(8,128)(2,1)} %bitcast.36), channel_id=1, source_target_pairs={{4,28},{12,20},{20,12},{28,4},{5,29},{13,21},{21,13},{29,5},{6,30}... | collective-permute-start | bytes 1179656 | tf_op jit(solution)/shard_map/ppermute | solution.py:282
  13.0 4.0 %collective-permute-start = (bf16[1536,128]{1,0:T(8,128)(2,1)}, bf16[1536,128]{1,0:T(8,128)(2,1)S(1)}, u32[]{:S(2)}, u32[]{:S(2)}) collective-permute-start(bf16[1536,128]{1,0:T(8,128)(2,1)} %bitcast.10), channel_id=1, source_target_pairs={{0,4},{4,0},{8,12},{12,8},{16,20},{20,16},{24,28},{28,24},{1,5},{5... | collective-permute-start | bytes 1179656 | tf_op jit(solution)/shard_map/ppermute | solution.py:12
  13.1 4.7 %collective-permute-start.1 = (bf16[1536,128]{1,0:T(8,128)(2,1)S(1)}, bf16[1536,128]{1,0:T(8,128)(2,1)S(1)}, u32[]{:S(2)}, u32[]{:S(2)}) collective-permute-start(bf16[1536,128]{1,0:T(8,128)(2,1)S(1)} %bitcast.134), channel_id=1, source_target_pairs={{0,4},{4,0},{8,12},{12,8},{16,20},{20,16},{24,28},{28,24},{1,5},{5... | collective-permute-start | bytes 1179656 | tf_op jit(solution)/shard_map/ppermute | solution.py:12
  13.6 41.9 %collective-permute-start.2 = (bf16[1536,128]{1,0:T(8,128)(2,1)}, bf16[1536,128]{1,0:T(8,128)(2,1)S(1)}, u32[]{:S(2)}, u32[]{:S(2)}) collective-permute-start(bf16[1536,128]{1,0:T(8,128)(2,1)} %bitcast.15), channel_id=1, source_target_pairs={{0,16},{4,20},{8,24},{12,28},{16,0},{20,4},{24,8},{28,12},{1,17},{... | collective-permute-start | bytes 1179656 | tf_op jit(solution)/shard_map/ppermute | solution.py:12
  17.1 40.2 %collective-permute-start.4 = (bf16[1536,128]{1,0:T(8,128)(2,1)}, bf16[1536,128]{1,0:T(8,128)(2,1)S(1)}, u32[]{:S(2)}, u32[]{:S(2)}) collective-permute-start(bf16[1536,128]{1,0:T(8,128)(2,1)} %bitcast.145), channel_id=1, source_target_pairs={{0,8},{4,12},{8,0},{12,4},{16,24},{20,28},{24,16},{28,20},{1,9},{5... | collective-permute-start | bytes 1179656 | tf_op jit(solution)/shard_map/ppermute | solution.py:12
  17.8 46.2 %collective-permute-start.6 = (bf16[1536,128]{1,0:T(8,128)(2,1)}, bf16[1536,128]{1,0:T(8,128)(2,1)S(1)}, u32[]{:S(2)}, u32[]{:S(2)}) collective-permute-start(bf16[1536,128]{1,0:T(8,128)(2,1)} %bitcast.144), channel_id=1, source_target_pairs={{0,16},{4,20},{8,24},{12,28},{16,0},{20,4},{24,8},{28,12},{1,17},{... | collective-permute-start | bytes 1179656 | tf_op jit(solution)/shard_map/ppermute | solution.py:12
  55.5 1.7 collective-permute-start.3
  57.3 23.2 %collective-permute-start.8 = (bf16[1536,128]{1,0:T(8,128)(2,1)}, bf16[1536,128]{1,0:T(8,128)(2,1)S(1)}, u32[]{:S(2)}, u32[]{:S(2)}) collective-permute-start(bf16[1536,128]{1,0:T(8,128)(2,1)} %bitcast.143), channel_id=1, source_target_pairs={{0,8},{4,12},{8,0},{12,4},{16,24},{20,28},{24,16},{28,20},{1,9},{5... | collective-permute-start | bytes 1179656 | tf_op jit(solution)/shard_map/ppermute | solution.py:12
  57.3 23.2 %collective-permute-start.10 = (bf16[1536,128]{1,0:T(8,128)(2,1)}, bf16[1536,128]{1,0:T(8,128)(2,1)S(1)}, u32[]{:S(2)}, u32[]{:S(2)}) collective-permute-start(bf16[1536,128]{1,0:T(8,128)(2,1)} %bitcast.142), channel_id=1, source_target_pairs={{0,24},{4,28},{8,16},{12,20},{16,8},{20,12},{24,0},{28,4},{1,25},{... | collective-permute-start | bytes 1179656 | tf_op jit(solution)/shard_map/ppermute | solution.py:12
  64.0 19.4 %collective-permute-start.5 = (bf16[1536,128]{1,0:T(8,128)(2,1)S(1)}, bf16[1536,128]{1,0:T(8,128)(2,1)S(1)}, u32[]{:S(2)}, u32[]{:S(2)}) collective-permute-start(bf16[1536,128]{1,0:T(8,128)(2,1)S(1)} %collective-permute-done.4), channel_id=1, source_target_pairs={{0,4},{4,0},{8,12},{12,8},{16,20},{20,16},{24,28},{28,24},{1,5},{5... | collective-permute-start | bytes 1179656 | tf_op jit(solution)/shard_map/ppermute | solution.py:12
  80.5 4.4 %collective-permute-start.7 = (bf16[1536,128]{1,0:T(8,128)(2,1)S(1)}, bf16[1536,128]{1,0:T(8,128)(2,1)S(1)}, u32[]{:S(2)}, u32[]{:S(2)}) collective-permute-start(bf16[1536,128]{1,0:T(8,128)(2,1)S(1)} %collective-permute-done.6), channel_id=1, source_target_pairs={{0,4},{4,0},{8,12},{12,8},{16,20},{20,16},{24,28},{28,24},{1,5},{5... | collective-permute-start | bytes 1179656 | tf_op jit(solution)/shard_map/ppermute | solution.py:12
  80.5 4.5 %collective-permute-start.9 = (bf16[1536,128]{1,0:T(8,128)(2,1)S(1)}, bf16[1536,128]{1,0:T(8,128)(2,1)S(1)}, u32[]{:S(2)}, u32[]{:S(2)}) collective-permute-start(bf16[1536,128]{1,0:T(8,128)(2,1)S(1)} %collective-permute-done.8), channel_id=1, source_target_pairs={{0,4},{4,0},{8,12},{12,8},{16,20},{20,16},{24,28},{28,24},{1,5},{5... | collective-permute-start | bytes 1179656 | tf_op jit(solution)/shard_map/ppermute | solution.py:12
  81.0 4.1 %collective-permute-start.11 = (bf16[1536,128]{1,0:T(8,128)(2,1)S(1)}, bf16[1536,128]{1,0:T(8,128)(2,1)S(1)}, u32[]{:S(2)}, u32[]{:S(2)}) collective-permute-start(bf16[1536,128]{1,0:T(8,128)(2,1)S(1)} %collective-permute-done.10), channel_id=1, source_target_pairs={{0,4},{4,0},{8,12},{12,8},{16,20},{20,16},{24,28},{28,24},{1,5},{5... | collective-permute-start | bytes 1179656 | tf_op jit(solution)/shard_map/ppermute | solution.py:12
  81.1 6.4 %collective-permute-start.16 = (bf16[1536,128]{1,0:T(8,128)(2,1)S(1)}, bf16[1536,128]{1,0:T(8,128)(2,1)S(1)}, u32[]{:S(2)}, u32[]{:S(2)}) collective-permute-start(bf16[1536,128]{1,0:T(8,128)(2,1)S(1)} %collective-permute-done.15), channel_id=1, source_target_pairs={{0,4},{8,12},{16,20},{24,28},{1,5},{9,13},{17,21},{25,29},{2,6},{1... | collective-permute-start | bytes 1179656 | tf_op jit(solution)/shard_map/ppermute | solution.py:283
  83.4 12.7 %collective-permute-start.21 = (bf16[1536,128]{1,0:T(8,128)(2,1)S(1)}, bf16[1536,128]{1,0:T(8,128)(2,1)S(1)}, u32[]{:S(2)}, u32[]{:S(2)}) collective-permute-start(bf16[1536,128]{1,0:T(8,128)(2,1)S(1)} %collective-permute-done.20), channel_id=1, source_target_pairs={{4,0},{12,8},{20,16},{28,24},{5,1},{13,9},{21,17},{29,25},{6,2},{1... | collective-permute-start | bytes 1179656 | tf_op jit(solution)/shard_map/ppermute | solution.py:283
  90.9 16.5 %collective-permute-start.17 = (f32[15,32,128]{2,1,0:T(8,128)S(1)}, f32[15,32,128]{2,1,0:T(8,128)S(1)}, u32[]{:S(2)}, u32[]{:S(2)}) collective-permute-start(f32[15,32,128]{2,1,0:T(8,128)S(1)} %get-tuple-element.25), channel_id=1, source_target_pairs={{0,1},{1,0},{2,3},{3,2},{4,5},{5,4},{6,7},{7,6},{8,9},{9,8},{10,11... | collective-permute-start | bytes 737288 | tf_op jit(solution)/shard_map/ppermute | solution.py:12
  92.5 10.3 %collective-permute-start.12 = (f32[9,32,128]{2,1,0:T(8,128)S(1)}, f32[9,32,128]{2,1,0:T(8,128)S(1)}, u32[]{:S(2)}, u32[]{:S(2)}) collective-permute-start(f32[9,32,128]{2,1,0:T(8,128)S(1)} %get-tuple-element.35), channel_id=1, source_target_pairs={{0,1},{1,0},{2,3},{3,2},{4,5},{5,4},{6,7},{7,6},{8,9},{9,8},{10,11... | collective-permute-start | bytes 442376 | tf_op jit(solution)/shard_map/ppermute | solution.py:12
  93.1 11.2 %collective-permute-start.13 = (f32[9,32,128]{2,1,0:T(8,128)S(1)}, f32[9,32,128]{2,1,0:T(8,128)S(1)}, u32[]{:S(2)}, u32[]{:S(2)}) collective-permute-start(f32[9,32,128]{2,1,0:T(8,128)S(1)} %get-tuple-element.34), channel_id=1, source_target_pairs={{0,2},{1,3},{2,0},{3,1},{4,6},{5,7},{6,4},{7,5},{8,10},{9,11},{10,... | collective-permute-start | bytes 442376 | tf_op jit(solution)/shard_map/ppermute | solution.py:12
  94.7 12.4 %collective-permute-start.14 = (f32[9,32,128]{2,1,0:T(8,128)S(1)}, f32[9,32,128]{2,1,0:T(8,128)S(1)}, u32[]{:S(2)}, u32[]{:S(2)}) collective-permute-start(f32[9,32,128]{2,1,0:T(8,128)S(1)} %get-tuple-element.33), channel_id=1, source_target_pairs={{0,3},{1,2},{2,1},{3,0},{4,7},{5,6},{6,5},{7,4},{8,11},{9,10},{10,... | collective-permute-start | bytes 442376 | tf_op jit(solution)/shard_map/ppermute | solution.py:12
  96.2 37.9 %copy-start.2 = (s32[80]{0:T(128)S(1)}, s32[80]{0:T(128)}, u32[]{:S(2)}) copy-start(s32[80]{0:T(128)} %param.7) | copy-start | bytes 964
  99.3 29.6 %collective-permute-start.22 = (f32[16,32,128]{2,1,0:T(8,128)S(1)}, f32[16,32,128]{2,1,0:T(8,128)S(1)}, u32[]{:S(2)}, u32[]{:S(2)}) collective-permute-start(f32[16,32,128]{2,1,0:T(8,128)S(1)} %get-tuple-element.22), channel_id=1, source_target_pairs={{0,1},{1,0},{2,3},{3,2},{4,5},{5,4},{6,7},{7,6},{8,9},{9,8},{10,11... | collective-permute-start | bytes 786440 | tf_op jit(solution)/shard_map/ppermute | solution.py:12
  102.8 26.1 %collective-permute-start.23 = (f32[16,32,128]{2,1,0:T(8,128)S(1)}, f32[16,32,128]{2,1,0:T(8,128)S(1)}, u32[]{:S(2)}, u32[]{:S(2)}) collective-permute-start(f32[16,32,128]{2,1,0:T(8,128)S(1)} %get-tuple-element.21), channel_id=1, source_target_pairs={{0,2},{1,3},{2,0},{3,1},{4,6},{5,7},{6,4},{7,5},{8,10},{9,11},{10,... | collective-permute-start | bytes 786440 | tf_op jit(solution)/shard_map/ppermute | solution.py:12
  104.3 24.6 %collective-permute-start.24 = (f32[16,32,128]{2,1,0:T(8,128)S(1)}, f32[16,32,128]{2,1,0:T(8,128)S(1)}, u32[]{:S(2)}, u32[]{:S(2)}) collective-permute-start(f32[16,32,128]{2,1,0:T(8,128)S(1)} %get-tuple-element.20), channel_id=1, source_target_pairs={{0,3},{1,2},{2,1},{3,0},{4,7},{5,6},{6,5},{7,4},{8,11},{9,10},{10,... | collective-permute-start | bytes 786440 | tf_op jit(solution)/shard_map/ppermute | solution.py:12
  107.0 21.9 %collective-permute-start.18 = (f32[15,32,128]{2,1,0:T(8,128)S(1)}, f32[15,32,128]{2,1,0:T(8,128)S(1)}, u32[]{:S(2)}, u32[]{:S(2)}) collective-permute-start(f32[15,32,128]{2,1,0:T(8,128)S(1)} %get-tuple-element.24), channel_id=1, source_target_pairs={{0,2},{1,3},{2,0},{3,1},{4,6},{5,7},{6,4},{7,5},{8,10},{9,11},{10,... | collective-permute-start | bytes 737288 | tf_op jit(solution)/shard_map/ppermute | solution.py:12
  107.5 21.4 %collective-permute-start.19 = (f32[15,32,128]{2,1,0:T(8,128)S(1)}, f32[15,32,128]{2,1,0:T(8,128)S(1)}, u32[]{:S(2)}, u32[]{:S(2)}) collective-permute-start(f32[15,32,128]{2,1,0:T(8,128)S(1)} %get-tuple-element.23), channel_id=1, source_target_pairs={{0,3},{1,2},{2,1},{3,0},{4,7},{5,6},{6,5},{7,4},{8,11},{9,10},{10,... | collective-permute-start | bytes 737288 | tf_op jit(solution)/shard_map/ppermute | solution.py:12
  129.7 9.2 %collective-permute-start.25 = (f32[10,32,128]{2,1,0:T(8,128)S(1)}, f32[10,32,128]{2,1,0:T(8,128)S(1)}, u32[]{:S(2)}, u32[]{:S(2)}) collective-permute-start(f32[10,32,128]{2,1,0:T(8,128)S(1)} %get-tuple-element.30), channel_id=1, source_target_pairs={{0,8},{4,12},{8,0},{12,4},{16,24},{20,28},{24,16},{28,20},{1,9},{5... | collective-permute-start | bytes 491528 | tf_op jit(solution)/shard_map/ppermute | solution.py:12
  129.9 15.0 %collective-permute-start.26 = (f32[10,32,128]{2,1,0:T(8,128)S(1)}, f32[10,32,128]{2,1,0:T(8,128)S(1)}, u32[]{:S(2)}, u32[]{:S(2)}) collective-permute-start(f32[10,32,128]{2,1,0:T(8,128)S(1)} %get-tuple-element.32), channel_id=1, source_target_pairs={{0,16},{4,20},{8,24},{12,28},{16,0},{20,4},{24,8},{28,12},{1,17},{... | collective-permute-start | bytes 491528 | tf_op jit(solution)/shard_map/ppermute | solution.py:12
  132.8 12.1 %collective-permute-start.27 = (f32[10,32,128]{2,1,0:T(8,128)S(1)}, f32[10,32,128]{2,1,0:T(8,128)S(1)}, u32[]{:S(2)}, u32[]{:S(2)}) collective-permute-start(f32[10,32,128]{2,1,0:T(8,128)S(1)} %get-tuple-element.31), channel_id=1, source_target_pairs={{0,24},{4,28},{8,16},{12,20},{16,8},{20,12},{24,0},{28,4},{1,25},{... | collective-permute-start | bytes 491528 | tf_op jit(solution)/shard_map/ppermute | solution.py:12
  144.9 8.8 %collective-permute-start.28 = (f32[10,32,128]{2,1,0:T(8,128)S(1)}, f32[10,32,128]{2,1,0:T(8,128)S(1)}, u32[]{:S(2)}, u32[]{:S(2)}) collective-permute-start(f32[10,32,128]{2,1,0:T(8,128)S(1)} %get-tuple-element.7), channel_id=1, source_target_pairs={{0,8},{4,12},{8,0},{12,4},{16,24},{20,28},{24,16},{28,20},{1,9},{5... | collective-permute-start | bytes 491528 | tf_op jit(solution)/shard_map/ppermute | solution.py:12
  148.2 14.7 %collective-permute-start.29 = (f32[10,32,128]{2,1,0:T(8,128)S(1)}, f32[10,32,128]{2,1,0:T(8,128)S(1)}, u32[]{:S(2)}, u32[]{:S(2)}) collective-permute-start(f32[10,32,128]{2,1,0:T(8,128)S(1)} %get-tuple-element.7), channel_id=1, source_target_pairs={{0,16},{4,20},{8,24},{12,28},{16,0},{20,4},{24,8},{28,12},{1,17},{... | collective-permute-start | bytes 491528 | tf_op jit(solution)/shard_map/ppermute | solution.py:12
  149.2 13.7 %collective-permute-start.30 = (f32[10,32,128]{2,1,0:T(8,128)S(1)}, f32[10,32,128]{2,1,0:T(8,128)S(1)}, u32[]{:S(2)}, u32[]{:S(2)}) collective-permute-start(f32[10,32,128]{2,1,0:T(8,128)S(1)} %get-tuple-element.7), channel_id=1, source_target_pairs={{0,24},{4,28},{8,16},{12,20},{16,8},{20,12},{24,0},{28,4},{1,25},{... | collective-permute-start | bytes 491528 | tf_op jit(solution)/shard_map/ppermute | solution.py:12
  163.9 5.5 %collective-permute-start.32 = (f32[10,32,128]{2,1,0:T(8,128)}, f32[10,32,128]{2,1,0:T(8,128)S(1)}, u32[]{:S(2)}, u32[]{:S(2)}) collective-permute-start(f32[10,32,128]{2,1,0:T(8,128)} %get-tuple-element.28), channel_id=1, source_target_pairs={{0,1},{1,0},{2,3},{3,2},{4,5},{5,4},{6,7},{7,6},{8,9},{9,8},{10,11... | collective-permute-start | bytes 491528 | tf_op jit(solution)/shard_map/ppermute | solution.py:12
  165.4 7.1 %collective-permute-start.33 = (f32[10,32,128]{2,1,0:T(8,128)S(1)}, f32[10,32,128]{2,1,0:T(8,128)S(1)}, u32[]{:S(2)}, u32[]{:S(2)}) collective-permute-start(f32[10,32,128]{2,1,0:T(8,128)S(1)} %get-tuple-element.27), channel_id=1, source_target_pairs={{0,2},{1,3},{2,0},{3,1},{4,6},{5,7},{6,4},{7,5},{8,10},{9,11},{10,... | collective-permute-start | bytes 491528 | tf_op jit(solution)/shard_map/ppermute | solution.py:12
  165.5 7.0 %collective-permute-start.34 = (f32[10,32,128]{2,1,0:T(8,128)S(1)}, f32[10,32,128]{2,1,0:T(8,128)S(1)}, u32[]{:S(2)}, u32[]{:S(2)}) collective-permute-start(f32[10,32,128]{2,1,0:T(8,128)S(1)} %get-tuple-element.29), channel_id=1, source_target_pairs={{0,3},{1,2},{2,1},{3,0},{4,7},{5,6},{6,5},{7,4},{8,11},{9,10},{10,... | collective-permute-start | bytes 491528 | tf_op jit(solution)/shard_map/ppermute | solution.py:12
  167.7 5.0 %collective-permute-start.31 = (f32[40,32,128]{2,1,0:T(8,128)S(1)}, f32[40,32,128]{2,1,0:T(8,128)S(1)}, u32[]{:S(2)}, u32[]{:S(2)}) collective-permute-start(f32[40,32,128]{2,1,0:T(8,128)S(1)} %pad_maximum_fusion.1), channel_id=1, source_target_pairs={{0,4},{4,0},{8,12},{12,8},{16,20},{20,16},{24,28},{28,24},{1,5},{5... | collective-permute-start | bytes 1966088 | tf_op jit(solution)/shard_map/ppermute | solution.py:12
  172.5 2.2 %collective-permute-start.35 = (f32[4,10,32,128]{3,2,1,0:T(8,128)S(1)}, f32[4,10,32,128]{3,2,1,0:T(8,128)S(1)}, u32[]{:S(2)}, u32[]{:S(2)}) collective-permute-start(f32[4,10,32,128]{3,2,1,0:T(8,128)S(1)} %pad_maximum_fusion.2), channel_id=1, source_target_pairs={{0,4},{4,0},{8,12},{12,8},{16,20},{20,16},{24,28},{28,24},{1,5},{5... | collective-permute-start | bytes 1966088 | tf_op jit(solution)/shard_map/ppermute | solution.py:12

commit v3 on v1

v3 whole, which is shorter than its diff:
```python
import functools

import jax
import jax.numpy as jnp
from jax import lax
from jax.experimental import pallas as pl
from jax.experimental.pallas import tpu as pltpu
from jax.sharding import PartitionSpec as P

VMEM_LIMIT = 24 << 20
TINY = pl.CostEstimate(flops=1, transcendentals=0, bytes_accessed=1)


def swap(value, axis, size, step):
    return lax.ppermute(value, axis, [(i, i ^ step) for i in range(size)])


def contract_kernel(spots, left, right, weight, column, *refs):
    *parts, out, tiles = refs
    parts = parts[: len(spots)]
    count = out.shape[1]
    rows = out.shape[2]
    length, width = tiles.shape[1:]
    for spot, part in zip(spots, parts):
        for inner in range(part.shape[1]):
            tiles[spot + inner] = part[:, inner].reshape(length, width)

    def one(index, carry):
        block = lax.dot_general(
            tiles[left[index]],
            tiles[right[index]],
            (((0,), (0,)), ((), ())),
            preferred_element_type=jnp.float32,
        ) * weight[index].astype(jnp.float32)
        for step in range(out.shape[0]):
            out[column[0] ^ step, index] = block[step * rows : (step + 1) * rows]
        return carry

    lax.fori_loop(0, count, one, 0, unroll=4)


def contract(parts, table, column, tile_count, aux_size, earlier):
    spots, values = zip(*parts)
    depth, _, orbitals, width = values[0].shape
    count = table.shape[1]
    return pl.pallas_call(
        functools.partial(contract_kernel, spots),
        out_shape=jax.ShapeDtypeStruct((aux_size, count, width // aux_size, width), jnp.float32),
        grid_spec=pltpu.PrefetchScalarGridSpec(
            num_scalar_prefetch=4,
            grid=(),
            in_specs=[pl.BlockSpec(memory_space=pltpu.VMEM)] * len(values)
            + [pl.BlockSpec(memory_space=pl.ANY)] * len(earlier),
            out_specs=pl.BlockSpec(memory_space=pltpu.VMEM),
            scratch_shapes=[pltpu.VMEM((tile_count, depth * orbitals, width), values[0].dtype)],
        ),
        cost_estimate=TINY,
        compiler_params=pltpu.CompilerParams(vmem_limit_bytes=VMEM_LIMIT),
    )(table[0], table[1], table[2], column.reshape(1), *values, *earlier)


LEVELS = 32766.0


def extra_blocks(count, rows):
    return -(-count // rows)


def packed_shape(count, rows, width):
    return jax.ShapeDtypeStruct((count + extra_blocks(count, rows), rows, width), jnp.int16)


def pack_block(block, factor):
    return jnp.round(block * factor).astype(jnp.int32).astype(jnp.int16)


def unpack_block(block, scale):
    return block.astype(jnp.int32).astype(jnp.float32) * scale


def load_scales(packed, count, scales):
    rows = packed.shape[1]
    for extra in range(extra_blocks(count, rows)):
        steps = packed[count + extra].astype(jnp.int32).astype(jnp.float32)
        scales[pl.ds(extra * rows, rows), :] = jnp.exp2(steps * (1 / 256)) * (1 / LEVELS)


def store_scales(packed, count, tops):
    rows = packed.shape[1]
    for extra in range(extra_blocks(count, rows)):
        here = pl.ds(extra * rows, rows)
        steps = jnp.ceil(jnp.log2(jnp.maximum(tops[here, :], 1e-30)) * 256) + 2
        packed[count + extra] = steps.astype(jnp.int32).astype(jnp.int16)
        tops[here, :] = jnp.exp2(steps * (-1 / 256)) * LEVELS


def top_of(block):
    return jnp.max(jnp.abs(block), axis=0, keepdims=True)


def loop(count, step, unroll=4):
    lax.fori_loop(0, count, lambda index, carry: (step(index), carry)[1], 0, unroll=unroll)


def split_kernel(kept, across, own, *refs):
    *outs, tops, total = refs
    count = own.shape[0]

    def keep(index):
        own[index] = kept[0, index] + across[0, index]

    loop(count, keep)
    for step, out in enumerate(outs):

        def add(index, step=step):
            block = kept[step + 1, index] + across[step + 1, index]
            total[index] = block
            tops[pl.ds(index, 1), :] = top_of(block)

        loop(count, add)
        store_scales(out, count, tops)

        def put(index, out=out):
            out[index] = pack_block(total[index], tops[pl.ds(index, 1), :])

        loop(count, put)


def scale_scratch(count, rows, width):
    return pltpu.VMEM((extra_blocks(count, rows) * rows, width), jnp.float32)


VMEM_SPEC = pl.BlockSpec(memory_space=pltpu.VMEM)
PARAMS = pltpu.CompilerParams(vmem_limit_bytes=VMEM_LIMIT)


def split_columns(kept, across):
    columns, count, rows, width = kept.shape
    return pl.pallas_call(
        split_kernel,
        out_shape=[jax.ShapeDtypeStruct((count, rows, width), jnp.float32)]
        + [packed_shape(count, rows, width)] * (columns - 1),
        in_specs=[VMEM_SPEC] * 2,
        out_specs=[VMEM_SPEC] * columns,
        scratch_shapes=[
            scale_scratch(count, rows, width),
            pltpu.VMEM((count, rows, width), jnp.float32),
        ],
        cost_estimate=TINY,
        compiler_params=PARAMS,
    )(kept, across)


def combine_kernel(counts, arrivals, keep_own, targets, *refs):
    flat, refs = refs[: len(counts) * (arrivals + 1)], refs[len(counts) * (arrivals + 1) :]
    outs, (total, tops, *scales) = refs[: -2 - arrivals], refs[-2 - arrivals :]
    share = outs[-1].shape[0] - extra_blocks_of(outs[-1])
    base = 0
    for part, count in enumerate(counts):
        own, *others = flat[part * (arrivals + 1) : (part + 1) * (arrivals + 1)]
        for other, scale in zip(others, scales):
            load_scales(other, count, scale)

        def add(index, own=own, others=others, base=base):
            block = own[index]
            for other, scale in zip(others, scales):
                block = block + unpack_block(other[index], scale[pl.ds(index, 1), :])
            total[targets[base + index]] = block

        loop(count, add)
        base += count
    packs = outs
    if keep_own:
        packs = outs[1:]

        def keep(index):
            outs[0][index] = total[index]

        loop(share, keep)
    for spot, out in enumerate(packs):
        start = (spot + 1) * share if keep_own else spot * share

        def look(index, start=start):
            tops[pl.ds(index, 1), :] = top_of(total[start + index])

        loop(share, look)
        store_scales(out, share, tops)

        def put(index, out=out, start=start):
            out[index] = pack_block(total[start + index], tops[pl.ds(index, 1), :])

        loop(share, put)


def extra_blocks_of(packed):
    blocks, rows = packed.shape[:2]
    count = next(n for n in range(blocks + 1) if n + extra_blocks(n, rows) == blocks)
    return blocks - count


def combine(targets, groups, share, keep_own):
    flat = [value for group in groups for value in group]
    _, rows, width = flat[0].shape
    counts = tuple(group[0].shape[0] for group in groups)
    whole = sum(counts)
    pieces = whole // share
    outs = [packed_shape(share, rows, width)] * (pieces - keep_own)
    if keep_own:
        outs = [jax.ShapeDtypeStruct((share, rows, width), jnp.float32)] + outs
    arrivals = len(groups[0]) - 1
    return pl.pallas_call(
        functools.partial(combine_kernel, counts, arrivals, keep_own),
        out_shape=outs,
        grid_spec=pltpu.PrefetchScalarGridSpec(
            num_scalar_prefetch=1,
            grid=(),
            in_specs=[VMEM_SPEC] * len(flat),
            out_specs=[VMEM_SPEC] * len(outs),
            scratch_shapes=[
                pltpu.VMEM((whole, rows, width), jnp.float32),
                scale_scratch(share, rows, width),
            ]
            + [scale_scratch(max(counts), rows, width)] * arrivals,
        ),
        cost_estimate=TINY,
        compiler_params=PARAMS,
    )(targets, *flat)


def turn_kernel(column, *refs):
    *parts, out, whole, scales, tops = refs
    share = parts[0].shape[0] - extra_blocks_of(parts[0])
    columns = out.shape[0]
    groups = out.shape[1] - extra_blocks(whole.shape[0] // columns, out.shape[2])
    rows, width = out.shape[2:]
    for spot, part in enumerate(parts):
        load_scales(part, share, scales)

        def fill(index, part=part, spot=spot):
            whole[spot * share + index] = unpack_block(part[index], scales[pl.ds(index, 1), :])

        loop(share, fill)
    for group in range(groups):
        block = whole[group * columns : (group + 1) * columns].reshape(columns * rows, width).T
        for step in range(columns):
            whole[group * columns + step] = block[step * rows : (step + 1) * rows]
    for step in range(columns):
        target = column[0] ^ step

        def look(index, step=step):
            tops[pl.ds(index, 1), :] = top_of(whole[index * columns + step])

        loop(groups, look, unroll=2)
        store_scales(out.at[target], groups, tops)

        def put(index, step=step, target=target):
            block = whole[index * columns + step]
            out[target, index] = pack_block(block, tops[pl.ds(index, 1), :])

        loop(groups, put, unroll=2)


def turn(column, parts, share):
    columns = lax.axis_size("aux")
    _, rows, width = parts[0].shape
    whole = share * len(parts)
    one = packed_shape(whole // columns, rows, width)
    return pl.pallas_call(
        turn_kernel,
        out_shape=jax.ShapeDtypeStruct((columns,) + one.shape, one.dtype),
        grid_spec=pltpu.PrefetchScalarGridSpec(
            num_scalar_prefetch=1,
            grid=(),
            in_specs=[VMEM_SPEC] * len(parts),
            out_specs=VMEM_SPEC,
            scratch_shapes=[
                pltpu.VMEM((whole, rows, width), jnp.float32),
                scale_scratch(share, rows, width),
                scale_scratch(whole // columns, rows, width),
            ],
        ),
        cost_estimate=TINY,
        compiler_params=PARAMS,
    )(column.reshape(1), *parts)


def place_kernel(share, columns, kinds, sources, slots, *refs):
    *inputs, matrix, tiles, direct_scales, mirror_scales = refs
    directs, mirrors = inputs[: len(inputs) // 2], inputs[len(inputs) // 2 :]
    here, rows, _ = matrix.shape
    tile_count = kinds.shape[0] // here
    width = matrix.shape[2] // tile_count
    pack = width // rows
    chips = directs[0].shape[0]
    half = chips * share
    groups = half // pack
    lane = lax.broadcasted_iota(jnp.int32, (rows, width), 1) // rows
    for side in range(2):
        for chip in range(chips):
            load_scales(directs[side].at[chip], share, direct_scales.at[side, chip])
        for step in range(pack):
            load_scales(mirrors[side].at[step], groups, mirror_scales.at[side, step])

    def direct_of(source, write):
        for side in range(2):

            @pl.when(source // half == side)
            def _():
                inside = source - side * half
                chip = inside // share
                index = inside - chip * share
                write(
                    unpack_block(
                        directs[side][chip, index],
                        direct_scales[side, chip, pl.ds(index, 1), :],
                    )
                )

    for tile in range(here):

        def one(other, tile=tile):
            spot = tile * tile_count + other
            kind = kinds[spot]
            source = sources[spot]
            target = pl.ds(pl.multiple_of(other * width, width), width)

            def write(block):
                matrix[tile, :, target] = block

            @pl.when(kind == 0)
            def _():
                write(jnp.zeros((rows, width), jnp.float32))

            @pl.when(kind == 1)
            def _():
                direct_of(source, write)

            for side in range(2):

                @pl.when((kind == 2) & (source // half == side))
                def _():
                    inside = source - side * half
                    group = inside // pack
                    spot_in = inside - group * pack
                    total = jnp.zeros((rows, width), jnp.float32)
                    for step in range(pack):
                        column = columns[step]
                        block = unpack_block(
                            mirrors[side][step, group],
                            mirror_scales[side, step, pl.ds(group, 1), :],
                        )
                        moved = pltpu.roll(block, ((column - spot_in + pack) % pack) * rows, 1)
                        total = jnp.where(lane == column, moved, total)
                    write(total)

        loop(tile_count, one, unroll=1)

    def fill(slot):
        source = slots[slot]

        def write(block):
            tiles[0, slot] = block

        @pl.when(source < 0)
        def _():
            write(jnp.zeros((rows, width), jnp.float32))

        @pl.when(source >= 0)
        def _():
            direct_of(source, write)

    loop(tiles.shape[1], fill, unroll=1)


def place(columns, kinds, sources, slots, directs, mirrors, share, here, tile_count):
    chips, _, rows, width = directs[0].shape
    pack = mirrors[0].shape[0]
    groups = chips * share // pack
    return pl.pallas_call(
        functools.partial(place_kernel, share),
        out_shape=(
            jax.ShapeDtypeStruct((here, rows, tile_count * width), jnp.float32),
            jax.ShapeDtypeStruct((1, slots.shape[0], rows, width), jnp.float32),
        ),
        grid_spec=pltpu.PrefetchScalarGridSpec(
            num_scalar_prefetch=4,
            grid=(),
            in_specs=[VMEM_SPEC] * 4,
            out_specs=[VMEM_SPEC] * 2,
            scratch_shapes=[
                pltpu.VMEM((2, chips) + scale_scratch(share, rows, width).shape, jnp.float32),
                pltpu.VMEM((2, pack) + scale_scratch(groups, rows, width).shape, jnp.float32),
            ],
        ),
        cost_estimate=TINY,
        compiler_params=PARAMS,
    )(columns, kinds, sources, slots, *directs, *mirrors)


def take(value, index):
    return lax.dynamic_index_in_dim(value, index, 0, keepdims=False)


def body(factors, pairs, shared, owners):
    aux_rows, here, orbitals, width = factors.shape
    pair_size = lax.axis_size("pair")
    aux_size = lax.axis_size("aux")
    chips = pair_size // 2
    tile_count = here * pair_size
    pair_count = pairs.shape[0]
    rows = width // aux_size
    slot_count = 4 * (pair_count // pair_size)
    me = lax.axis_index("pair")
    core = me % 2
    chip = me // 2
    column = lax.axis_index("aux")
    depth = aux_rows // pair_size
    pack = aux_size
    unit = max(pack, chips)
    half = -(-(-(-pair_count // 2)) // unit) * unit
    share = half // chips
    padded = 2 * half

    pair_ids = jnp.arange(pair_count, dtype=jnp.int32)
    lefts, rights = pairs[:, 0], pairs[:, 1]
    same_owner = owners[:, None] == owners[None, :]
    rank = jnp.sum(
        (same_owner & (pair_ids[None, :] < pair_ids[:, None])).astype(jnp.int32), axis=1
    )
    tile_ids = jnp.arange(tile_count, dtype=jnp.int32)
    all_chips = jnp.arange(chips, dtype=jnp.int32)[:, None]
    steps_away = (tile_ids // (2 * here)) ^ all_chips
    is_last = (steps_away == chips - 1).astype(jnp.int32)
    group_of = is_last + is_last * (tile_ids % here == here - 1)
    left_hot = (lefts[:, None] == tile_ids).astype(jnp.int32)
    right_hot = (rights[:, None] == tile_ids).astype(jnp.int32)
    left_group = jnp.sum(left_hot[None] * group_of[:, None], axis=2)
    right_group = jnp.sum(right_hot[None] * group_of[:, None], axis=2)
    ready_at = jnp.maximum(left_group, right_group)
    arrival = ((tile_ids // here) ^ me) * here + tile_ids % here
    left_slots = jnp.sum(left_hot * arrival, axis=1)
    right_slots = jnp.sum(right_hot * arrival, axis=1)
    ready = take(ready_at, chip)

    real_half = -(-pair_count // 2)
    all_pairs = tile_count * (tile_count + 1) // 2
    bounds, enough = [0], jnp.bool_(True)
    stage_of = [here - 1]
    for stage in stage_of:
        known = tile_count - 2 * (here - stage)
        part = known * (known + 1) / 2 / all_pairs
        spread = (real_half * part * (1 - part) * (1 - real_half / all_pairs)) ** 0.5
        early = int(real_half * part - 3.75 * spread)
        bounds.append(early)
        ahead = (ready_at <= (stage if here > 1 else 0)).astype(jnp.int32)
        ahead = jnp.pad(ahead, ((0, 0), (0, padded - pair_count)))
        enough &= jnp.all(jnp.sum(ahead.reshape(chips, 2, half), axis=2) >= early)
    bounds.append(half)

    values = jnp.stack([left_slots, right_slots, shared[:, 0], ready])
    values = jnp.pad(values, ((0, 0), (0, padded - pair_count)))
    values = values.at[3, pair_count:].set(64) if padded > pair_count else values
    values = values.reshape(4, 2, half)
    local_ids = jnp.arange(half, dtype=jnp.int32)
    target_of = ((local_ids // share) ^ chip) * share + local_ids % share
    key = values[3] * half + local_ids
    spot_of = jnp.sum((key[:, None, :] < key[:, :, None]).astype(jnp.int32), axis=2)
    sorter = spot_of[:, None, :] == local_ids[:, None]
    fields = jnp.concatenate([values[:3], jnp.broadcast_to(target_of, (1, 2, half))])
    fields = jnp.sum(jnp.where(sorter[None], fields[:, :, None, :], 0), axis=3).astype(jnp.int32)
    mine = take(jnp.swapaxes(fields, 0, 1), core)
    theirs = take(jnp.swapaxes(fields, 0, 1), 1 - core)

    local = pair_ids % half
    part_core = pair_ids // half
    final_pos = (part_core ^ core) * half + ((local // share) ^ chip) * share + local % share
    my_rows = me * here + jnp.arange(here, dtype=jnp.int32)
    others = jnp.arange(tile_count, dtype=jnp.int32)
    is_direct = (lefts == my_rows[:, None, None]) & (rights == others[None, :, None])
    is_mirror = (rights == my_rows[:, None, None]) & (lefts == others[None, :, None])
    any_direct = jnp.any(is_direct, axis=-1)
    any_mirror = jnp.any(is_mirror, axis=-1)
    kinds = jnp.where(any_direct, 1, jnp.where(any_mirror, 2, 0)).astype(jnp.int32).reshape(-1)
    chosen = jnp.where(any_direct[..., None], is_direct, is_mirror)
    sources = jnp.sum(jnp.where(chosen, final_pos, 0), axis=-1).astype(jnp.int32).reshape(-1)
    slot_ids = jnp.arange(slot_count, dtype=jnp.int32)
    matches = (owners[None, :] == me) & (rank[None, :] == slot_ids[:, None])
    slots = jnp.sum(jnp.where(matches, final_pos + 1, 0), axis=1).astype(jnp.int32) - 1
    columns = column ^ jnp.arange(aux_size, dtype=jnp.int32)

    def piece(step, low, high, *earlier):
        source = lax.optimization_barrier((factors, earlier))[0] if earlier else factors
        start = ((me ^ step) * depth, low, 0, 0)
        return lax.dynamic_slice(source, start, (depth, high - low, orbitals, width))

    last = [pair_size - 2, pair_size - 1]
    far = [(step, 0, here) for step in range(pair_size - 3, 3, -1)]
    far += [(step, inner, inner + 1) for inner in range(here) for step in last]
    sent, order = {}, []
    for spot, (step, low, high) in enumerate(far):
        gate = order[spot - 2 : spot - 2 + 1] if spot >= 2 else ([first] if spot else [])
        block = piece(step, low, high, *gate)
        sent[step, low] = swap(block, "pair", pair_size, step)
        order.append(sent[step, low])
        if spot == 0:
            first = block
    for step in (3, 2, 1):
        sent[step, 0] = swap(piece(step, 0, here, first), "pair", pair_size, step)
    sent[0, 0] = piece(0, 0, here, first)
    parts = [
        [key for key in sent if key[0] not in last or key[1] < stage] for stage in stage_of
    ] + [list(sent)]

    def chip_blocks(keys, low, high, *earlier):
        given = [(step * here + inner, sent[step, inner]) for step, inner in keys]
        away = contract(given, theirs[:3, low:high], column, tile_count, aux_size, earlier)
        kept = contract(given, mine[:3, low:high], column, tile_count, aux_size, (away,))
        own, *others = split_columns(kept, swap(away, "pair", pair_size, 1))
        return [own] + [
            swap(other, "aux", aux_size, step + 1) for step, other in enumerate(others)
        ], kept

    groups, earlier = [], ()
    for keys, low, high in zip(parts, bounds[:-1], bounds[1:]):
        group, kept = chip_blocks(keys, low, high, *earlier)
        groups.append(group)
        earlier = (kept,)
    shares = combine(mine[3], groups, share, True)

    shares = lax.cond(
        enough,
        lambda: list(shares),
        lambda: list(combine(mine[3], [chip_blocks(list(sent), 0, half)[0]], share, True)),
    )

    line = [shares[0]] + [
        swap(shares[step], "pair", pair_size, 2 * step) for step in range(1, chips)
    ]
    total = combine(jnp.arange(share, dtype=jnp.int32), [line], share, False)[0]
    line = [total] + [swap(total, "pair", pair_size, 2 * step) for step in range(1, chips)]
    own_direct = jnp.stack(line)
    other_direct = swap(own_direct, "pair", pair_size, 1)

    turned = turn(column, line, share)
    own_mirror = jnp.stack(
        [turned[0]] + [swap(turned[step], "aux", aux_size, step) for step in range(1, aux_size)]
    )
    other_mirror = swap(own_mirror, "pair", pair_size, 1)
    return place(
        columns,
        kinds,
        sources,
        slots,
        (own_direct, other_direct),
        (own_mirror, other_mirror),
        share,
        here,
        tile_count,
    )


def solution(mesh):
    placed = (P("aux", "pair", None, None), P(), P(None, "aux"), P())
    return jax.shard_map(
        body,
        mesh=mesh,
        in_specs=placed,
        out_specs=(P("pair", "aux", None), P("pair", None, "aux", None)),
        check_vma=False,
    )
```

time: 187 us -> 155 us (0.83)
  waiting for transfers between devices: 97.2 us -> 52.4 us
  Pallas kernels: 20 us -> 32.7 us
  starting transfers between devices: 43.2 us -> 51 us
  local copies, waits for them, and re-layouts: 18.8 us -> 12.9 us
    ppermute x22 -> x28, waiting for transfers between devices: 97.2 us -> 52.4 us  [swap(): return lax.ppermute(value, axis, [(i, i ^ step) for i in range(size)])]
    pallas_call x4 -> x10, Pallas kernels: 20 us -> 32.7 us  [the longest x4 17.5 us: contract(): pl.pallas_call(functools.partial(contract_kernel, spots), out_shape=jax.S...]
    unnamed x42 -> x37, local copies, waits for them, and re-layouts: 13.8 us -> 1.53 us
    dynamic_slice x0 -> x6, local copies, waits for them, and re-layouts: none -> 7.92 us  [piece(): lax.dynamic_slice(source, start, (depth, high - low, orbitals, width))]
    ppermute x22 -> x28, starting transfers between devices: 43.2 us -> 51 us  [swap(): return lax.ppermute(value, axis, [(i, i ^ step) for i in range(size)])]
    squeeze x5, local copies, waits for them, and re-layouts: 4 us -> 0.16 us  [the longest x4 0.15 us: contract(): table[2]]
    cond x0 -> x3, local copies, waits for them, and re-layouts: none -> 2.67 us
    add x3, other arithmetic: 2.5 us -> 0.03 us  [the longest x1 0.01 us: body(): target_of = (local_ids // share ^ chip) * share + local_ids % share]
  transfers between devices with their start and end apart: 22 -> 28, of which waited for: 12 -> 14; matrix products, arithmetic and copies ran while one was open for 1% -> 7% of each run, Pallas kernels for 5% -> 15%
where the time goes in v3:
time: 155 us; the launch traced here: 154 us
  waiting for transfers between devices  52.4 us (34%)
  starting transfers between devices  51 us (33%)
  Pallas kernels  32.7 us (21%)
  local copies, waits for them, and re-layouts  12.9 us (8%)
  other arithmetic  3.07 us (2%)
  between operations  1.69 us (1%)
    ppermute x28, waiting for transfers between devices, swap(): return lax.ppermute(value, axis, [(i, i ^ step) for i in range(size)])  52.4 us
    ppermute x28, starting transfers between devices, swap(): return lax.ppermute(value, axis, [(i, i ^ step) for i in range(size)])  51 us
    pallas_call x4, Pallas kernels, contract(): pl.pallas_call(functools.partial(contract_kernel, spots), out_shape=jax.S...  17.5 us
    dynamic_slice x6, local copies, waits for them, and re-layouts, piece(): lax.dynamic_slice(source, start, (depth, high - low, orbitals, width))  7.92 us
    pallas_call x2, Pallas kernels, split_columns(): pl.pallas_call(split_kernel, out_shape=[jax.ShapeDtypeStruct((count, rows...  5.31 us
    pallas_call x2, Pallas kernels, combine(): pl.pallas_call(functools.partial(combine_kernel, counts, arrivals, keep_o...  4.57 us
    pallas_call x1, Pallas kernels, place(): pl.pallas_call(functools.partial(place_kernel, share), out_shape=(jax.Sha...  4.38 us
  transfers between devices with their start and end apart: 28, of which 14 were waited for; matrix products, arithmetic and copies ran while one was open for 7% of the time, Pallas kernels for 15%

profile of v3, /device:TPU:0, one launch (start us, length us, event | category | flops | bytes accessed | tf_op | source)
XLA Modules:
  0.0 153.8 jit_solution(3808097117610539390)
XLA Ops:
  0.7 1.0 constant_dynamic-slice_fusion.8
  1.7 3.5 %collective-permute-start.4 = (bf16[12,2,64,128]{3,2,1,0:T(8,128)(2,1)S(1)}, bf16[12,2,64,128]{3,2,1,0:T(8,128)(2,1)S(1)}, u32[]{:S(2)}, u32[]{:S(2)}) collective-permute-start(bf16[12,2,64,128]{3,2,1,0:T(8,128)(2,1)S(1)} %constant_dynamic-slice_fusion.8), channel_id=1, source_target_pairs={{0,20},{4,16},{8,28},{12,24},{16,4},{20,0},{24,12},{28,8},{1,21},{... | collective-permute-start | bytes 1179656 | tf_op jit(solution)/shard_map/ppermute | solution.py:15
  5.2 2.7 %constant_dynamic-slice_fusion.12 = (bf16[12,2,64,128]{3,2,1,0:T(8,128)(2,1)S(1)}, bf16[12,2,64,128]{3,2,1,0:T(8,128)(2,1)}, bf16[12,2,64,128]{3,2,1,0:T(8,128)(...) fusion(bf16[96,2,64,128]{3,2,1,0:T(8,128)(2,1)} %param.6, s32[]{:T(128)S(6)} %select_n.174, ...), kind=kLoop, calls=%fused_computation.48 | loop fusion | bytes 3932180 | tf_op jit(solution)/shard_map/dynamic_slice | solution.py:494
  8.6 1.6 %collective-permute-start.11 = (bf16[12,2,64,128]{3,2,1,0:T(8,128)(2,1)}, bf16[12,2,64,128]{3,2,1,0:T(8,128)(2,1)S(1)}, u32[]{:S(2)}, u32[]{:S(2)}) collective-permute-start(bf16[12,2,64,128]{3,2,1,0:T(8,128)(2,1)} %get-tuple-element.104), channel_id=1, source_target_pairs={{0,8},{4,12},{8,0},{12,4},{16,24},{20,28},{24,16},{28,20},{1,9},{5... | collective-permute-start | bytes 1179656 | tf_op jit(solution)/shard_map/ppermute | solution.py:15
  12.9 9.7 %collective-permute-done.4.refs_0_ = bf16[12,2,64,128]{3,2,1,0:T(8,128)(2,1)S(1)} collective-permute-done((bf16[12,2,64,128]{3,2,1,0:T(8,128)(2,1)S(1)}, bf16[12,2,64,128]{3,2,1,0:T(8,128)(2,1)S(1)}, u32[]{:S(2)}, u32[]{:S(2)}) %collective-permute-start.4) | collective-permute-done | bytes 393248 | tf_op jit(solution)/shard_map/ppermute | solution.py:15
  22.6 1.1 constant_dynamic-slice_fusion.6
  23.7 5.0 %collective-permute-start.6 = (bf16[12,1,64,128]{3,2,1,0:T(8,128)(2,1)S(1)}, bf16[12,1,64,128]{3,2,1,0:T(8,128)(2,1)S(1)}, u32[]{:S(2)}, u32[]{:S(2)}) collective-permute-start(bf16[12,1,64,128]{3,2,1,0:T(8,128)(2,1)S(1)} %constant_dynamic-slice_fusion.6), channel_id=1, source_target_pairs={{0,24},{4,28},{8,16},{12,20},{16,8},{20,12},{24,0},{28,4},{1,25},{... | collective-permute-start | bytes 589832 | tf_op jit(solution)/shard_map/ppermute | solution.py:15
  28.7 11.5 %collective-permute-done.5.refs_1_ = bf16[12,2,64,128]{3,2,1,0:T(8,128)(2,1)S(1)} collective-permute-done((bf16[12,2,64,128]{3,2,1,0:T(8,128)(2,1)}, bf16[12,2,64,128]{3,2,1,0:T(8,128)(2,1)S(1)}, u32[]{:S(2)}, u32[]{:S(2)}) %collective-permute-start.5) | collective-permute-done | bytes 393248 | tf_op jit(solution)/shard_map/ppermute | solution.py:15
  40.2 1.1 constant_dynamic-slice_fusion.5
  42.2 4.1 %collective-permute-done.6.refs_2_ = bf16[12,1,64,128]{3,2,1,0:T(8,128)(2,1)S(1)} collective-permute-done((bf16[12,1,64,128]{3,2,1,0:T(8,128)(2,1)S(1)}, bf16[12,1,64,128]{3,2,1,0:T(8,128)(2,1)S(1)}, u32[]{:S(2)}, u32[]{:S(2)}) %collective-permute-start.6) | collective-permute-done | bytes 196640 | tf_op jit(solution)/shard_map/ppermute | solution.py:15
  46.3 1.0 constant_dynamic-slice_fusion.4
  47.3 2.6 %collective-permute-start.8 = (bf16[12,1,64,128]{3,2,1,0:T(8,128)(2,1)S(1)}, bf16[12,1,64,128]{3,2,1,0:T(8,128)(2,1)S(1)}, u32[]{:S(2)}, u32[]{:S(2)}) collective-permute-start(bf16[12,1,64,128]{3,2,1,0:T(8,128)(2,1)S(1)} %constant_dynamic-slice_fusion.4), channel_id=1, source_target_pairs={{0,24},{4,28},{8,16},{12,20},{16,8},{20,12},{24,0},{28,4},{1,25},{... | collective-permute-start | bytes 589832 | tf_op jit(solution)/shard_map/ppermute | solution.py:15
  50.2 1.0 constant_dynamic-slice_fusion.3
  51.2 2.4 %collective-permute-start.9 = (bf16[12,1,64,128]{3,2,1,0:T(8,128)(2,1)S(1)}, bf16[12,1,64,128]{3,2,1,0:T(8,128)(2,1)S(1)}, u32[]{:S(2)}, u32[]{:S(2)}) collective-permute-start(bf16[12,1,64,128]{3,2,1,0:T(8,128)(2,1)S(1)} %constant_dynamic-slice_fusion.3), channel_id=1, source_target_pairs={{0,28},{4,24},{8,20},{12,16},{16,12},{20,8},{24,4},{28,0},{1,29},{... | collective-permute-start | bytes 589832 | tf_op jit(solution)/shard_map/ppermute | solution.py:15
  53.7 0.9 copy-done.11
  54.7 4.4 %shard_map.59.refs_8_ = f32[4,22,32,128]{3,2,1,0:T(8,128)S(1)} custom-call(s32[22]{0:T(128)S(1)} %get-tuple-element.121.left, s32[22]{0:T(128)S(1)} %get-tuple-element.120.right, s32[22]{0:T(128)S(1)} %get-tuple-element.119.weight, s32[1]{0:T(128)} %bitcast.17.column, bf16[12,2,64,128]{3,2,1,0:T(8,128)(2,1)S(1)} %collective-permute-done.4.refs_0_, ...), custom_call_target="tpu_custom_call" | custom-call | flops 1 | bytes 1 | tf_op jit(solution)/shard_map/pallas_call | solution.py:46
  59.1 2.6 %collective-permute-start.13 = (f32[4,22,32,128]{3,2,1,0:T(8,128)S(1)}, f32[4,22,32,128]{3,2,1,0:T(8,128)}, u32[]{:S(2)}, u32[]{:S(2)}) collective-permute-start(f32[4,22,32,128]{3,2,1,0:T(8,128)S(1)} %shard_map.59.refs_8_), channel_id=1, source_target_pairs={{0,4},{4,0},{8,12},{12,8},{16,20},{20,16},{24,28},{28,24},{1,5},{5... | collective-permute-start | bytes 4325384 | tf_op jit(solution)/shard_map/ppermute | solution.py:15
  61.7 4.5 %shard_map.60.kept.refs_10_ = f32[4,22,32,128]{3,2,1,0:T(8,128)S(1)} custom-call(s32[22]{0:T(128)S(1)} %get-tuple-element.124.left, s32[22]{0:T(128)S(1)} %get-tuple-element.123.right, s32[22]{0:T(128)S(1)} %get-tuple-element.122.weight, s32[1]{0:T(128)} %bitcast.17.column, bf16[12,2,64,128]{3,2,1,0:T(8,128)(2,1)} %copy-done.2, ...), custom_call_target="tpu_custom_call" | custom-call | flops 1 | bytes 1 | tf_op jit(solution)/shard_map/pallas_call | solution.py:46
  66.3 4.0 %shard_map.62.refs_10_ = f32[4,18,32,128]{3,2,1,0:T(8,128)} custom-call(s32[18]{0:T(128)S(1)} %get-tuple-element.115.left, s32[18]{0:T(128)S(1)} %get-tuple-element.114.right, s32[18]{0:T(128)S(1)} %get-tuple-element.113.weight, s32[1]{0:T(128)} %bitcast.17.column, bf16[12,2,64,128]{3,2,1,0:T(8,128)(2,1)S(1)} %copy-done.3, ...), custom_call_target="tpu_custom_call" | custom-call | flops 1 | bytes 1 | tf_op jit(solution)/shard_map/pallas_call | solution.py:46
  71.0 4.6 %shard_map.63.kept = f32[4,18,32,128]{3,2,1,0:T(8,128)S(1)} custom-call(s32[18]{0:T(128)S(1)} %get-tuple-element.118.left, s32[18]{0:T(128)S(1)} %get-tuple-element.117.right, s32[18]{0:T(128)S(1)} %get-tuple-element.116.weight, s32[1]{0:T(128)} %bitcast.17.column, bf16[12,2,64,128]{3,2,1,0:T(8,128)(2,1)} %copy-done.2, bf16[12,2,64,128]{3,2,1,0:T(8,128)(2,1)} %copy-done.14, ...), custom_call_target="tpu_custom_call" | custom-call | flops 1 | bytes 1 | tf_op jit(solution)/shard_map/pallas_call | solution.py:46
  75.6 2.6 %shard_map.64 = (f32[18,32,128]{2,1,0:T(8,128)S(1)}, s16[19,32,128]{2,1,0:T(8,128)(2,1)S(1)}, s16[19,32,128]{2,1,0:T(8,128)(2,1)}, s16[19,32,128]{2,1,0:T(8,128)(2,1)}) custom-call(f32[4,18,32,128]{3,2,1,0:T(8,128)S(1)} %shard_map.63.kept, f32[4,18,32,128]{3,2,1,0:T(8,128)} %collective-permute-done.17.across), custom_call_target="tpu_custom_call" | custom-call | flops 1 | bytes 1 | tf_op jit(solution)/shard_map/pallas_call | solution.py:139
  78.2 5.8 %collective-permute-start.18 = (s16[19,32,128]{2,1,0:T(8,128)(2,1)S(1)}, s16[19,32,128]{2,1,0:T(8,128)(2,1)S(1)}, u32[]{:S(2)}, u32[]{:S(2)}) collective-permute-start(s16[19,32,128]{2,1,0:T(8,128)(2,1)S(1)} %get-tuple-element.80), channel_id=1, source_target_pairs={{0,1},{1,0},{2,3},{3,2},{4,5},{5,4},{6,7},{7,6},{8,9},{9,8},{10,11... | collective-permute-start | bytes 466952 | tf_op jit(solution)/shard_map/ppermute | solution.py:15
  84.0 1.5 collective-permute-start.19
  85.6 2.7 %shard_map.61 = (f32[22,32,128]{2,1,0:T(8,128)S(1)}, s16[23,32,128]{2,1,0:T(8,128)(2,1)}, s16[23,32,128]{2,1,0:T(8,128)(2,1)S(1)}, s16[23,32,128]{2,1,0:T(8,128)(2,1)S(1)}) custom-call(f32[4,22,32,128]{3,2,1,0:T(8,128)S(1)} %shard_map.60.kept.refs_10_, f32[4,22,32,128]{3,2,1,0:T(8,128)} %collective-permute-done.13.across), custom_call_target="tpu_custom_call" | custom-call | flops 1 | bytes 1 | tf_op jit(solution)/shard_map/pallas_call | solution.py:139
  88.3 1.9 %collective-permute-start.14 = (s16[23,32,128]{2,1,0:T(8,128)(2,1)}, s16[23,32,128]{2,1,0:T(8,128)(2,1)S(1)}, u32[]{:S(2)}, u32[]{:S(2)}) collective-permute-start(s16[23,32,128]{2,1,0:T(8,128)(2,1)} %get-tuple-element.76), channel_id=1, source_target_pairs={{0,1},{1,0},{2,3},{3,2},{4,5},{5,4},{6,7},{7,6},{8,9},{9,8},{10,11... | collective-permute-start | bytes 565256 | tf_op jit(solution)/shard_map/ppermute | solution.py:15
  90.3 1.5 collective-permute-start.15
  94.0 2.8 %collective-permute-done.14.refs_1_ = s16[23,32,128]{2,1,0:T(8,128)(2,1)S(1)} collective-permute-done((s16[23,32,128]{2,1,0:T(8,128)(2,1)}, s16[23,32,128]{2,1,0:T(8,128)(2,1)S(1)}, u32[]{:S(2)}, u32[]{:S(2)}) %collective-permute-start.14) | collective-permute-done | bytes 188448 | tf_op jit(solution)/shard_map/ppermute | solution.py:15
  96.8 5.0 %collective-permute-done.15.refs_2_ = s16[23,32,128]{2,1,0:T(8,128)(2,1)S(1)} collective-permute-done((s16[23,32,128]{2,1,0:T(8,128)(2,1)S(1)}, s16[23,32,128]{2,1,0:T(8,128)(2,1)S(1)}, u32[]{:S(2)}, u32[]{:S(2)}) %collective-permute-start.15) | collective-permute-done | bytes 188448 | tf_op jit(solution)/shard_map/ppermute | solution.py:15
  101.8 2.9 %shard_map.65 = (f32[10,32,128]{2,1,0:T(8,128)}, s16[11,32,128]{2,1,0:T(8,128)(2,1)}, s16[11,32,128]{2,1,0:T(8,128)(2,1)}, s16[11,32,128]{2,1,0:T(8,128)(2,1)}) custom-call(s32[40]{0:T(128)S(1)} %slice_bitcast_fusion.22.targets, f32[22,32,128]{2,1,0:T(8,128)S(1)} %get-tuple-element.75.refs_0_, s16[23,32,128]{2,1,0:T(8,128)(2,1)S(1)} %collective-permute-done.14.refs_1_, ...), custom_call_target="tpu_custom_call" | custom-call | flops 1 | bytes 1 | tf_op jit(solution)/shard_map/pallas_call | solution.py:211
  104.7 2.7 %conditional.1 = ((f32[10,32,128]{2,1,0:T(8,128)}, s16[11,32,128]{2,1,0:T(8,128)(2,1)S(1)}, s16[11,32,128]{2,1,0:T(8,128)(2,1)S(1)}, s16[11,32,128]{2,1,0:T(8,128)(2,1)S(1)})) conditional(s32[]{:T(128)} %convert_element_type.55, (s32[4,40]{1,0:T(4,128)S(1)}, s32[]{:T(128)}, s32[4,40]{1,0:T(4,128)S(1)}, bf16[12,2,64,128]{3,2,1,0:T(8,128)(2,1)}, ...), branch_computations={%region_13.14_spmd, %region_14.15_spmd} | conditional | flops 4 | bytes 27200132 | solution.py:530
  104.7 0.9 copy.11
  105.6 0.9 copy.12
  107.4 10.0 %collective-permute-start.21 = (s16[11,32,128]{2,1,0:T(8,128)(2,1)S(1)}, s16[11,32,128]{2,1,0:T(8,128)(2,1)S(1)}, u32[]{:S(2)}, u32[]{:S(2)}) collective-permute-start(s16[11,32,128]{2,1,0:T(8,128)(2,1)S(1)} %get-tuple-element.84), channel_id=1, source_target_pairs={{0,8},{4,12},{8,0},{12,4},{16,24},{20,28},{24,16},{28,20},{1,9},{5... | collective-permute-start | bytes 270344 | tf_op jit(solution)/shard_map/ppermute | solution.py:15
  117.4 2.4 %collective-permute-start.23 = (s16[11,32,128]{2,1,0:T(8,128)(2,1)S(1)}, s16[11,32,128]{2,1,0:T(8,128)(2,1)S(1)}, u32[]{:S(2)}, u32[]{:S(2)}) collective-permute-start(s16[11,32,128]{2,1,0:T(8,128)(2,1)S(1)} %get-tuple-element.86), channel_id=1, source_target_pairs={{0,24},{4,28},{8,16},{12,20},{16,8},{20,12},{24,0},{28,4},{1,25},{... | collective-permute-start | bytes 270344 | tf_op jit(solution)/shard_map/ppermute | solution.py:15
  120.4 6.3 %collective-permute-done.22.refs_2_ = s16[11,32,128]{2,1,0:T(8,128)(2,1)S(1)} collective-permute-done((s16[11,32,128]{2,1,0:T(8,128)(2,1)S(1)}, s16[11,32,128]{2,1,0:T(8,128)(2,1)S(1)}, u32[]{:S(2)}, u32[]{:S(2)}) %collective-permute-start.22) | collective-permute-done | bytes 90144 | tf_op jit(solution)/shard_map/ppermute | solution.py:15
  126.7 1.7 %shard_map.66.refs_0_ = s16[11,32,128]{2,1,0:T(8,128)(2,1)S(1)} custom-call(s32[10]{0:T(128)S(1)} %iota.106.targets, f32[10,32,128]{2,1,0:T(8,128)} %get-tuple-element.83.refs_0_, s16[11,32,128]{2,1,0:T(8,128)(2,1)S(1)} %collective-permute-done.21.refs_1_, s16[11,32,128]{2,1,0:T(8,128)(2,1)S(1)} %collective-permute-done.22.refs_2_, ...), custom_call_target="tpu_custom_call" | custom-call | flops 1 | bytes 1 | tf_op jit(solution)/shard_map/pallas_call | solution.py:211
  128.4 1.5 collective-permute-start.26
  129.9 1.8 %collective-permute-start.25 = (s16[11,32,128]{2,1,0:T(8,128)(2,1)S(1)}, s16[11,32,128]{2,1,0:T(8,128)(2,1)S(1)}, u32[]{:S(2)}, u32[]{:S(2)}) collective-permute-start(s16[11,32,128]{2,1,0:T(8,128)(2,1)S(1)} %shard_map.66.refs_0_), channel_id=1, source_target_pairs={{0,16},{4,20},{8,24},{12,28},{16,0},{20,4},{24,8},{28,12},{1,17},{... | collective-permute-start | bytes 270344 | tf_op jit(solution)/shard_map/ppermute | solution.py:15
  131.7 1.1 collective-permute-start.24
  133.0 2.7 %collective-permute-done.26.refs_3_ = s16[11,32,128]{2,1,0:T(8,128)(2,1)S(1)} collective-permute-done((s16[11,32,128]{2,1,0:T(8,128)(2,1)S(1)}, s16[11,32,128]{2,1,0:T(8,128)(2,1)S(1)}, u32[]{:S(2)}, u32[]{:S(2)}) %collective-permute-start.26) | collective-permute-done | bytes 90144 | tf_op jit(solution)/shard_map/ppermute | solution.py:15
  135.7 3.6 %collective-permute-done.25.refs_2_ = s16[11,32,128]{2,1,0:T(8,128)(2,1)S(1)} collective-permute-done((s16[11,32,128]{2,1,0:T(8,128)(2,1)S(1)}, s16[11,32,128]{2,1,0:T(8,128)(2,1)S(1)}, u32[]{:S(2)}, u32[]{:S(2)}) %collective-permute-start.25) | collective-permute-done | bytes 90144 | tf_op jit(solution)/shard_map/ppermute | solution.py:15
  139.3 0.9 shard_map.67
  140.3 1.5 collective-permute-start.30
  142.5 1.3 collective-permute-start.28
  143.9 2.4 %collective-permute-done.30 = s16[11,32,128]{2,1,0:T(8,128)(2,1)S(1)} collective-permute-done((s16[11,32,128]{2,1,0:T(8,128)(2,1)S(1)}, s16[11,32,128]{2,1,0:T(8,128)(2,1)S(1)}, u32[]{:S(2)}, u32[]{:S(2)}) %collective-permute-start.30) | collective-permute-done | bytes 90144 | tf_op jit(solution)/shard_map/ppermute | solution.py:15
  146.4 1.2 collective-permute-done.29
  148.0 1.4 collective-permute-done.31.refs_3_
  149.4 4.4 %shard_map.68 = (f32[2,32,2048]{2,1,0:T(8,128)}, f32[1,40,32,128]{3,2,1,0:T(8,128)}) custom-call(s32[4]{0:T(128)S(1)} %iota_xor_fusion.columns, s32[32]{0:T(128)S(1)} %select_n.148.kinds, s32[32]{0:T(128)S(1)} %reshape.318.sources, s32[40]{0:T(128)S(1)} %broadcast_add_fusion.slots, s16[4,11,32,128]{3,2,1,0:T(8,128)(2,1)S(1)} %pad_add_fusion.refs_0_, ...), custom_call_target="tpu_custom_call" | custom-call | flops 1 | bytes 1 | tf_op jit(solution)/shard_map/pallas_call | solution.py:379
  (114 shorter events, 10.0 us)
Async XLA Ops:
  0.6 10.5 %copy-start.26 = (s32[80,1]{0,1:T(1,128)S(1)}, s32[80,1]{0,1:T(1,128)}, u32[]{:S(2)}) copy-start(s32[80,1]{0,1:T(1,128)} %param.8) | copy-start | bytes 964
  0.6 11.2 %copy-start.25 = (s32[80,2]{0,1:T(2,128)S(1)}, s32[80,2]{0,1:T(2,128)}, u32[]{:S(2)}) copy-start(s32[80,2]{0,1:T(2,128)} %param.7) | copy-start | bytes 1924
  1.7 20.9 %collective-permute-start.4 = (bf16[12,2,64,128]{3,2,1,0:T(8,128)(2,1)S(1)}, bf16[12,2,64,128]{3,2,1,0:T(8,128)(2,1)S(1)}, u32[]{:S(2)}, u32[]{:S(2)}) collective-permute-start(bf16[12,2,64,128]{3,2,1,0:T(8,128)(2,1)S(1)} %constant_dynamic-slice_fusion.8), channel_id=1, source_target_pairs={{0,20},{4,16},{8,28},{12,24},{16,4},{20,0},{24,12},{28,8},{1,21},{... | collective-permute-start | bytes 1179656 | tf_op jit(solution)/shard_map/ppermute | solution.py:15
  7.9 63.1 %copy-start = (bf16[12,2,64,128]{3,2,1,0:T(8,128)(2,1)}, bf16[12,2,64,128]{3,2,1,0:T(8,128)(2,1)S(1)}, u32[]{:S(2)}) copy-start(bf16[12,2,64,128]{3,2,1,0:T(8,128)(2,1)S(1)} %get-tuple-element.102.refs_7_.refs_9_) | copy-start | bytes 1179652
  7.9 45.7 %collective-permute-start.12 = (bf16[12,2,64,128]{3,2,1,0:T(8,128)(2,1)}, bf16[12,2,64,128]{3,2,1,0:T(8,128)(2,1)S(1)}, u32[]{:S(2)}, u32[]{:S(2)}) collective-permute-start(bf16[12,2,64,128]{3,2,1,0:T(8,128)(2,1)} %get-tuple-element.103), channel_id=1, source_target_pairs={{0,4},{4,0},{8,12},{12,8},{16,20},{20,16},{24,28},{28,24},{1,5},{5... | collective-permute-start | bytes 1179656 | tf_op jit(solution)/shard_map/ppermute | solution.py:15
  8.6 45.0 %collective-permute-start.11 = (bf16[12,2,64,128]{3,2,1,0:T(8,128)(2,1)}, bf16[12,2,64,128]{3,2,1,0:T(8,128)(2,1)S(1)}, u32[]{:S(2)}, u32[]{:S(2)}) collective-permute-start(bf16[12,2,64,128]{3,2,1,0:T(8,128)(2,1)} %get-tuple-element.104), channel_id=1, source_target_pairs={{0,8},{4,12},{8,0},{12,4},{16,24},{20,28},{24,16},{28,20},{1,9},{5... | collective-permute-start | bytes 1179656 | tf_op jit(solution)/shard_map/ppermute | solution.py:15
  10.2 43.5 %collective-permute-start.10 = (bf16[12,2,64,128]{3,2,1,0:T(8,128)(2,1)}, bf16[12,2,64,128]{3,2,1,0:T(8,128)(2,1)S(1)}, u32[]{:S(2)}, u32[]{:S(2)}) collective-permute-start(bf16[12,2,64,128]{3,2,1,0:T(8,128)(2,1)} %get-tuple-element.105), channel_id=1, source_target_pairs={{0,12},{4,8},{8,4},{12,0},{16,28},{20,24},{24,20},{28,16},{1,13},{... | collective-permute-start | bytes 1179656 | tf_op jit(solution)/shard_map/ppermute | solution.py:15
  10.2 30.0 %collective-permute-start.5 = (bf16[12,2,64,128]{3,2,1,0:T(8,128)(2,1)}, bf16[12,2,64,128]{3,2,1,0:T(8,128)(2,1)S(1)}, u32[]{:S(2)}, u32[]{:S(2)}) collective-permute-start(bf16[12,2,64,128]{3,2,1,0:T(8,128)(2,1)} %get-tuple-element.106), channel_id=1, source_target_pairs={{0,16},{4,20},{8,24},{12,28},{16,0},{20,4},{24,8},{28,12},{1,17},{... | collective-permute-start | bytes 1179656 | tf_op jit(solution)/shard_map/ppermute | solution.py:15
  22.6 39.1 %copy-start.2 = (bf16[12,2,64,128]{3,2,1,0:T(8,128)(2,1)}, bf16[12,2,64,128]{3,2,1,0:T(8,128)(2,1)S(1)}, u32[]{:S(2)}) copy-start(bf16[12,2,64,128]{3,2,1,0:T(8,128)(2,1)S(1)} %collective-permute-done.4.refs_0_) | copy-start | bytes 1179652
  23.7 22.6 %collective-permute-start.6 = (bf16[12,1,64,128]{3,2,1,0:T(8,128)(2,1)S(1)}, bf16[12,1,64,128]{3,2,1,0:T(8,128)(2,1)S(1)}, u32[]{:S(2)}, u32[]{:S(2)}) collective-permute-start(bf16[12,1,64,128]{3,2,1,0:T(8,128)(2,1)S(1)} %constant_dynamic-slice_fusion.6), channel_id=1, source_target_pairs={{0,24},{4,28},{8,16},{12,20},{16,8},{20,12},{24,0},{28,4},{1,25},{... | collective-permute-start | bytes 589832 | tf_op jit(solution)/shard_map/ppermute | solution.py:15
  40.2 13.5 %copy-start.14 = (bf16[12,2,64,128]{3,2,1,0:T(8,128)(2,1)}, bf16[12,2,64,128]{3,2,1,0:T(8,128)(2,1)S(1)}, u32[]{:S(2)}) copy-start(bf16[12,2,64,128]{3,2,1,0:T(8,128)(2,1)S(1)} %collective-permute-done.5.refs_1_) | copy-start | bytes 1179652
  41.3 8.9 %collective-permute-start.7 = (bf16[12,1,64,128]{3,2,1,0:T(8,128)(2,1)S(1)}, bf16[12,1,64,128]{3,2,1,0:T(8,128)(2,1)S(1)}, u32[]{:S(2)}, u32[]{:S(2)}) collective-permute-start(bf16[12,1,64,128]{3,2,1,0:T(8,128)(2,1)S(1)} %constant_dynamic-slice_fusion.5), channel_id=1, source_target_pairs={{0,28},{4,24},{8,20},{12,16},{16,12},{20,8},{24,4},{28,0},{1,29},{... | collective-permute-start | bytes 589832 | tf_op jit(solution)/shard_map/ppermute | solution.py:15
  46.3 24.7 %copy-start.17 = (bf16[12,1,64,128]{3,2,1,0:T(8,128)(2,1)}, bf16[12,1,64,128]{3,2,1,0:T(8,128)(2,1)S(1)}, u32[]{:S(2)}) copy-start(bf16[12,1,64,128]{3,2,1,0:T(8,128)(2,1)S(1)} %collective-permute-done.6.refs_2_) | copy-start | bytes 589828
  47.3 19.0 %collective-permute-start.8 = (bf16[12,1,64,128]{3,2,1,0:T(8,128)(2,1)S(1)}, bf16[12,1,64,128]{3,2,1,0:T(8,128)(2,1)S(1)}, u32[]{:S(2)}, u32[]{:S(2)}) collective-permute-start(bf16[12,1,64,128]{3,2,1,0:T(8,128)(2,1)S(1)} %constant_dynamic-slice_fusion.4), channel_id=1, source_target_pairs={{0,24},{4,28},{8,16},{12,20},{16,8},{20,12},{24,0},{28,4},{1,25},{... | collective-permute-start | bytes 589832 | tf_op jit(solution)/shard_map/ppermute | solution.py:15
  50.2 16.1 %copy-start.19 = (bf16[12,1,64,128]{3,2,1,0:T(8,128)(2,1)}, bf16[12,1,64,128]{3,2,1,0:T(8,128)(2,1)S(1)}, u32[]{:S(2)}) copy-start(bf16[12,1,64,128]{3,2,1,0:T(8,128)(2,1)S(1)} %collective-permute-done.7.refs_3_) | copy-start | bytes 589828
  51.2 15.0 %collective-permute-start.9 = (bf16[12,1,64,128]{3,2,1,0:T(8,128)(2,1)S(1)}, bf16[12,1,64,128]{3,2,1,0:T(8,128)(2,1)S(1)}, u32[]{:S(2)}, u32[]{:S(2)}) collective-permute-start(bf16[12,1,64,128]{3,2,1,0:T(8,128)(2,1)S(1)} %constant_dynamic-slice_fusion.3), channel_id=1, source_target_pairs={{0,28},{4,24},{8,20},{12,16},{16,12},{20,8},{24,4},{28,0},{1,29},{... | collective-permute-start | bytes 589832 | tf_op jit(solution)/shard_map/ppermute | solution.py:15
  53.6 8.0 %copy-start.5 = (bf16[12,2,64,128]{3,2,1,0:T(8,128)(2,1)}, bf16[12,2,64,128]{3,2,1,0:T(8,128)(2,1)S(1)}, u32[]{:S(2)}) copy-start(bf16[12,2,64,128]{3,2,1,0:T(8,128)(2,1)S(1)} %collective-permute-done.12.refs_6_.refs_8_) | copy-start | bytes 1179652
  53.7 8.0 %copy-start.8 = (bf16[12,2,64,128]{3,2,1,0:T(8,128)(2,1)}, bf16[12,2,64,128]{3,2,1,0:T(8,128)(2,1)S(1)}, u32[]{:S(2)}) copy-start(bf16[12,2,64,128]{3,2,1,0:T(8,128)(2,1)S(1)} %collective-permute-done.11.refs_5_.refs_7_) | copy-start | bytes 1179652
  53.7 1.0 copy-start.11
  54.6 7.0 %copy-start.12 = (bf16[12,2,64,128]{3,2,1,0:T(8,128)(2,1)S(1)}, bf16[12,2,64,128]{3,2,1,0:T(8,128)(2,1)}, u32[]{:S(2)}) copy-start(bf16[12,2,64,128]{3,2,1,0:T(8,128)(2,1)} %copy-done.11) | copy-start | bytes 1179652
  54.6 7.0 %copy-start.15 = (bf16[12,2,64,128]{3,2,1,0:T(8,128)(2,1)S(1)}, bf16[12,2,64,128]{3,2,1,0:T(8,128)(2,1)}, u32[]{:S(2)}) copy-start(bf16[12,2,64,128]{3,2,1,0:T(8,128)(2,1)} %copy-done.14) | copy-start | bytes 1179652
  59.1 26.5 %collective-permute-start.13 = (f32[4,22,32,128]{3,2,1,0:T(8,128)S(1)}, f32[4,22,32,128]{3,2,1,0:T(8,128)}, u32[]{:S(2)}, u32[]{:S(2)}) collective-permute-start(f32[4,22,32,128]{3,2,1,0:T(8,128)S(1)} %shard_map.59.refs_8_), channel_id=1, source_target_pairs={{0,4},{4,0},{8,12},{12,8},{16,20},{20,16},{24,28},{28,24},{1,5},{5... | collective-permute-start | bytes 4325384 | tf_op jit(solution)/shard_map/ppermute | solution.py:15
  61.7 4.6 %copy-start.3 = (bf16[12,2,64,128]{3,2,1,0:T(8,128)(2,1)S(1)}, bf16[12,2,64,128]{3,2,1,0:T(8,128)(2,1)}, u32[]{:S(2)}) copy-start(bf16[12,2,64,128]{3,2,1,0:T(8,128)(2,1)} %copy-done.2) | copy-start | bytes 1179652
  61.7 4.6 %copy-start.6 = (bf16[12,2,64,128]{3,2,1,0:T(8,128)(2,1)S(1)}, bf16[12,2,64,128]{3,2,1,0:T(8,128)(2,1)}, u32[]{:S(2)}) copy-start(bf16[12,2,64,128]{3,2,1,0:T(8,128)(2,1)} %copy-done.5) | copy-start | bytes 1179652
  61.7 4.6 %copy-start.9 = (bf16[12,2,64,128]{3,2,1,0:T(8,128)(2,1)S(1)}, bf16[12,2,64,128]{3,2,1,0:T(8,128)(2,1)}, u32[]{:S(2)}) copy-start(bf16[12,2,64,128]{3,2,1,0:T(8,128)(2,1)} %copy-done.8) | copy-start | bytes 1179652
  66.3 4.0 %copy-start.21 = (bf16[12,1,64,128]{3,2,1,0:T(8,128)(2,1)}, bf16[12,1,64,128]{3,2,1,0:T(8,128)(2,1)S(1)}, u32[]{:S(2)}) copy-start(bf16[12,1,64,128]{3,2,1,0:T(8,128)(2,1)S(1)} %collective-permute-done.8.refs_4_) | copy-start | bytes 589828
  66.3 4.0 %copy-start.23 = (bf16[12,1,64,128]{3,2,1,0:T(8,128)(2,1)}, bf16[12,1,64,128]{3,2,1,0:T(8,128)(2,1)S(1)}, u32[]{:S(2)}) copy-start(bf16[12,1,64,128]{3,2,1,0:T(8,128)(2,1)S(1)} %collective-permute-done.9.refs_5_) | copy-start | bytes 589828
  70.3 5.3 %collective-permute-start.17 = (f32[4,18,32,128]{3,2,1,0:T(8,128)}, f32[4,18,32,128]{3,2,1,0:T(8,128)}, u32[]{:S(2)}, u32[]{:S(2)}) collective-permute-start(f32[4,18,32,128]{3,2,1,0:T(8,128)} %shard_map.62.refs_10_), channel_id=1, source_target_pairs={{0,4},{4,0},{8,12},{12,8},{16,20},{20,16},{24,28},{28,24},{1,5},{5... | collective-permute-start | bytes 3538952 | tf_op jit(solution)/shard_map/ppermute | solution.py:15
  71.0 13.0 %copy-start.27 = (s32[80]{0:T(128)S(1)}, s32[80]{0:T(128)}, u32[]{:S(2)}) copy-start(s32[80]{0:T(128)} %param.9) | copy-start | bytes 964
  78.2 13.6 %collective-permute-start.18 = (s16[19,32,128]{2,1,0:T(8,128)(2,1)S(1)}, s16[19,32,128]{2,1,0:T(8,128)(2,1)S(1)}, u32[]{:S(2)}, u32[]{:S(2)}) collective-permute-start(s16[19,32,128]{2,1,0:T(8,128)(2,1)S(1)} %get-tuple-element.80), channel_id=1, source_target_pairs={{0,1},{1,0},{2,3},{3,2},{4,5},{5,4},{6,7},{7,6},{8,9},{9,8},{10,11... | collective-permute-start | bytes 466952 | tf_op jit(solution)/shard_map/ppermute | solution.py:15
  84.0 10.0 %collective-permute-start.19 = (s16[19,32,128]{2,1,0:T(8,128)(2,1)}, s16[19,32,128]{2,1,0:T(8,128)(2,1)S(1)}, u32[]{:S(2)}, u32[]{:S(2)}) collective-permute-start(s16[19,32,128]{2,1,0:T(8,128)(2,1)} %get-tuple-element.81), channel_id=1, source_target_pairs={{0,2},{1,3},{2,0},{3,1},{4,6},{5,7},{6,4},{7,5},{8,10},{9,11},{10,... | collective-permute-start | bytes 466952 | tf_op jit(solution)/shard_map/ppermute | solution.py:15
  85.6 8.4 %collective-permute-start.20 = (s16[19,32,128]{2,1,0:T(8,128)(2,1)}, s16[19,32,128]{2,1,0:T(8,128)(2,1)}, u32[]{:S(2)}, u32[]{:S(2)}) collective-permute-start(s16[19,32,128]{2,1,0:T(8,128)(2,1)} %get-tuple-element.82), channel_id=1, source_target_pairs={{0,3},{1,2},{2,1},{3,0},{4,7},{5,6},{6,5},{7,4},{8,11},{9,10},{10,... | collective-permute-start | bytes 466952 | tf_op jit(solution)/shard_map/ppermute | solution.py:15
  88.3 8.4 %collective-permute-start.14 = (s16[23,32,128]{2,1,0:T(8,128)(2,1)}, s16[23,32,128]{2,1,0:T(8,128)(2,1)S(1)}, u32[]{:S(2)}, u32[]{:S(2)}) collective-permute-start(s16[23,32,128]{2,1,0:T(8,128)(2,1)} %get-tuple-element.76), channel_id=1, source_target_pairs={{0,1},{1,0},{2,3},{3,2},{4,5},{5,4},{6,7},{7,6},{8,9},{9,8},{10,11... | collective-permute-start | bytes 565256 | tf_op jit(solution)/shard_map/ppermute | solution.py:15
  90.3 11.5 %collective-permute-start.15 = (s16[23,32,128]{2,1,0:T(8,128)(2,1)S(1)}, s16[23,32,128]{2,1,0:T(8,128)(2,1)S(1)}, u32[]{:S(2)}, u32[]{:S(2)}) collective-permute-start(s16[23,32,128]{2,1,0:T(8,128)(2,1)S(1)} %get-tuple-element.77), channel_id=1, source_target_pairs={{0,2},{1,3},{2,0},{3,1},{4,6},{5,7},{6,4},{7,5},{8,10},{9,11},{10,... | collective-permute-start | bytes 565256 | tf_op jit(solution)/shard_map/ppermute | solution.py:15
  91.8 10.0 %collective-permute-start.16 = (s16[23,32,128]{2,1,0:T(8,128)(2,1)S(1)}, s16[23,32,128]{2,1,0:T(8,128)(2,1)S(1)}, u32[]{:S(2)}, u32[]{:S(2)}) collective-permute-start(s16[23,32,128]{2,1,0:T(8,128)(2,1)S(1)} %get-tuple-element.78), channel_id=1, source_target_pairs={{0,3},{1,2},{2,1},{3,0},{4,7},{5,6},{6,5},{7,4},{8,11},{9,10},{10,... | collective-permute-start | bytes 565256 | tf_op jit(solution)/shard_map/ppermute | solution.py:15
  107.4 13.1 %collective-permute-start.21 = (s16[11,32,128]{2,1,0:T(8,128)(2,1)S(1)}, s16[11,32,128]{2,1,0:T(8,128)(2,1)S(1)}, u32[]{:S(2)}, u32[]{:S(2)}) collective-permute-start(s16[11,32,128]{2,1,0:T(8,128)(2,1)S(1)} %get-tuple-element.84), channel_id=1, source_target_pairs={{0,8},{4,12},{8,0},{12,4},{16,24},{20,28},{24,16},{28,20},{1,9},{5... | collective-permute-start | bytes 270344 | tf_op jit(solution)/shard_map/ppermute | solution.py:15
  117.4 9.4 %collective-permute-start.22 = (s16[11,32,128]{2,1,0:T(8,128)(2,1)S(1)}, s16[11,32,128]{2,1,0:T(8,128)(2,1)S(1)}, u32[]{:S(2)}, u32[]{:S(2)}) collective-permute-start(s16[11,32,128]{2,1,0:T(8,128)(2,1)S(1)} %get-tuple-element.85), channel_id=1, source_target_pairs={{0,16},{4,20},{8,24},{12,28},{16,0},{20,4},{24,8},{28,12},{1,17},{... | collective-permute-start | bytes 270344 | tf_op jit(solution)/shard_map/ppermute | solution.py:15
  117.4 9.4 %collective-permute-start.23 = (s16[11,32,128]{2,1,0:T(8,128)(2,1)S(1)}, s16[11,32,128]{2,1,0:T(8,128)(2,1)S(1)}, u32[]{:S(2)}, u32[]{:S(2)}) collective-permute-start(s16[11,32,128]{2,1,0:T(8,128)(2,1)S(1)} %get-tuple-element.86), channel_id=1, source_target_pairs={{0,24},{4,28},{8,16},{12,20},{16,8},{20,12},{24,0},{28,4},{1,25},{... | collective-permute-start | bytes 270344 | tf_op jit(solution)/shard_map/ppermute | solution.py:15
  128.4 7.3 %collective-permute-start.26 = (s16[11,32,128]{2,1,0:T(8,128)(2,1)S(1)}, s16[11,32,128]{2,1,0:T(8,128)(2,1)S(1)}, u32[]{:S(2)}, u32[]{:S(2)}) collective-permute-start(s16[11,32,128]{2,1,0:T(8,128)(2,1)S(1)} %shard_map.66.refs_0_), channel_id=1, source_target_pairs={{0,24},{4,28},{8,16},{12,20},{16,8},{20,12},{24,0},{28,4},{1,25},{... | collective-permute-start | bytes 270344 | tf_op jit(solution)/shard_map/ppermute | solution.py:15
  129.9 9.4 %collective-permute-start.25 = (s16[11,32,128]{2,1,0:T(8,128)(2,1)S(1)}, s16[11,32,128]{2,1,0:T(8,128)(2,1)S(1)}, u32[]{:S(2)}, u32[]{:S(2)}) collective-permute-start(s16[11,32,128]{2,1,0:T(8,128)(2,1)S(1)} %shard_map.66.refs_0_), channel_id=1, source_target_pairs={{0,16},{4,20},{8,24},{12,28},{16,0},{20,4},{24,8},{28,12},{1,17},{... | collective-permute-start | bytes 270344 | tf_op jit(solution)/shard_map/ppermute | solution.py:15
  131.7 7.6 %collective-permute-start.24 = (s16[11,32,128]{2,1,0:T(8,128)(2,1)S(1)}, s16[11,32,128]{2,1,0:T(8,128)(2,1)S(1)}, u32[]{:S(2)}, u32[]{:S(2)}) collective-permute-start(s16[11,32,128]{2,1,0:T(8,128)(2,1)S(1)} %shard_map.66.refs_0_), channel_id=1, source_target_pairs={{0,8},{4,12},{8,0},{12,4},{16,24},{20,28},{24,16},{28,20},{1,9},{5... | collective-permute-start | bytes 270344 | tf_op jit(solution)/shard_map/ppermute | solution.py:15
  140.3 6.1 %collective-permute-start.30 = (s16[11,32,128]{2,1,0:T(8,128)(2,1)S(1)}, s16[11,32,128]{2,1,0:T(8,128)(2,1)S(1)}, u32[]{:S(2)}, u32[]{:S(2)}) collective-permute-start(s16[11,32,128]{2,1,0:T(8,128)(2,1)S(1)} %get-tuple-element.108), channel_id=1, source_target_pairs={{0,3},{1,2},{2,1},{3,0},{4,7},{5,6},{6,5},{7,4},{8,11},{9,10},{10,... | collective-permute-start | bytes 270344 | tf_op jit(solution)/shard_map/ppermute | solution.py:15
  141.7 5.9 %collective-permute-start.29 = (s16[11,32,128]{2,1,0:T(8,128)(2,1)S(1)}, s16[11,32,128]{2,1,0:T(8,128)(2,1)S(1)}, u32[]{:S(2)}, u32[]{:S(2)}) collective-permute-start(s16[11,32,128]{2,1,0:T(8,128)(2,1)S(1)} %get-tuple-element.109), channel_id=1, source_target_pairs={{0,2},{1,3},{2,0},{3,1},{4,6},{5,7},{6,4},{7,5},{8,10},{9,11},{10,... | collective-permute-start | bytes 270344 | tf_op jit(solution)/shard_map/ppermute | solution.py:15
  142.5 5.1 %collective-permute-start.28 = (s16[11,32,128]{2,1,0:T(8,128)(2,1)S(1)}, s16[11,32,128]{2,1,0:T(8,128)(2,1)S(1)}, u32[]{:S(2)}, u32[]{:S(2)}) collective-permute-start(s16[11,32,128]{2,1,0:T(8,128)(2,1)S(1)} %get-tuple-element.110), channel_id=1, source_target_pairs={{0,1},{1,0},{2,3},{3,2},{4,5},{5,4},{6,7},{7,6},{8,9},{9,8},{10,11... | collective-permute-start | bytes 270344 | tf_op jit(solution)/shard_map/ppermute | solution.py:15
  143.9 4.2 %collective-permute-start.27 = (s16[4,11,32,128]{3,2,1,0:T(8,128)(2,1)S(1)}, s16[4,11,32,128]{3,2,1,0:T(8,128)(2,1)S(1)}, u32[]{:S(2)}, u32[]{:S(2)}) collective-permute-start(s16[4,11,32,128]{3,2,1,0:T(8,128)(2,1)S(1)} %pad_add_fusion.refs_0_), channel_id=1, source_target_pairs={{0,4},{4,0},{8,12},{12,8},{16,20},{20,16},{24,28},{28,24},{1,5},{5... | collective-permute-start | bytes 1081352 | tf_op jit(solution)/shard_map/ppermute | solution.py:15
  147.6 1.7 %collective-permute-start.31 = (s16[4,11,32,128]{3,2,1,0:T(8,128)(2,1)S(1)}, s16[4,11,32,128]{3,2,1,0:T(8,128)(2,1)S(1)}, u32[]{:S(2)}, u32[]{:S(2)}) collective-permute-start(s16[4,11,32,128]{3,2,1,0:T(8,128)(2,1)S(1)} %pad_add_fusion.1.refs_2_), channel_id=1, source_target_pairs={{0,4},{4,0},{8,12},{12,8},{16,20},{20,16},{24,28},{28,24},{1,5},{5... | collective-permute-start | bytes 1081352 | tf_op jit(solution)/shard_map/ppermute | solution.py:15

commit v4 on v3

--- a/solution.py
+++ b/solution.py
@@ -15,28 +15,29 @@
     return lax.ppermute(value, axis, [(i, i ^ step) for i in range(size)])
 
 
-def contract_kernel(spots, left, right, weight, column, *refs):
+def contract_kernel(spots, table, *refs):
     *parts, out, tiles = refs
     parts = parts[: len(spots)]
     count = out.shape[1]
     rows = out.shape[2]
     length, width = tiles.shape[1:]
+    column = table[3 * count]
     for spot, part in zip(spots, parts):
         for inner in range(part.shape[1]):
             tiles[spot + inner] = part[:, inner].reshape(length, width)
 
     def one(index, carry):
         block = lax.dot_general(
-            tiles[left[index]],
-            tiles[right[index]],
+            tiles[table[index]],
+            tiles[table[count + index]],
             (((0,), (0,)), ((), ())),
             preferred_element_type=jnp.float32,
-        ) * weight[index].astype(jnp.float32)
+        ) * table[2 * count + index].astype(jnp.float32)
         for step in range(out.shape[0]):
-            out[column[0] ^ step, index] = block[step * rows : (step + 1) * rows]
+            out[column ^ step, index] = block[step * rows : (step + 1) * rows]
         return carry
 
-    lax.fori_loop(0, count, one, 0, unroll=4)
+    lax.fori_loop(0, count, one, 0, unroll=count if count <= 28 else 4)
 
 
 def contract(parts, table, column, tile_count, aux_size, earlier):
@@ -47,7 +48,7 @@
         functools.partial(contract_kernel, spots),
         out_shape=jax.ShapeDtypeStruct((aux_size, count, width // aux_size, width), jnp.float32),
         grid_spec=pltpu.PrefetchScalarGridSpec(
-            num_scalar_prefetch=4,
+            num_scalar_prefetch=1,
             grid=(),
             in_specs=[pl.BlockSpec(memory_space=pltpu.VMEM)] * len(values)
             + [pl.BlockSpec(memory_space=pl.ANY)] * len(earlier),
@@ -56,7 +57,7 @@
         ),
         cost_estimate=TINY,
         compiler_params=pltpu.CompilerParams(vmem_limit_bytes=VMEM_LIMIT),
-    )(table[0], table[1], table[2], column.reshape(1), *values, *earlier)
+    )(jnp.concatenate([table.reshape(-1), column.reshape(1)]), *values, *earlier)
 
 
 LEVELS = 32766.0
@@ -98,7 +99,7 @@
     return jnp.max(jnp.abs(block), axis=0, keepdims=True)
 
 
-def loop(count, step, unroll=4):
+def loop(count, step, unroll=8):
     lax.fori_loop(0, count, lambda index, carry: (step(index), carry)[1], 0, unroll=unroll)
 
 
@@ -151,7 +152,10 @@
     )(kept, across)
 
 
-def combine_kernel(counts, arrivals, keep_own, targets, *refs):
+def combine_kernel(counts, arrivals, keep_own, placed, *refs):
+    targets = None
+    if placed:
+        targets, *refs = refs
     flat, refs = refs[: len(counts) * (arrivals + 1)], refs[len(counts) * (arrivals + 1) :]
     outs, (total, tops, *scales) = refs[: -2 - arrivals], refs[-2 - arrivals :]
     share = outs[-1].shape[0] - extra_blocks_of(outs[-1])
@@ -165,7 +169,7 @@
             block = own[index]
             for other, scale in zip(others, scales):
                 block = block + unpack_block(other[index], scale[pl.ds(index, 1), :])
-            total[targets[base + index]] = block
+            total[base + index if targets is None else targets[base + index]] = block
 
         loop(count, add)
         base += count
@@ -209,10 +213,10 @@
         outs = [jax.ShapeDtypeStruct((share, rows, width), jnp.float32)] + outs
     arrivals = len(groups[0]) - 1
     return pl.pallas_call(
-        functools.partial(combine_kernel, counts, arrivals, keep_own),
+        functools.partial(combine_kernel, counts, arrivals, keep_own, targets is not None),
         out_shape=outs,
         grid_spec=pltpu.PrefetchScalarGridSpec(
-            num_scalar_prefetch=1,
+            num_scalar_prefetch=int(targets is not None),
             grid=(),
             in_specs=[VMEM_SPEC] * len(flat),
             out_specs=[VMEM_SPEC] * len(outs),
@@ -224,7 +228,7 @@
         ),
         cost_estimate=TINY,
         compiler_params=PARAMS,
-    )(targets, *flat)
+    )(*([] if targets is None else [targets]), *flat)
 
 
 def turn_kernel(column, *refs):
@@ -284,13 +288,14 @@
     )(column.reshape(1), *parts)
 
 
-def place_kernel(share, columns, kinds, sources, slots, *refs):
+def place_kernel(share, table, *refs):
     *inputs, matrix, tiles, direct_scales, mirror_scales = refs
     directs, mirrors = inputs[: len(inputs) // 2], inputs[len(inputs) // 2 :]
     here, rows, _ = matrix.shape
-    tile_count = kinds.shape[0] // here
-    width = matrix.shape[2] // tile_count
+    width = directs[0].shape[-1]
+    tile_count = matrix.shape[2] // width
     pack = width // rows
+    spots = here * tile_count
     chips = directs[0].shape[0]
     half = chips * share
     groups = half // pack
@@ -320,8 +325,8 @@
 
         def one(other, tile=tile):
             spot = tile * tile_count + other
-            kind = kinds[spot]
-            source = sources[spot]
+            kind = table[pack + spot]
+            source = table[pack + spots + spot]
             target = pl.ds(pl.multiple_of(other * width, width), width)
 
             def write(block):
@@ -344,7 +349,7 @@
                     spot_in = inside - group * pack
                     total = jnp.zeros((rows, width), jnp.float32)
                     for step in range(pack):
-                        column = columns[step]
+                        column = table[step]
                         block = unpack_block(
                             mirrors[side][step, group],
                             mirror_scales[side, step, pl.ds(group, 1), :],
@@ -356,7 +361,7 @@
         loop(tile_count, one, unroll=1)
 
     def fill(slot):
-        source = slots[slot]
+        source = table[pack + 2 * spots + slot]
 
         def write(block):
             tiles[0, slot] = block
@@ -383,7 +388,7 @@
             jax.ShapeDtypeStruct((1, slots.shape[0], rows, width), jnp.float32),
         ),
         grid_spec=pltpu.PrefetchScalarGridSpec(
-            num_scalar_prefetch=4,
+            num_scalar_prefetch=1,
             grid=(),
             in_specs=[VMEM_SPEC] * 4,
             out_specs=[VMEM_SPEC] * 2,
@@ -394,7 +399,7 @@
         ),
         cost_estimate=TINY,
         compiler_params=PARAMS,
-    )(columns, kinds, sources, slots, *directs, *mirrors)
+    )(jnp.concatenate([columns, kinds, sources, slots]), *directs, *mirrors)
 
 
 def take(value, index):
@@ -498,7 +503,7 @@
     far += [(step, inner, inner + 1) for inner in range(here) for step in last]
     sent, order = {}, []
     for spot, (step, low, high) in enumerate(far):
-        gate = order[spot - 2 : spot - 2 + 1] if spot >= 2 else ([first] if spot else [])
+        gate = [order[spot - 2]] if spot >= 2 else ([first] if spot else [])
         block = piece(step, low, high, *gate)
         sent[step, low] = swap(block, "pair", pair_size, step)
         order.append(sent[step, low])
@@ -524,19 +529,17 @@
     for keys, low, high in zip(parts, bounds[:-1], bounds[1:]):
         group, kept = chip_blocks(keys, low, high, *earlier)
         groups.append(group)
-        earlier = (kept,)
-    shares = combine(mine[3], groups, share, True)
-
+        earlier = (group[0],)
     shares = lax.cond(
         enough,
-        lambda: list(shares),
+        lambda: list(combine(mine[3], groups, share, True)),
         lambda: list(combine(mine[3], [chip_blocks(list(sent), 0, half)[0]], share, True)),
     )
 
     line = [shares[0]] + [
         swap(shares[step], "pair", pair_size, 2 * step) for step in range(1, chips)
     ]
-    total = combine(jnp.arange(share, dtype=jnp.int32), [line], share, False)[0]
+    total = combine(None, [line], share, False)[0]
     line = [total] + [swap(total, "pair", pair_size, 2 * step) for step in range(1, chips)]
     own_direct = jnp.stack(line)
     other_direct = swap(own_direct, "pair", pair_size, 1)

time: 155 us -> 140 us (0.903)
  Pallas kernels: 32.7 us -> 23 us
  starting transfers between devices: 51 us -> 42.9 us
  waiting for transfers between devices: 52.4 us -> 57 us
  local copies, waits for them, and re-layouts: 12.9 us -> 11.2 us
    ppermute x28, starting transfers between devices: 51 us -> 42.9 us  [swap(): return lax.ppermute(value, axis, [(i, i ^ step) for i in range(size)])]
    ppermute x28, waiting for transfers between devices: 52.4 us -> 57 us  [swap(): return lax.ppermute(value, axis, [(i, i ^ step) for i in range(size)])]
    pallas_call x4, Pallas kernels: 17.5 us -> 13.4 us  [contract(): pl.pallas_call(functools.partial(contract_kernel, spots), out_shape=jax.S...]
    pallas_call x2, Pallas kernels: 5.31 us -> 1.96 us  [split_columns(): pl.pallas_call(split_kernel, out_shape=[jax.ShapeDtypeStruct((count, rows...]
    cond x3 -> x0, local copies, waits for them, and re-layouts: 2.67 us -> none
    pallas_call x2, Pallas kernels: 4.57 us -> 2.43 us  [combine(): pl.pallas_call(functools.partial(combine_kernel, counts, arrivals, keep_o...]
  transfers between devices with their start and end apart: 28 -> 28, of which waited for: 14 -> 16; matrix products, arithmetic and copies ran while one was open for 7% -> 9% of each run, Pallas kernels for 15% -> 6%
where the time goes in v4:
time: 140 us; the launch traced here: 139 us
  waiting for transfers between devices  57 us (41%)
  starting transfers between devices  42.9 us (31%)
  Pallas kernels  23 us (16%)
  local copies, waits for them, and re-layouts  11.2 us (8%)
  other arithmetic  3.43 us (2%)
  between operations  1.63 us (1%)
    ppermute x28, waiting for transfers between devices, swap(): return lax.ppermute(value, axis, [(i, i ^ step) for i in range(size)])  57 us
    ppermute x28, starting transfers between devices, swap(): return lax.ppermute(value, axis, [(i, i ^ step) for i in range(size)])  42.9 us
    pallas_call x4, Pallas kernels, contract(): pl.pallas_call(functools.partial(contract_kernel, spots), out_shape=jax.S...  13.4 us
    dynamic_slice x6, local copies, waits for them, and re-layouts, piece(): lax.dynamic_slice(source, start, (depth, high - low, orbitals, width))  8.88 us
    pallas_call x1, Pallas kernels, place(): pl.pallas_call(functools.partial(place_kernel, share), out_shape=(jax.Sha...  4.32 us
  transfers between devices with their start and end apart: 28, of which 16 were waited for; matrix products, arithmetic and copies ran while one was open for 9% of the time, Pallas kernels for 6%

profile of v4, /device:TPU:0, one launch (start us, length us, event | category | flops | bytes accessed | tf_op | source)
XLA Modules:
  0.0 139.2 jit_solution(5857816486622426483)
XLA Ops:
  0.7 1.0 constant_dynamic-slice_fusion.9
  1.7 3.5 %collective-permute-start.4 = (bf16[12,2,64,128]{3,2,1,0:T(8,128)(2,1)S(1)}, bf16[12,2,64,128]{3,2,1,0:T(8,128)(2,1)S(1)}, u32[]{:S(2)}, u32[]{:S(2)}) collective-permute-start(bf16[12,2,64,128]{3,2,1,0:T(8,128)(2,1)S(1)} %constant_dynamic-slice_fusion.9), channel_id=1, source_target_pairs={{0,20},{4,16},{8,28},{12,24},{16,4},{20,0},{24,12},{28,8},{1,21},{... | collective-permute-start | bytes 1179656 | tf_op jit(solution)/shard_map/ppermute | solution.py:15
  5.2 2.4 %constant_dynamic-slice_fusion = (bf16[12,2,64,128]{3,2,1,0:T(8,128)(2,1)S(1)}, bf16[12,2,64,128]{3,2,1,0:T(8,128)(2,1)S(1)}, bf16[12,2,64,128]{3,2,1,0:T(8,128)...) fusion(bf16[96,2,64,128]{3,2,1,0:T(8,128)(2,1)} %param.6, s32[]{:T(128)S(6)} %select_n.174, ...), kind=kLoop, calls=%fused_computation.33 | loop fusion | bytes 3932180 | tf_op jit(solution)/shard_map/dynamic_slice | solution.py:499
  8.3 1.6 %collective-permute-start.11 = (bf16[12,2,64,128]{3,2,1,0:T(8,128)(2,1)S(1)}, bf16[12,2,64,128]{3,2,1,0:T(8,128)(2,1)}, u32[]{:S(2)}, u32[]{:S(2)}) collective-permute-start(bf16[12,2,64,128]{3,2,1,0:T(8,128)(2,1)S(1)} %get-tuple-element.116), channel_id=1, source_target_pairs={{0,8},{4,12},{8,0},{12,4},{16,24},{20,28},{24,16},{28,20},{1,9},{5... | collective-permute-start | bytes 1179656 | tf_op jit(solution)/shard_map/ppermute | solution.py:15
  12.6 10.1 %collective-permute-done.4.refs_0_ = bf16[12,2,64,128]{3,2,1,0:T(8,128)(2,1)S(1)} collective-permute-done((bf16[12,2,64,128]{3,2,1,0:T(8,128)(2,1)S(1)}, bf16[12,2,64,128]{3,2,1,0:T(8,128)(2,1)S(1)}, u32[]{:S(2)}, u32[]{:S(2)}) %collective-permute-start.4) | collective-permute-done | bytes 393248 | tf_op jit(solution)/shard_map/ppermute | solution.py:15
  22.6 1.1 constant_dynamic-slice_fusion.7
  23.7 5.0 %collective-permute-start.6 = (bf16[12,1,64,128]{3,2,1,0:T(8,128)(2,1)S(1)}, bf16[12,1,64,128]{3,2,1,0:T(8,128)(2,1)S(1)}, u32[]{:S(2)}, u32[]{:S(2)}) collective-permute-start(bf16[12,1,64,128]{3,2,1,0:T(8,128)(2,1)S(1)} %constant_dynamic-slice_fusion.7), channel_id=1, source_target_pairs={{0,24},{4,28},{8,16},{12,20},{16,8},{20,12},{24,0},{28,4},{1,25},{... | collective-permute-start | bytes 589832 | tf_op jit(solution)/shard_map/ppermute | solution.py:15
  28.7 11.5 %collective-permute-done.5.refs_1_ = bf16[12,2,64,128]{3,2,1,0:T(8,128)(2,1)S(1)} collective-permute-done((bf16[12,2,64,128]{3,2,1,0:T(8,128)(2,1)}, bf16[12,2,64,128]{3,2,1,0:T(8,128)(2,1)S(1)}, u32[]{:S(2)}, u32[]{:S(2)}) %collective-permute-start.5) | collective-permute-done | bytes 393248 | tf_op jit(solution)/shard_map/ppermute | solution.py:15
  40.2 1.1 constant_dynamic-slice_fusion.6
  41.3 0.9 collective-permute-start.7
  42.4 3.9 %collective-permute-done.6.refs_2_ = bf16[12,1,64,128]{3,2,1,0:T(8,128)(2,1)S(1)} collective-permute-done((bf16[12,1,64,128]{3,2,1,0:T(8,128)(2,1)S(1)}, bf16[12,1,64,128]{3,2,1,0:T(8,128)(2,1)S(1)}, u32[]{:S(2)}, u32[]{:S(2)}) %collective-permute-start.6) | collective-permute-done | bytes 196640 | tf_op jit(solution)/shard_map/ppermute | solution.py:15
  46.3 3.9 %collective-permute-done.7.refs_3_ = bf16[12,1,64,128]{3,2,1,0:T(8,128)(2,1)S(1)} collective-permute-done((bf16[12,1,64,128]{3,2,1,0:T(8,128)(2,1)S(1)}, bf16[12,1,64,128]{3,2,1,0:T(8,128)(2,1)S(1)}, u32[]{:S(2)}, u32[]{:S(2)}) %collective-permute-start.7) | collective-permute-done | bytes 196640 | tf_op jit(solution)/shard_map/ppermute | solution.py:15
  50.9 3.3 %shard_map.59.refs_8_ = f32[4,22,32,128]{3,2,1,0:T(8,128)S(1)} custom-call(s32[67]{0:T(128)S(1)} %pad_add_fusion.7.table, bf16[12,2,64,128]{3,2,1,0:T(8,128)(2,1)S(1)} %collective-permute-done.4.refs_0_, bf16[12,2,64,128]{3,2,1,0:T(8,128)(2,1)S(1)} %collective-permute-done.5.refs_1_, bf16[12,1,64,128]{3,2,1,0:T(8,128)(2,1)S(1)} %collective-permute-done.6.refs_2_, ...), custom_call_target="tpu_custom_call" | custom-call | flops 1 | bytes 1 | tf_op jit(solution)/shard_map/pallas_call | solution.py:47
  54.2 1.2 collective-permute-start.13
  56.0 1.6 %constant_dynamic-slice_fusion.5 = bf16[12,1,64,128]{3,2,1,0:T(8,128)(2,1)} fusion(bf16[96,2,64,128]{3,2,1,0:T(8,128)(2,1)} %param.6, s32[]{:T(128)S(6)} %select_n.169), kind=kLoop, calls=%fused_computation.38 | loop fusion | bytes 393220 | tf_op jit(solution)/shard_map/dynamic_slice | solution.py:499
  57.6 3.1 %collective-permute-start.8 = (bf16[12,1,64,128]{3,2,1,0:T(8,128)(2,1)}, bf16[12,1,64,128]{3,2,1,0:T(8,128)(2,1)}, u32[]{:S(2)}, u32[]{:S(2)}) collective-permute-start(bf16[12,1,64,128]{3,2,1,0:T(8,128)(2,1)} %constant_dynamic-slice_fusion.5), channel_id=1, source_target_pairs={{0,24},{4,28},{8,16},{12,20},{16,8},{20,12},{24,0},{28,4},{1,25},{... | collective-permute-start | bytes 589832 | tf_op jit(solution)/shard_map/ppermute | solution.py:15
  60.7 1.6 %constant_dynamic-slice_fusion.4 = bf16[12,1,64,128]{3,2,1,0:T(8,128)(2,1)} fusion(bf16[96,2,64,128]{3,2,1,0:T(8,128)(2,1)} %param.6, s32[]{:T(128)S(6)} %select_n.170), kind=kLoop, calls=%fused_computation.37 | loop fusion | bytes 393220 | tf_op jit(solution)/shard_map/dynamic_slice | solution.py:499
  63.2 3.6 %shard_map.60.kept = f32[4,22,32,128]{3,2,1,0:T(8,128)S(1)} custom-call(s32[67]{0:T(128)S(1)} %pad_add_fusion.6.table, bf16[12,2,64,128]{3,2,1,0:T(8,128)(2,1)} %copy-done, bf16[12,2,64,128]{3,2,1,0:T(8,128)(2,1)} %copy-done.3, bf16[12,1,64,128]{3,2,1,0:T(8,128)(2,1)S(1)} %collective-permute-done.6.refs_2_, bf16[12,1,64,128]{3,2,1,0:T(8,128)(2,1)} %copy-done.6, ...), custom_call_target="tpu_custom_call" | custom-call | flops 1 | bytes 1 | tf_op jit(solution)/shard_map/pallas_call | solution.py:47
  67.6 4.0 %collective-permute-done.9.refs_5_ = bf16[12,1,64,128]{3,2,1,0:T(8,128)(2,1)} collective-permute-done((bf16[12,1,64,128]{3,2,1,0:T(8,128)(2,1)}, bf16[12,1,64,128]{3,2,1,0:T(8,128)(2,1)}, u32[]{:S(2)}, u32[]{:S(2)}) %collective-permute-start.9) | collective-permute-done | bytes 196640 | tf_op jit(solution)/shard_map/ppermute | solution.py:15
  71.7 3.3 %shard_map.62.refs_10_ = f32[4,18,32,128]{3,2,1,0:T(8,128)S(1)} custom-call(s32[55]{0:T(128)S(1)} %pad_add_fusion.9.table, bf16[12,2,64,128]{3,2,1,0:T(8,128)(2,1)S(1)} %copy-done.1, bf16[12,2,64,128]{3,2,1,0:T(8,128)(2,1)S(1)} %copy-done.4, bf16[12,1,64,128]{3,2,1,0:T(8,128)(2,1)S(1)} %collective-permute-done.6.refs_2_, ...), custom_call_target="tpu_custom_call" | custom-call | flops 1 | bytes 1 | tf_op jit(solution)/shard_map/pallas_call | solution.py:47
  75.4 1.6 %collective-permute-start.14 = (s16[23,32,128]{2,1,0:T(8,128)(2,1)S(1)}, s16[23,32,128]{2,1,0:T(8,128)(2,1)S(1)}, u32[]{:S(2)}, u32[]{:S(2)}) collective-permute-start(s16[23,32,128]{2,1,0:T(8,128)(2,1)S(1)} %get-tuple-element.95), channel_id=1, source_target_pairs={{0,1},{1,0},{2,3},{3,2},{4,5},{5,4},{6,7},{7,6},{8,9},{9,8},{10,11... | collective-permute-start | bytes 565256 | tf_op jit(solution)/shard_map/ppermute | solution.py:15
  77.0 1.5 %collective-permute-start.15 = (s16[23,32,128]{2,1,0:T(8,128)(2,1)S(1)}, s16[23,32,128]{2,1,0:T(8,128)(2,1)S(1)}, u32[]{:S(2)}, u32[]{:S(2)}) collective-permute-start(s16[23,32,128]{2,1,0:T(8,128)(2,1)S(1)} %get-tuple-element.96), channel_id=1, source_target_pairs={{0,2},{1,3},{2,0},{3,1},{4,6},{5,7},{6,4},{7,5},{8,10},{9,11},{10,... | collective-permute-start | bytes 565256 | tf_op jit(solution)/shard_map/ppermute | solution.py:15
  79.0 3.3 %shard_map.63.kept = f32[4,18,32,128]{3,2,1,0:T(8,128)S(1)} custom-call(s32[55]{0:T(128)S(1)} %pad_add_fusion.8.table, bf16[12,2,64,128]{3,2,1,0:T(8,128)(2,1)S(1)} %copy-done.1, bf16[12,2,64,128]{3,2,1,0:T(8,128)(2,1)S(1)} %copy-done.4, bf16[12,1,64,128]{3,2,1,0:T(8,128)(2,1)} %copy-done.5, bf16[12,1,64,128]{3,2,1,0:T(8,128)(2,1)S(1)} %copy-done.7, ...), custom_call_target="tpu_custom_call" | custom-call | flops 1 | bytes 1 | tf_op jit(solution)/shard_map/pallas_call | solution.py:47
  82.3 1.2 shard_map.64
  83.6 1.5 %collective-permute-start.18 = (s16[19,32,128]{2,1,0:T(8,128)(2,1)S(1)}, s16[19,32,128]{2,1,0:T(8,128)(2,1)S(1)}, u32[]{:S(2)}, u32[]{:S(2)}) collective-permute-start(s16[19,32,128]{2,1,0:T(8,128)(2,1)S(1)} %get-tuple-element.99), channel_id=1, source_target_pairs={{0,1},{1,0},{2,3},{3,2},{4,5},{5,4},{6,7},{7,6},{8,9},{9,8},{10,11... | collective-permute-start | bytes 466952 | tf_op jit(solution)/shard_map/ppermute | solution.py:15
  85.1 1.5 %collective-permute-start.19 = (s16[19,32,128]{2,1,0:T(8,128)(2,1)S(1)}, s16[19,32,128]{2,1,0:T(8,128)(2,1)S(1)}, u32[]{:S(2)}, u32[]{:S(2)}) collective-permute-start(s16[19,32,128]{2,1,0:T(8,128)(2,1)S(1)} %get-tuple-element.100), channel_id=1, source_target_pairs={{0,2},{1,3},{2,0},{3,1},{4,6},{5,7},{6,4},{7,5},{8,10},{9,11},{10,... | collective-permute-start | bytes 466952 | tf_op jit(solution)/shard_map/ppermute | solution.py:15
  88.1 2.5 %collective-permute-done.18 = s16[19,32,128]{2,1,0:T(8,128)(2,1)S(1)} collective-permute-done((s16[19,32,128]{2,1,0:T(8,128)(2,1)S(1)}, s16[19,32,128]{2,1,0:T(8,128)(2,1)S(1)}, u32[]{:S(2)}, u32[]{:S(2)}) %collective-permute-start.18) | collective-permute-done | bytes 155680 | tf_op jit(solution)/shard_map/ppermute | solution.py:15
  90.5 4.0 %collective-permute-done.19 = s16[19,32,128]{2,1,0:T(8,128)(2,1)S(1)} collective-permute-done((s16[19,32,128]{2,1,0:T(8,128)(2,1)S(1)}, s16[19,32,128]{2,1,0:T(8,128)(2,1)S(1)}, u32[]{:S(2)}, u32[]{:S(2)}) %collective-permute-start.19) | collective-permute-done | bytes 155680 | tf_op jit(solution)/shard_map/ppermute | solution.py:15
  94.6 2.3 %conditional.1 = ((f32[10,32,128]{2,1,0:T(8,128)S(1)}, s16[11,32,128]{2,1,0:T(8,128)(2,1)S(1)}, s16[11,32,128]{2,1,0:T(8,128)(2,1)S(1)}, s16[11,32,128]{2,1,0:T(8,128)(2,1)S(1)})) conditional(s32[]{:T(128)} %convert_element_type.55, (s32[4,40]{1,0:T(4,128)S(1)}, s32[]{:T(128)}, s32[4,40]{1,0:T(4,128)S(1)}, bf16[12,2,64,128]{3,2,1,0:T(8,128)(2,1)S(1)}, ...), branch_computations={%region_13.14_spmd, %region_14.15_spmd} | conditional | flops 246 | bytes 14618876 | solution.py:533
  94.6 2.3 %branch_1_fun.1 = (f32[10,32,128]{2,1,0:T(8,128)S(1)}, s16[11,32,128]{2,1,0:T(8,128)(2,1)S(1)}, s16[11,32,128]{2,1,0:T(8,128)(2,1)S(1)}, s16[11,32,128]{2,1,0:T(8,128)(2,1)S(1)}) custom-call(s32[40]{0:T(128)S(1)} %slice_bitcast_fusion.1.refs_0_, f32[22,32,128]{2,1,0:T(8,128)} %get-tuple-element.62.refs_1_, ...), custom_call_target="tpu_custom_call" | custom-call | flops 1 | bytes 1 | tf_op jit(solution)/shard_map/cond/branch_1_fun/pallas_call | solution.py:215
  96.8 8.9 %collective-permute-start.21 = (s16[11,32,128]{2,1,0:T(8,128)(2,1)S(1)}, s16[11,32,128]{2,1,0:T(8,128)(2,1)S(1)}, u32[]{:S(2)}, u32[]{:S(2)}) collective-permute-start(s16[11,32,128]{2,1,0:T(8,128)(2,1)S(1)} %get-tuple-element.103), channel_id=1, source_target_pairs={{0,8},{4,12},{8,0},{12,4},{16,24},{20,28},{24,16},{28,20},{1,9},{5... | collective-permute-start | bytes 270344 | tf_op jit(solution)/shard_map/ppermute | solution.py:15
  105.8 0.9 collective-permute-start.22
  106.6 1.6 %collective-permute-start.23 = (s16[11,32,128]{2,1,0:T(8,128)(2,1)S(1)}, s16[11,32,128]{2,1,0:T(8,128)(2,1)S(1)}, u32[]{:S(2)}, u32[]{:S(2)}) collective-permute-start(s16[11,32,128]{2,1,0:T(8,128)(2,1)S(1)} %get-tuple-element.105), channel_id=1, source_target_pairs={{0,24},{4,28},{8,16},{12,20},{16,8},{20,12},{24,0},{28,4},{1,25},{... | collective-permute-start | bytes 270344 | tf_op jit(solution)/shard_map/ppermute | solution.py:15
  108.8 6.2 %collective-permute-done.22.refs_2_ = s16[11,32,128]{2,1,0:T(8,128)(2,1)S(1)} collective-permute-done((s16[11,32,128]{2,1,0:T(8,128)(2,1)S(1)}, s16[11,32,128]{2,1,0:T(8,128)(2,1)S(1)}, u32[]{:S(2)}, u32[]{:S(2)}) %collective-permute-start.22) | collective-permute-done | bytes 90144 | tf_op jit(solution)/shard_map/ppermute | solution.py:15
  115.2 2.1 %collective-permute-start.26 = (s16[11,32,128]{2,1,0:T(8,128)(2,1)S(1)}, s16[11,32,128]{2,1,0:T(8,128)(2,1)S(1)}, u32[]{:S(2)}, u32[]{:S(2)}) collective-permute-start(s16[11,32,128]{2,1,0:T(8,128)(2,1)S(1)} %shard_map.65.refs_0_), channel_id=1, source_target_pairs={{0,24},{4,28},{8,16},{12,20},{16,8},{20,12},{24,0},{28,4},{1,25},{... | collective-permute-start | bytes 270344 | tf_op jit(solution)/shard_map/ppermute | solution.py:15
  117.3 1.1 collective-permute-start.25
  118.4 1.3 collective-permute-start.24
  119.8 2.8 %collective-permute-done.26.refs_3_ = s16[11,32,128]{2,1,0:T(8,128)(2,1)S(1)} collective-permute-done((s16[11,32,128]{2,1,0:T(8,128)(2,1)S(1)}, s16[11,32,128]{2,1,0:T(8,128)(2,1)S(1)}, u32[]{:S(2)}, u32[]{:S(2)}) %collective-permute-start.26) | collective-permute-done | bytes 90144 | tf_op jit(solution)/shard_map/ppermute | solution.py:15
  122.5 2.4 %collective-permute-done.25.refs_2_ = s16[11,32,128]{2,1,0:T(8,128)(2,1)S(1)} collective-permute-done((s16[11,32,128]{2,1,0:T(8,128)(2,1)S(1)}, s16[11,32,128]{2,1,0:T(8,128)(2,1)S(1)}, u32[]{:S(2)}, u32[]{:S(2)}) %collective-permute-start.25) | collective-permute-done | bytes 90144 | tf_op jit(solution)/shard_map/ppermute | solution.py:15
  125.0 0.9 shard_map.66
  125.9 1.4 collective-permute-start.30
  127.2 1.4 collective-permute-start.29
  128.6 0.8 collective-permute-start.28
  129.6 1.9 %collective-permute-done.30 = s16[11,32,128]{2,1,0:T(8,128)(2,1)S(1)} collective-permute-done((s16[11,32,128]{2,1,0:T(8,128)(2,1)S(1)}, s16[11,32,128]{2,1,0:T(8,128)(2,1)S(1)}, u32[]{:S(2)}, u32[]{:S(2)}) %collective-permute-start.30) | collective-permute-done | bytes 90144 | tf_op jit(solution)/shard_map/ppermute | solution.py:15
  131.4 0.9 collective-permute-done.29
  132.4 0.8 collective-permute-done.28
  133.5 1.4 %collective-permute-done.31.refs_3_ = s16[4,11,32,128]{3,2,1,0:T(8,128)(2,1)S(1)} collective-permute-done((s16[4,11,32,128]{3,2,1,0:T(8,128)(2,1)S(1)}, s16[4,11,32,128]{3,2,1,0:T(8,128)(2,1)S(1)}, u32[]{:S(2)}, u32[]{:S(2)}) %collective-permute-start.31) | collective-permute-done | bytes 360480 | tf_op jit(solution)/shard_map/ppermute | solution.py:15
  134.9 4.3 %shard_map.67 = (f32[2,32,2048]{2,1,0:T(8,128)}, f32[1,40,32,128]{3,2,1,0:T(8,128)}) custom-call(s32[108]{0:T(128)S(1)} %pad_add_fusion.5.table, s16[4,11,32,128]{3,2,1,0:T(8,128)(2,1)S(1)} %pad_add_fusion.2.refs_0_, s16[4,11,32,128]{3,2,1,0:T(8,128)(2,1)S(1)} %collective-permute-done.27.refs_1_, s16[4,11,32,128]{3,2,1,0:T(8,128)(2,1)S(1)} %pad_add_fusion.3.refs_2_, ...), custom_call_target="tpu_custom_call" | custom-call | flops 1 | bytes 1 | tf_op jit(solution)/shard_map/pallas_call | solution.py:384
  (105 shorter events, 9.6 us)
Async XLA Ops:
  0.6 9.6 %copy-start.9 = (s32[80,2]{0,1:T(2,128)S(1)}, s32[80,2]{0,1:T(2,128)}, u32[]{:S(2)}) copy-start(s32[80,2]{0,1:T(2,128)} %param.7) | copy-start | bytes 1924
  0.6 10.8 %copy-start.10 = (s32[80,1]{0,1:T(1,128)S(1)}, s32[80,1]{0,1:T(1,128)}, u32[]{:S(2)}) copy-start(s32[80,1]{0,1:T(1,128)} %param.8) | copy-start | bytes 964
  1.7 20.9 %collective-permute-start.4 = (bf16[12,2,64,128]{3,2,1,0:T(8,128)(2,1)S(1)}, bf16[12,2,64,128]{3,2,1,0:T(8,128)(2,1)S(1)}, u32[]{:S(2)}, u32[]{:S(2)}) collective-permute-start(bf16[12,2,64,128]{3,2,1,0:T(8,128)(2,1)S(1)} %constant_dynamic-slice_fusion.9), channel_id=1, source_target_pairs={{0,20},{4,16},{8,28},{12,24},{16,4},{20,0},{24,12},{28,8},{1,21},{... | collective-permute-start | bytes 1179656 | tf_op jit(solution)/shard_map/ppermute | solution.py:15
  7.7 34.7 %collective-permute-start.12 = (bf16[12,2,64,128]{3,2,1,0:T(8,128)(2,1)S(1)}, bf16[12,2,64,128]{3,2,1,0:T(8,128)(2,1)}, u32[]{:S(2)}, u32[]{:S(2)}) collective-permute-start(bf16[12,2,64,128]{3,2,1,0:T(8,128)(2,1)S(1)} %get-tuple-element.115), channel_id=1, source_target_pairs={{0,4},{4,0},{8,12},{12,8},{16,20},{20,16},{24,28},{28,24},{1,5},{5... | collective-permute-start | bytes 1179656 | tf_op jit(solution)/shard_map/ppermute | solution.py:15
  8.3 34.0 %collective-permute-start.11 = (bf16[12,2,64,128]{3,2,1,0:T(8,128)(2,1)S(1)}, bf16[12,2,64,128]{3,2,1,0:T(8,128)(2,1)}, u32[]{:S(2)}, u32[]{:S(2)}) collective-permute-start(bf16[12,2,64,128]{3,2,1,0:T(8,128)(2,1)S(1)} %get-tuple-element.116), channel_id=1, source_target_pairs={{0,8},{4,12},{8,0},{12,4},{16,24},{20,28},{24,16},{28,20},{1,9},{5... | collective-permute-start | bytes 1179656 | tf_op jit(solution)/shard_map/ppermute | solution.py:15
  9.9 32.4 %collective-permute-start.10 = (bf16[12,2,64,128]{3,2,1,0:T(8,128)(2,1)S(1)}, bf16[12,2,64,128]{3,2,1,0:T(8,128)(2,1)}, u32[]{:S(2)}, u32[]{:S(2)}) collective-permute-start(bf16[12,2,64,128]{3,2,1,0:T(8,128)(2,1)S(1)} %get-tuple-element.117), channel_id=1, source_target_pairs={{0,12},{4,8},{8,4},{12,0},{16,28},{20,24},{24,20},{28,16},{1,13},{... | collective-permute-start | bytes 1179656 | tf_op jit(solution)/shard_map/ppermute | solution.py:15
  9.9 30.3 %collective-permute-start.5 = (bf16[12,2,64,128]{3,2,1,0:T(8,128)(2,1)}, bf16[12,2,64,128]{3,2,1,0:T(8,128)(2,1)S(1)}, u32[]{:S(2)}, u32[]{:S(2)}) collective-permute-start(bf16[12,2,64,128]{3,2,1,0:T(8,128)(2,1)} %get-tuple-element.118), channel_id=1, source_target_pairs={{0,16},{4,20},{8,24},{12,28},{16,0},{20,4},{24,8},{28,12},{1,17},{... | collective-permute-start | bytes 1179656 | tf_op jit(solution)/shard_map/ppermute | solution.py:15
  22.6 27.6 %copy-start = (bf16[12,2,64,128]{3,2,1,0:T(8,128)(2,1)}, bf16[12,2,64,128]{3,2,1,0:T(8,128)(2,1)S(1)}, u32[]{:S(2)}) copy-start(bf16[12,2,64,128]{3,2,1,0:T(8,128)(2,1)S(1)} %collective-permute-done.4.refs_0_) | copy-start | bytes 1179652
  23.7 22.6 %collective-permute-start.6 = (bf16[12,1,64,128]{3,2,1,0:T(8,128)(2,1)S(1)}, bf16[12,1,64,128]{3,2,1,0:T(8,128)(2,1)S(1)}, u32[]{:S(2)}, u32[]{:S(2)}) collective-permute-start(bf16[12,1,64,128]{3,2,1,0:T(8,128)(2,1)S(1)} %constant_dynamic-slice_fusion.7), channel_id=1, source_target_pairs={{0,24},{4,28},{8,16},{12,20},{16,8},{20,12},{24,0},{28,4},{1,25},{... | collective-permute-start | bytes 589832 | tf_op jit(solution)/shard_map/ppermute | solution.py:15
  40.2 10.0 %copy-start.3 = (bf16[12,2,64,128]{3,2,1,0:T(8,128)(2,1)}, bf16[12,2,64,128]{3,2,1,0:T(8,128)(2,1)S(1)}, u32[]{:S(2)}) copy-start(bf16[12,2,64,128]{3,2,1,0:T(8,128)(2,1)S(1)} %collective-permute-done.5.refs_1_) | copy-start | bytes 1179652
  41.3 8.9 %collective-permute-start.7 = (bf16[12,1,64,128]{3,2,1,0:T(8,128)(2,1)S(1)}, bf16[12,1,64,128]{3,2,1,0:T(8,128)(2,1)S(1)}, u32[]{:S(2)}, u32[]{:S(2)}) collective-permute-start(bf16[12,1,64,128]{3,2,1,0:T(8,128)(2,1)S(1)} %constant_dynamic-slice_fusion.6), channel_id=1, source_target_pairs={{0,28},{4,24},{8,20},{12,16},{16,12},{20,8},{24,4},{28,0},{1,29},{... | collective-permute-start | bytes 589832 | tf_op jit(solution)/shard_map/ppermute | solution.py:15
  46.3 25.4 %copy-start.5 = (bf16[12,1,64,128]{3,2,1,0:T(8,128)(2,1)}, bf16[12,1,64,128]{3,2,1,0:T(8,128)(2,1)S(1)}, u32[]{:S(2)}) copy-start(bf16[12,1,64,128]{3,2,1,0:T(8,128)(2,1)S(1)} %collective-permute-done.6.refs_2_) | copy-start | bytes 589828
  50.2 0.7 copy-start.6
  54.2 12.6 %collective-permute-start.13 = (f32[4,22,32,128]{3,2,1,0:T(8,128)S(1)}, f32[4,22,32,128]{3,2,1,0:T(8,128)S(1)}, u32[]{:S(2)}, u32[]{:S(2)}) collective-permute-start(f32[4,22,32,128]{3,2,1,0:T(8,128)S(1)} %shard_map.59.refs_8_), channel_id=1, source_target_pairs={{0,4},{4,0},{8,12},{12,8},{16,20},{20,16},{24,28},{28,24},{1,5},{5... | collective-permute-start | bytes 4325384 | tf_op jit(solution)/shard_map/ppermute | solution.py:15
  57.6 10.0 %collective-permute-start.8 = (bf16[12,1,64,128]{3,2,1,0:T(8,128)(2,1)}, bf16[12,1,64,128]{3,2,1,0:T(8,128)(2,1)}, u32[]{:S(2)}, u32[]{:S(2)}) collective-permute-start(bf16[12,1,64,128]{3,2,1,0:T(8,128)(2,1)} %constant_dynamic-slice_fusion.5), channel_id=1, source_target_pairs={{0,24},{4,28},{8,16},{12,20},{16,8},{20,12},{24,0},{28,4},{1,25},{... | collective-permute-start | bytes 589832 | tf_op jit(solution)/shard_map/ppermute | solution.py:15
  62.3 9.3 %collective-permute-start.9 = (bf16[12,1,64,128]{3,2,1,0:T(8,128)(2,1)}, bf16[12,1,64,128]{3,2,1,0:T(8,128)(2,1)}, u32[]{:S(2)}, u32[]{:S(2)}) collective-permute-start(bf16[12,1,64,128]{3,2,1,0:T(8,128)(2,1)} %constant_dynamic-slice_fusion.4), channel_id=1, source_target_pairs={{0,28},{4,24},{8,20},{12,16},{16,12},{20,8},{24,4},{28,0},{1,29},{... | collective-permute-start | bytes 589832 | tf_op jit(solution)/shard_map/ppermute | solution.py:15
  66.8 4.9 %copy-start.1 = (bf16[12,2,64,128]{3,2,1,0:T(8,128)(2,1)S(1)}, bf16[12,2,64,128]{3,2,1,0:T(8,128)(2,1)}, u32[]{:S(2)}) copy-start(bf16[12,2,64,128]{3,2,1,0:T(8,128)(2,1)} %copy-done) | copy-start | bytes 1179652
  66.8 4.8 %copy-start.4 = (bf16[12,2,64,128]{3,2,1,0:T(8,128)(2,1)S(1)}, bf16[12,2,64,128]{3,2,1,0:T(8,128)(2,1)}, u32[]{:S(2)}) copy-start(bf16[12,2,64,128]{3,2,1,0:T(8,128)(2,1)} %copy-done.3) | copy-start | bytes 1179652
  66.8 4.8 %copy-start.7 = (bf16[12,1,64,128]{3,2,1,0:T(8,128)(2,1)S(1)}, bf16[12,1,64,128]{3,2,1,0:T(8,128)(2,1)}, u32[]{:S(2)}) copy-start(bf16[12,1,64,128]{3,2,1,0:T(8,128)(2,1)} %copy-done.6) | copy-start | bytes 589828
  67.6 14.7 %copy-start.8 = (f32[22,32,128]{2,1,0:T(8,128)}, f32[22,32,128]{2,1,0:T(8,128)S(1)}, u32[]{:S(2)}) copy-start(f32[22,32,128]{2,1,0:T(8,128)S(1)} %get-tuple-element.94.refs_10_) | copy-start | bytes 1081348
  67.6 9.4 %copy-start.11 = (s32[80]{0:T(128)S(1)}, s32[80]{0:T(128)}, u32[]{:S(2)}) copy-start(s32[80]{0:T(128)} %param.9) | copy-start | bytes 964
  74.9 7.4 %collective-permute-start.17 = (f32[4,18,32,128]{3,2,1,0:T(8,128)S(1)}, f32[4,18,32,128]{3,2,1,0:T(8,128)S(1)}, u32[]{:S(2)}, u32[]{:S(2)}) collective-permute-start(f32[4,18,32,128]{3,2,1,0:T(8,128)S(1)} %shard_map.62.refs_10_), channel_id=1, source_target_pairs={{0,4},{4,0},{8,12},{12,8},{16,20},{20,16},{24,28},{28,24},{1,5},{5... | collective-permute-start | bytes 3538952 | tf_op jit(solution)/shard_map/ppermute | solution.py:15
  75.4 11.1 %collective-permute-start.14 = (s16[23,32,128]{2,1,0:T(8,128)(2,1)S(1)}, s16[23,32,128]{2,1,0:T(8,128)(2,1)S(1)}, u32[]{:S(2)}, u32[]{:S(2)}) collective-permute-start(s16[23,32,128]{2,1,0:T(8,128)(2,1)S(1)} %get-tuple-element.95), channel_id=1, source_target_pairs={{0,1},{1,0},{2,3},{3,2},{4,5},{5,4},{6,7},{7,6},{8,9},{9,8},{10,11... | collective-permute-start | bytes 565256 | tf_op jit(solution)/shard_map/ppermute | solution.py:15
  77.0 10.9 %collective-permute-start.15 = (s16[23,32,128]{2,1,0:T(8,128)(2,1)S(1)}, s16[23,32,128]{2,1,0:T(8,128)(2,1)S(1)}, u32[]{:S(2)}, u32[]{:S(2)}) collective-permute-start(s16[23,32,128]{2,1,0:T(8,128)(2,1)S(1)} %get-tuple-element.96), channel_id=1, source_target_pairs={{0,2},{1,3},{2,0},{3,1},{4,6},{5,7},{6,4},{7,5},{8,10},{9,11},{10,... | collective-permute-start | bytes 565256 | tf_op jit(solution)/shard_map/ppermute | solution.py:15
  78.5 16.0 %copy-start.2 = (bf16[12,2,64,128]{3,2,1,0:T(8,128)(2,1)S(1)}, bf16[12,2,64,128]{3,2,1,0:T(8,128)(2,1)}, u32[]{:S(2)}) copy-start(bf16[12,2,64,128]{3,2,1,0:T(8,128)(2,1)} %copy-done) | copy-start | bytes 1179652
  78.5 9.5 %collective-permute-start.16 = (s16[23,32,128]{2,1,0:T(8,128)(2,1)S(1)}, s16[23,32,128]{2,1,0:T(8,128)(2,1)S(1)}, u32[]{:S(2)}, u32[]{:S(2)}) collective-permute-start(s16[23,32,128]{2,1,0:T(8,128)(2,1)S(1)} %get-tuple-element.97), channel_id=1, source_target_pairs={{0,3},{1,2},{2,1},{3,0},{4,7},{5,6},{6,5},{7,4},{8,11},{9,10},{10,... | collective-permute-start | bytes 565256 | tf_op jit(solution)/shard_map/ppermute | solution.py:15
  83.6 7.0 %collective-permute-start.18 = (s16[19,32,128]{2,1,0:T(8,128)(2,1)S(1)}, s16[19,32,128]{2,1,0:T(8,128)(2,1)S(1)}, u32[]{:S(2)}, u32[]{:S(2)}) collective-permute-start(s16[19,32,128]{2,1,0:T(8,128)(2,1)S(1)} %get-tuple-element.99), channel_id=1, source_target_pairs={{0,1},{1,0},{2,3},{3,2},{4,5},{5,4},{6,7},{7,6},{8,9},{9,8},{10,11... | collective-permute-start | bytes 466952 | tf_op jit(solution)/shard_map/ppermute | solution.py:15
  85.1 9.5 %collective-permute-start.19 = (s16[19,32,128]{2,1,0:T(8,128)(2,1)S(1)}, s16[19,32,128]{2,1,0:T(8,128)(2,1)S(1)}, u32[]{:S(2)}, u32[]{:S(2)}) collective-permute-start(s16[19,32,128]{2,1,0:T(8,128)(2,1)S(1)} %get-tuple-element.100), channel_id=1, source_target_pairs={{0,2},{1,3},{2,0},{3,1},{4,6},{5,7},{6,4},{7,5},{8,10},{9,11},{10,... | collective-permute-start | bytes 466952 | tf_op jit(solution)/shard_map/ppermute | solution.py:15
  86.6 8.0 %collective-permute-start.20 = (s16[19,32,128]{2,1,0:T(8,128)(2,1)S(1)}, s16[19,32,128]{2,1,0:T(8,128)(2,1)S(1)}, u32[]{:S(2)}, u32[]{:S(2)}) collective-permute-start(s16[19,32,128]{2,1,0:T(8,128)(2,1)S(1)} %get-tuple-element.101), channel_id=1, source_target_pairs={{0,3},{1,2},{2,1},{3,0},{4,7},{5,6},{6,5},{7,4},{8,11},{9,10},{10,... | collective-permute-start | bytes 466952 | tf_op jit(solution)/shard_map/ppermute | solution.py:15
  96.8 12.0 %collective-permute-start.21 = (s16[11,32,128]{2,1,0:T(8,128)(2,1)S(1)}, s16[11,32,128]{2,1,0:T(8,128)(2,1)S(1)}, u32[]{:S(2)}, u32[]{:S(2)}) collective-permute-start(s16[11,32,128]{2,1,0:T(8,128)(2,1)S(1)} %get-tuple-element.103), channel_id=1, source_target_pairs={{0,8},{4,12},{8,0},{12,4},{16,24},{20,28},{24,16},{28,20},{1,9},{5... | collective-permute-start | bytes 270344 | tf_op jit(solution)/shard_map/ppermute | solution.py:15
  105.8 9.3 %collective-permute-start.22 = (s16[11,32,128]{2,1,0:T(8,128)(2,1)S(1)}, s16[11,32,128]{2,1,0:T(8,128)(2,1)S(1)}, u32[]{:S(2)}, u32[]{:S(2)}) collective-permute-start(s16[11,32,128]{2,1,0:T(8,128)(2,1)S(1)} %get-tuple-element.104), channel_id=1, source_target_pairs={{0,16},{4,20},{8,24},{12,28},{16,0},{20,4},{24,8},{28,12},{1,17},{... | collective-permute-start | bytes 270344 | tf_op jit(solution)/shard_map/ppermute | solution.py:15
  106.6 8.4 %collective-permute-start.23 = (s16[11,32,128]{2,1,0:T(8,128)(2,1)S(1)}, s16[11,32,128]{2,1,0:T(8,128)(2,1)S(1)}, u32[]{:S(2)}, u32[]{:S(2)}) collective-permute-start(s16[11,32,128]{2,1,0:T(8,128)(2,1)S(1)} %get-tuple-element.105), channel_id=1, source_target_pairs={{0,24},{4,28},{8,16},{12,20},{16,8},{20,12},{24,0},{28,4},{1,25},{... | collective-permute-start | bytes 270344 | tf_op jit(solution)/shard_map/ppermute | solution.py:15
  115.2 7.3 %collective-permute-start.26 = (s16[11,32,128]{2,1,0:T(8,128)(2,1)S(1)}, s16[11,32,128]{2,1,0:T(8,128)(2,1)S(1)}, u32[]{:S(2)}, u32[]{:S(2)}) collective-permute-start(s16[11,32,128]{2,1,0:T(8,128)(2,1)S(1)} %shard_map.65.refs_0_), channel_id=1, source_target_pairs={{0,24},{4,28},{8,16},{12,20},{16,8},{20,12},{24,0},{28,4},{1,25},{... | collective-permute-start | bytes 270344 | tf_op jit(solution)/shard_map/ppermute | solution.py:15
  117.3 7.7 %collective-permute-start.25 = (s16[11,32,128]{2,1,0:T(8,128)(2,1)S(1)}, s16[11,32,128]{2,1,0:T(8,128)(2,1)S(1)}, u32[]{:S(2)}, u32[]{:S(2)}) collective-permute-start(s16[11,32,128]{2,1,0:T(8,128)(2,1)S(1)} %shard_map.65.refs_0_), channel_id=1, source_target_pairs={{0,16},{4,20},{8,24},{12,28},{16,0},{20,4},{24,8},{28,12},{1,17},{... | collective-permute-start | bytes 270344 | tf_op jit(solution)/shard_map/ppermute | solution.py:15
  118.4 6.6 %collective-permute-start.24 = (s16[11,32,128]{2,1,0:T(8,128)(2,1)S(1)}, s16[11,32,128]{2,1,0:T(8,128)(2,1)S(1)}, u32[]{:S(2)}, u32[]{:S(2)}) collective-permute-start(s16[11,32,128]{2,1,0:T(8,128)(2,1)S(1)} %shard_map.65.refs_0_), channel_id=1, source_target_pairs={{0,8},{4,12},{8,0},{12,4},{16,24},{20,28},{24,16},{28,20},{1,9},{5... | collective-permute-start | bytes 270344 | tf_op jit(solution)/shard_map/ppermute | solution.py:15
  125.9 5.6 %collective-permute-start.30 = (s16[11,32,128]{2,1,0:T(8,128)(2,1)S(1)}, s16[11,32,128]{2,1,0:T(8,128)(2,1)S(1)}, u32[]{:S(2)}, u32[]{:S(2)}) collective-permute-start(s16[11,32,128]{2,1,0:T(8,128)(2,1)S(1)} %get-tuple-element.120), channel_id=1, source_target_pairs={{0,3},{1,2},{2,1},{3,0},{4,7},{5,6},{6,5},{7,4},{8,11},{9,10},{10,... | collective-permute-start | bytes 270344 | tf_op jit(solution)/shard_map/ppermute | solution.py:15
  127.2 5.1 %collective-permute-start.29 = (s16[11,32,128]{2,1,0:T(8,128)(2,1)S(1)}, s16[11,32,128]{2,1,0:T(8,128)(2,1)S(1)}, u32[]{:S(2)}, u32[]{:S(2)}) collective-permute-start(s16[11,32,128]{2,1,0:T(8,128)(2,1)S(1)} %get-tuple-element.121), channel_id=1, source_target_pairs={{0,2},{1,3},{2,0},{3,1},{4,6},{5,7},{6,4},{7,5},{8,10},{9,11},{10,... | collective-permute-start | bytes 270344 | tf_op jit(solution)/shard_map/ppermute | solution.py:15
  128.6 4.5 %collective-permute-start.28 = (s16[11,32,128]{2,1,0:T(8,128)(2,1)S(1)}, s16[11,32,128]{2,1,0:T(8,128)(2,1)S(1)}, u32[]{:S(2)}, u32[]{:S(2)}) collective-permute-start(s16[11,32,128]{2,1,0:T(8,128)(2,1)S(1)} %get-tuple-element.122), channel_id=1, source_target_pairs={{0,1},{1,0},{2,3},{3,2},{4,5},{5,4},{6,7},{7,6},{8,9},{9,8},{10,11... | collective-permute-start | bytes 270344 | tf_op jit(solution)/shard_map/ppermute | solution.py:15
  129.5 4.0 %collective-permute-start.27 = (s16[4,11,32,128]{3,2,1,0:T(8,128)(2,1)S(1)}, s16[4,11,32,128]{3,2,1,0:T(8,128)(2,1)S(1)}, u32[]{:S(2)}, u32[]{:S(2)}) collective-permute-start(s16[4,11,32,128]{3,2,1,0:T(8,128)(2,1)S(1)} %pad_add_fusion.2.refs_0_), channel_id=1, source_target_pairs={{0,4},{4,0},{8,12},{12,8},{16,20},{20,16},{24,28},{28,24},{1,5},{5... | collective-permute-start | bytes 1081352 | tf_op jit(solution)/shard_map/ppermute | solution.py:15
  133.2 1.7 %collective-permute-start.31 = (s16[4,11,32,128]{3,2,1,0:T(8,128)(2,1)S(1)}, s16[4,11,32,128]{3,2,1,0:T(8,128)(2,1)S(1)}, u32[]{:S(2)}, u32[]{:S(2)}) collective-permute-start(s16[4,11,32,128]{3,2,1,0:T(8,128)(2,1)S(1)} %pad_add_fusion.3.refs_2_), channel_id=1, source_target_pairs={{0,4},{4,0},{8,12},{12,8},{16,20},{20,16},{24,28},{28,24},{1,5},{5... | collective-permute-start | bytes 1081352 | tf_op jit(solution)/shard_map/ppermute | solution.py:15

commit v5 on v4

--- a/solution.py
+++ b/solution.py
@@ -288,118 +288,121 @@
     )(column.reshape(1), *parts)
 
 
-def place_kernel(share, table, *refs):
-    *inputs, matrix, tiles, direct_scales, mirror_scales = refs
-    directs, mirrors = inputs[: len(inputs) // 2], inputs[len(inputs) // 2 :]
+def place_kernel(share, chips, table, *refs):
+    direct, *mirrors, matrix, tiles, direct_scales, mirror_scales = refs
     here, rows, _ = matrix.shape
-    width = directs[0].shape[-1]
+    width = direct.shape[-1]
     tile_count = matrix.shape[2] // width
     pack = width // rows
     spots = here * tile_count
-    chips = directs[0].shape[0]
+    slots = tiles.shape[1]
     half = chips * share
     groups = half // pack
-    lane = lax.broadcasted_iota(jnp.int32, (rows, width), 1) // rows
+    blocks = share + extra_blocks(share, rows)
+    behind = extra_blocks(share, rows) * rows
+    for chip in range(2 * chips):
+        load_scales(
+            direct.at[pl.ds(chip * blocks, blocks)],
+            share,
+            direct_scales.at[pl.ds(chip * behind, behind)],
+        )
+    direct_scales[pl.ds(2 * chips * behind, rows), :] = jnp.zeros((rows, width), jnp.float32)
     for side in range(2):
-        for chip in range(chips):
-            load_scales(directs[side].at[chip], share, direct_scales.at[side, chip])
         for step in range(pack):
             load_scales(mirrors[side].at[step], groups, mirror_scales.at[side, step])
 
-    def direct_of(source, write):
+    def direct_block(spot):
+        scale = direct_scales[pl.ds(table[spots + slots + spot], 1), :]
+        return unpack_block(direct[table[spot]], scale)
+
+    for tile in range(here):
+
+        def one(other, tile=tile):
+            target = pl.ds(pl.multiple_of(other * width, width), width)
+            matrix[tile, :, target] = direct_block(tile * tile_count + other)
+
+        loop(tile_count, one)
+
+    def fill(slot):
+        tiles[0, slot] = direct_block(spots + slot)
+
+    loop(slots, fill)
+
+    lane = lax.broadcasted_iota(jnp.int32, (rows, width), 1) // rows
+    base = 2 * (spots + slots)
+
+    def transposed(item, carry):
+        spot = table[base + 1 + item]
+        source = table[base + 1 + spots + item]
         for side in range(2):
 
             @pl.when(source // half == side)
             def _():
                 inside = source - side * half
-                chip = inside // share
-                index = inside - chip * share
-                write(
-                    unpack_block(
-                        directs[side][chip, index],
-                        direct_scales[side, chip, pl.ds(index, 1), :],
-                    )
-                )
-
-    for tile in range(here):
-
-        def one(other, tile=tile):
-            spot = tile * tile_count + other
-            kind = table[pack + spot]
-            source = table[pack + spots + spot]
-            target = pl.ds(pl.multiple_of(other * width, width), width)
-
-            def write(block):
-                matrix[tile, :, target] = block
-
-            @pl.when(kind == 0)
-            def _():
-                write(jnp.zeros((rows, width), jnp.float32))
-
-            @pl.when(kind == 1)
-            def _():
-                direct_of(source, write)
-
-            for side in range(2):
-
-                @pl.when((kind == 2) & (source // half == side))
-                def _():
-                    inside = source - side * half
-                    group = inside // pack
-                    spot_in = inside - group * pack
-                    total = jnp.zeros((rows, width), jnp.float32)
-                    for step in range(pack):
-                        column = table[step]
-                        block = unpack_block(
-                            mirrors[side][step, group],
-                            mirror_scales[side, step, pl.ds(group, 1), :],
-                        )
-                        moved = pltpu.roll(block, ((column - spot_in + pack) % pack) * rows, 1)
-                        total = jnp.where(lane == column, moved, total)
-                    write(total)
-
-        loop(tile_count, one, unroll=1)
-
-    def fill(slot):
-        source = table[pack + 2 * spots + slot]
-
-        def write(block):
-            tiles[0, slot] = block
-
-        @pl.when(source < 0)
-        def _():
-            write(jnp.zeros((rows, width), jnp.float32))
-
-        @pl.when(source >= 0)
-        def _():
-            direct_of(source, write)
-
-    loop(tiles.shape[1], fill, unroll=1)
-
-
-def place(columns, kinds, sources, slots, directs, mirrors, share, here, tile_count):
-    chips, _, rows, width = directs[0].shape
+                group = inside // pack
+                spot_in = inside - group * pack
+                total = jnp.zeros((rows, width), jnp.float32)
+                for step in range(pack):
+                    column = table[base + 1 + 2 * spots + step]
+                    scale = mirror_scales[side, step, pl.ds(group, 1), :]
+                    block = unpack_block(mirrors[side][step, group], scale)
+                    moved = pltpu.roll(block, ((column - spot_in + pack) % pack) * rows, 1)
+                    total = jnp.where(lane == column, moved, total)
+                tile = spot // tile_count
+                other = spot - tile * tile_count
+                target = pl.ds(pl.multiple_of(other * width, width), width)
+                matrix[tile, :, target] = total
+
+        return carry
+
+    lax.fori_loop(0, table[base], transposed, 0)
+
+
+def place_table(columns, kinds, sources, slots, share, chips, rows):
+    blocks = share + extra_blocks(share, rows)
+    behind = extra_blocks(share, rows) * rows
+    spots = kinds.shape[0]
+    wanted = jnp.concatenate([jnp.where(kinds == 1, sources, -1), slots])
+    there = wanted >= 0
+    chip = wanted // share
+    inside = wanted % share
+    block_at = jnp.where(there, chip * blocks + inside, 0)
+    scale_at = jnp.where(there, chip * behind + inside, 2 * chips * behind)
+    turned = kinds == 2
+    spot_ids = jnp.arange(spots, dtype=jnp.int32)
+    rank = jnp.sum((turned[None, :] & (spot_ids[None, :] < spot_ids[:, None])), axis=1)
+    hot = turned[None, :] & (rank[None, :] == spot_ids[:, None])
+    listed = jnp.sum(jnp.where(hot[None], jnp.stack([spot_ids, sources])[:, None], 0), axis=2)
+    count = jnp.sum(turned.astype(jnp.int32)).reshape(1)
+    table = jnp.concatenate([block_at, scale_at, count, listed.reshape(-1), columns])
+    return table.astype(jnp.int32)
+
+
+def place(table, directs, mirrors, share, here, tile_count, slot_count):
+    chips, blocks, rows, width = directs[0].shape
     pack = mirrors[0].shape[0]
     groups = chips * share // pack
+    behind = extra_blocks(share, rows) * rows
+    direct = jnp.concatenate(directs, axis=0).reshape(2 * chips * blocks, rows, width)
     return pl.pallas_call(
-        functools.partial(place_kernel, share),
+        functools.partial(place_kernel, share, chips),
         out_shape=(
             jax.ShapeDtypeStruct((here, rows, tile_count * width), jnp.float32),
-            jax.ShapeDtypeStruct((1, slots.shape[0], rows, width), jnp.float32),
+            jax.ShapeDtypeStruct((1, slot_count, rows, width), jnp.float32),
         ),
         grid_spec=pltpu.PrefetchScalarGridSpec(
             num_scalar_prefetch=1,
             grid=(),
-            in_specs=[VMEM_SPEC] * 4,
+            in_specs=[VMEM_SPEC] * 3,
             out_specs=[VMEM_SPEC] * 2,
             scratch_shapes=[
-                pltpu.VMEM((2, chips) + scale_scratch(share, rows, width).shape, jnp.float32),
+                pltpu.VMEM((2 * chips * behind + rows, width), jnp.float32),
                 pltpu.VMEM((2, pack) + scale_scratch(groups, rows, width).shape, jnp.float32),
             ],
         ),
         cost_estimate=TINY,
         compiler_params=PARAMS,
-    )(jnp.concatenate([columns, kinds, sources, slots]), *directs, *mirrors)
+    )(table, direct, *mirrors)
 
 
 def take(value, index):
@@ -492,6 +495,7 @@
     matches = (owners[None, :] == me) & (rank[None, :] == slot_ids[:, None])
     slots = jnp.sum(jnp.where(matches, final_pos + 1, 0), axis=1).astype(jnp.int32) - 1
     columns = column ^ jnp.arange(aux_size, dtype=jnp.int32)
+    table = place_table(columns, kinds, sources, slots, share, chips, rows)
 
     def piece(step, low, high, *earlier):
         source = lax.optimization_barrier((factors, earlier))[0] if earlier else factors
@@ -503,7 +507,7 @@
     far += [(step, inner, inner + 1) for inner in range(here) for step in last]
     sent, order = {}, []
     for spot, (step, low, high) in enumerate(far):
-        gate = [order[spot - 2]] if spot >= 2 else ([first] if spot else [])
+        gate = [order[max(0, spot - 4) if spot > 3 else 0]] if spot >= 2 else [first] if spot else []
         block = piece(step, low, high, *gate)
         sent[step, low] = swap(block, "pair", pair_size, step)
         order.append(sent[step, low])
@@ -525,7 +529,7 @@
             swap(other, "aux", aux_size, step + 1) for step, other in enumerate(others)
         ], kept
 
-    groups, earlier = [], ()
+    groups, earlier = [], (table, mine, theirs, enough.astype(jnp.int32).reshape(1))
     for keys, low, high in zip(parts, bounds[:-1], bounds[1:]):
         group, kept = chip_blocks(keys, low, high, *earlier)
         groups.append(group)
@@ -549,17 +553,8 @@
         [turned[0]] + [swap(turned[step], "aux", aux_size, step) for step in range(1, aux_size)]
     )
     other_mirror = swap(own_mirror, "pair", pair_size, 1)
-    return place(
-        columns,
-        kinds,
-        sources,
-        slots,
-        (own_direct, other_direct),
-        (own_mirror, other_mirror),
-        share,
-        here,
-        tile_count,
-    )
+    directs, mirrors = (own_direct, other_direct), (own_mirror, other_mirror)
+    return place(table, directs, mirrors, share, here, tile_count, slot_count)
 
 
 def solution(mesh):

time: 140 us -> 137 us (0.979)
  waiting for transfers between devices: 57 us -> 53.3 us
  starting transfers between devices: 42.9 us -> 45.8 us
  Pallas kernels: 23 us -> 20.4 us
    ppermute x28, waiting for transfers between devices: 57 us -> 53.3 us  [swap(): return lax.ppermute(value, axis, [(i, i ^ step) for i in range(size)])]
    ppermute x28, starting transfers between devices: 42.9 us -> 45.8 us  [swap(): return lax.ppermute(value, axis, [(i, i ^ step) for i in range(size)])]
    pallas_call x1, Pallas kernels: 4.32 us -> 1.85 us  [place(): pl.pallas_call(functools.partial(place_kernel, share, chips), out_shape=(...]
    dynamic_slice x6 -> x4, local copies, waits for them, and re-layouts: 8.88 us -> 6.55 us  [piece(): lax.dynamic_slice(source, start, (depth, high - low, orbitals, width))]
  transfers between devices with their start and end apart: 28 -> 28, of which waited for: 16 -> 15; matrix products, arithmetic and copies ran while one was open for 9% -> 9% of each run, Pallas kernels for 6% -> 7%
where the time goes in v5:
time: 137 us; the launch traced here: 136 us
  waiting for transfers between devices  53.3 us (39%)
  starting transfers between devices  45.8 us (33%)
  Pallas kernels  20.4 us (15%)
  local copies, waits for them, and re-layouts  10.1 us (7%)
  other arithmetic  4.47 us (3%)
  between operations  1.78 us (1%)
    ppermute x28, waiting for transfers between devices, swap(): return lax.ppermute(value, axis, [(i, i ^ step) for i in range(size)])  53.3 us
    ppermute x28, starting transfers between devices, swap(): return lax.ppermute(value, axis, [(i, i ^ step) for i in range(size)])  45.8 us
    pallas_call x4, Pallas kernels, contract(): pl.pallas_call(functools.partial(contract_kernel, spots), out_shape=jax.S...  13.3 us
    dynamic_slice x4, local copies, waits for them, and re-layouts, piece(): lax.dynamic_slice(source, start, (depth, high - low, orbitals, width))  6.55 us
  transfers between devices with their start and end apart: 28, of which 15 were waited for; matrix products, arithmetic and copies ran while one was open for 9% of the time, Pallas kernels for 7%

profile of v5, /device:TPU:0, one launch (start us, length us, event | category | flops | bytes accessed | tf_op | source)
XLA Modules:
  0.0 136.0 jit_solution(14437380117251666881)
XLA Ops:
  0.7 1.0 constant_dynamic-slice_fusion.9
  1.7 3.5 %collective-permute-start.4 = (bf16[12,2,64,128]{3,2,1,0:T(8,128)(2,1)S(1)}, bf16[12,2,64,128]{3,2,1,0:T(8,128)(2,1)S(1)}, u32[]{:S(2)}, u32[]{:S(2)}) collective-permute-start(bf16[12,2,64,128]{3,2,1,0:T(8,128)(2,1)S(1)} %constant_dynamic-slice_fusion.9), channel_id=1, source_target_pairs={{0,20},{4,16},{8,28},{12,24},{16,4},{20,0},{24,12},{28,8},{1,21},{... | collective-permute-start | bytes 1179656 | tf_op jit(solution)/shard_map/ppermute | solution.py:15
  5.2 2.6 %constant_dynamic-slice_fusion = (bf16[12,2,64,128]{3,2,1,0:T(8,128)(2,1)S(1)}, bf16[12,2,64,128]{3,2,1,0:T(8,128)(2,1)S(1)}, bf16[12,2,64,128]{3,2,1,0:T(8,128)...) fusion(bf16[96,2,64,128]{3,2,1,0:T(8,128)(2,1)} %param.6, s32[]{:T(128)S(6)} %select_n.217, ...), kind=kLoop, calls=%fused_computation.44 | loop fusion | bytes 3932180 | tf_op jit(solution)/shard_map/dynamic_slice | solution.py:503
  7.8 1.9 %collective-permute-start.10 = (bf16[12,2,64,128]{3,2,1,0:T(8,128)(2,1)}, bf16[12,2,64,128]{3,2,1,0:T(8,128)(2,1)}, u32[]{:S(2)}, u32[]{:S(2)}) collective-permute-start(bf16[12,2,64,128]{3,2,1,0:T(8,128)(2,1)} %get-tuple-element.117), channel_id=1, source_target_pairs={{0,12},{4,8},{8,4},{12,0},{16,28},{20,24},{24,20},{28,16},{1,13},{... | collective-permute-start | bytes 1179656 | tf_op jit(solution)/shard_map/ppermute | solution.py:15
  13.1 0.7 convert_reduce_fusion.3
  16.6 6.0 %collective-permute-done.4.refs_0_ = bf16[12,2,64,128]{3,2,1,0:T(8,128)(2,1)S(1)} collective-permute-done((bf16[12,2,64,128]{3,2,1,0:T(8,128)(2,1)S(1)}, bf16[12,2,64,128]{3,2,1,0:T(8,128)(2,1)S(1)}, u32[]{:S(2)}, u32[]{:S(2)}) %collective-permute-start.4) | collective-permute-done | bytes 393248 | tf_op jit(solution)/shard_map/ppermute | solution.py:15
  22.6 2.0 %constant_dynamic-slice_fusion.5 = (bf16[12,1,64,128]{3,2,1,0:T(8,128)(2,1)}, bf16[12,1,64,128]{3,2,1,0:T(8,128)(2,1)S(1)}, bf16[12,1,64,128]{3,2,1,0:T(8,128)(2,1)S(1)}) fusion(bf16[96,2,64,128]{3,2,1,0:T(8,128)(2,1)} %param.6, s32[]{:T(128)S(6)} %select_n.212, s32[]{:T(128)S(6)} %select_n.213), kind=kLoop, calls=%fused_computation.49 | loop fusion | bytes 1179656 | tf_op jit(solution)/shard_map/dynamic_slice | solution.py:503
  24.6 4.9 %collective-permute-start.6 = (bf16[12,1,64,128]{3,2,1,0:T(8,128)(2,1)S(1)}, bf16[12,1,64,128]{3,2,1,0:T(8,128)(2,1)S(1)}, u32[]{:S(2)}, u32[]{:S(2)}) collective-permute-start(bf16[12,1,64,128]{3,2,1,0:T(8,128)(2,1)S(1)} %get-tuple-element.121), channel_id=1, source_target_pairs={{0,24},{4,28},{8,16},{12,20},{16,8},{20,12},{24,0},{28,4},{1,25},{... | collective-permute-start | bytes 589832 | tf_op jit(solution)/shard_map/ppermute | solution.py:15
  29.5 4.6 %collective-permute-done.10.refs_4_.refs_6_ = bf16[12,2,64,128]{3,2,1,0:T(8,128)(2,1)} collective-permute-done((bf16[12,2,64,128]{3,2,1,0:T(8,128)(2,1)}, bf16[12,2,64,128]{3,2,1,0:T(8,128)(2,1)}, u32[]{:S(2)}, u32[]{:S(2)}) %collective-permute-start.10) | collective-permute-done | bytes 393248 | tf_op jit(solution)/shard_map/ppermute | solution.py:15
  34.1 3.8 %collective-permute-start.7 = (bf16[12,1,64,128]{3,2,1,0:T(8,128)(2,1)S(1)}, bf16[12,1,64,128]{3,2,1,0:T(8,128)(2,1)S(1)}, u32[]{:S(2)}, u32[]{:S(2)}) collective-permute-start(bf16[12,1,64,128]{3,2,1,0:T(8,128)(2,1)S(1)} %get-tuple-element.120), channel_id=1, source_target_pairs={{0,28},{4,24},{8,20},{12,16},{16,12},{20,8},{24,4},{28,0},{1,29},{... | collective-permute-start | bytes 589832 | tf_op jit(solution)/shard_map/ppermute | solution.py:15
  37.9 0.8 concatenate.35.refs_8_.table
  38.8 12.9 %collective-permute-done.11.refs_5_.refs_7_ = bf16[12,2,64,128]{3,2,1,0:T(8,128)(2,1)} collective-permute-done((bf16[12,2,64,128]{3,2,1,0:T(8,128)(2,1)}, bf16[12,2,64,128]{3,2,1,0:T(8,128)(2,1)}, u32[]{:S(2)}, u32[]{:S(2)}) %collective-permute-start.11) | collective-permute-done | bytes 393248 | tf_op jit(solution)/shard_map/ppermute | solution.py:15
  52.6 3.2 %shard_map.59.refs_8_ = f32[4,22,32,128]{3,2,1,0:T(8,128)S(1)} custom-call(s32[67]{0:T(128)S(1)} %pad_add_fusion.8.table, bf16[12,2,64,128]{3,2,1,0:T(8,128)(2,1)S(1)} %collective-permute-done.4.refs_0_, bf16[12,2,64,128]{3,2,1,0:T(8,128)(2,1)S(1)} %collective-permute-done.5.refs_1_, bf16[12,1,64,128]{3,2,1,0:T(8,128)(2,1)S(1)} %collective-permute-done.6.refs_2_, ...), custom_call_target="tpu_custom_call" | custom-call | flops 1 | bytes 1 | tf_op jit(solution)/shard_map/pallas_call | solution.py:47
  56.1 0.9 constant_dynamic-slice_fusion.4
  57.1 3.3 %collective-permute-start.9 = (bf16[12,1,64,128]{3,2,1,0:T(8,128)(2,1)S(1)}, bf16[12,1,64,128]{3,2,1,0:T(8,128)(2,1)S(1)}, u32[]{:S(2)}, u32[]{:S(2)}) collective-permute-start(bf16[12,1,64,128]{3,2,1,0:T(8,128)(2,1)S(1)} %constant_dynamic-slice_fusion.4), channel_id=1, source_target_pairs={{0,28},{4,24},{8,20},{12,16},{16,12},{20,8},{24,4},{28,0},{1,29},{... | collective-permute-start | bytes 589832 | tf_op jit(solution)/shard_map/ppermute | solution.py:15
  61.2 3.6 %shard_map.60.kept = f32[4,22,32,128]{3,2,1,0:T(8,128)S(1)} custom-call(s32[67]{0:T(128)S(1)} %pad_add_fusion.7.table, bf16[12,2,64,128]{3,2,1,0:T(8,128)(2,1)} %copy-done, bf16[12,2,64,128]{3,2,1,0:T(8,128)(2,1)} %copy-done.5, bf16[12,1,64,128]{3,2,1,0:T(8,128)(2,1)S(1)} %collective-permute-done.6.refs_2_, bf16[12,1,64,128]{3,2,1,0:T(8,128)(2,1)} %copy-done.8, ...), custom_call_target="tpu_custom_call" | custom-call | flops 1 | bytes 1 | tf_op jit(solution)/shard_map/pallas_call | solution.py:47
  64.8 0.7 shard_map.61
  65.6 4.8 %collective-permute-done.8.refs_4_ = bf16[12,1,64,128]{3,2,1,0:T(8,128)(2,1)S(1)} collective-permute-done((bf16[12,1,64,128]{3,2,1,0:T(8,128)(2,1)}, bf16[12,1,64,128]{3,2,1,0:T(8,128)(2,1)S(1)}, u32[]{:S(2)}, u32[]{:S(2)}) %collective-permute-start.8) | collective-permute-done | bytes 196640 | tf_op jit(solution)/shard_map/ppermute | solution.py:15
  70.5 3.0 %shard_map.62.refs_10_ = f32[4,18,32,128]{3,2,1,0:T(8,128)S(1)} custom-call(s32[55]{0:T(128)S(1)} %pad_add_fusion.10.table, bf16[12,2,64,128]{3,2,1,0:T(8,128)(2,1)S(1)} %copy-done.1, bf16[12,2,64,128]{3,2,1,0:T(8,128)(2,1)S(1)} %copy-done.6, bf16[12,1,64,128]{3,2,1,0:T(8,128)(2,1)S(1)} %collective-permute-done.6.refs_2_, ...), custom_call_target="tpu_custom_call" | custom-call | flops 1 | bytes 1 | tf_op jit(solution)/shard_map/pallas_call | solution.py:47
  73.5 2.2 %collective-permute-start.14 = (s16[23,32,128]{2,1,0:T(8,128)(2,1)S(1)}, s16[23,32,128]{2,1,0:T(8,128)(2,1)}, u32[]{:S(2)}, u32[]{:S(2)}) collective-permute-start(s16[23,32,128]{2,1,0:T(8,128)(2,1)S(1)} %get-tuple-element.91), channel_id=1, source_target_pairs={{0,1},{1,0},{2,3},{3,2},{4,5},{5,4},{6,7},{7,6},{8,9},{9,8},{10,11... | collective-permute-start | bytes 565256 | tf_op jit(solution)/shard_map/ppermute | solution.py:15
  75.9 1.5 %collective-permute-start.15 = (s16[23,32,128]{2,1,0:T(8,128)(2,1)S(1)}, s16[23,32,128]{2,1,0:T(8,128)(2,1)S(1)}, u32[]{:S(2)}, u32[]{:S(2)}) collective-permute-start(s16[23,32,128]{2,1,0:T(8,128)(2,1)S(1)} %get-tuple-element.92), channel_id=1, source_target_pairs={{0,2},{1,3},{2,0},{3,1},{4,6},{5,7},{6,4},{7,5},{8,10},{9,11},{10,... | collective-permute-start | bytes 565256 | tf_op jit(solution)/shard_map/ppermute | solution.py:15
  77.5 3.6 %shard_map.63.kept = f32[4,18,32,128]{3,2,1,0:T(8,128)S(1)} custom-call(s32[55]{0:T(128)S(1)} %pad_add_fusion.9.table, bf16[12,2,64,128]{3,2,1,0:T(8,128)(2,1)} %copy-done, bf16[12,2,64,128]{3,2,1,0:T(8,128)(2,1)} %copy-done.5, bf16[12,1,64,128]{3,2,1,0:T(8,128)(2,1)S(1)} %collective-permute-done.6.refs_2_, bf16[12,1,64,128]{3,2,1,0:T(8,128)(2,1)} %copy-done.8, ...), custom_call_target="tpu_custom_call" | custom-call | flops 1 | bytes 1 | tf_op jit(solution)/shard_map/pallas_call | solution.py:47
  81.0 1.2 shard_map.64
  82.2 2.0 %collective-permute-start.18 = (s16[19,32,128]{2,1,0:T(8,128)(2,1)S(1)}, s16[19,32,128]{2,1,0:T(8,128)(2,1)S(1)}, u32[]{:S(2)}, u32[]{:S(2)}) collective-permute-start(s16[19,32,128]{2,1,0:T(8,128)(2,1)S(1)} %get-tuple-element.95), channel_id=1, source_target_pairs={{0,1},{1,0},{2,3},{3,2},{4,5},{5,4},{6,7},{7,6},{8,9},{9,8},{10,11... | collective-permute-start | bytes 466952 | tf_op jit(solution)/shard_map/ppermute | solution.py:15
  84.2 1.5 %collective-permute-start.19 = (s16[19,32,128]{2,1,0:T(8,128)(2,1)S(1)}, s16[19,32,128]{2,1,0:T(8,128)(2,1)S(1)}, u32[]{:S(2)}, u32[]{:S(2)}) collective-permute-start(s16[19,32,128]{2,1,0:T(8,128)(2,1)S(1)} %get-tuple-element.96), channel_id=1, source_target_pairs={{0,2},{1,3},{2,0},{3,1},{4,6},{5,7},{6,4},{7,5},{8,10},{9,11},{10,... | collective-permute-start | bytes 466952 | tf_op jit(solution)/shard_map/ppermute | solution.py:15
  85.7 1.2 collective-permute-done.15
  86.9 2.3 %collective-permute-done.18 = s16[19,32,128]{2,1,0:T(8,128)(2,1)S(1)} collective-permute-done((s16[19,32,128]{2,1,0:T(8,128)(2,1)S(1)}, s16[19,32,128]{2,1,0:T(8,128)(2,1)S(1)}, u32[]{:S(2)}, u32[]{:S(2)}) %collective-permute-start.18) | collective-permute-done | bytes 155680 | tf_op jit(solution)/shard_map/ppermute | solution.py:15
  89.2 4.2 %collective-permute-done.19 = s16[19,32,128]{2,1,0:T(8,128)(2,1)S(1)} collective-permute-done((s16[19,32,128]{2,1,0:T(8,128)(2,1)S(1)}, s16[19,32,128]{2,1,0:T(8,128)(2,1)S(1)}, u32[]{:S(2)}, u32[]{:S(2)}) %collective-permute-start.19) | collective-permute-done | bytes 155680 | tf_op jit(solution)/shard_map/ppermute | solution.py:15
  93.4 2.4 %conditional.1 = ((f32[10,32,128]{2,1,0:T(8,128)S(1)}, s16[11,32,128]{2,1,0:T(8,128)(2,1)S(1)}, s16[11,32,128]{2,1,0:T(8,128)(2,1)S(1)}, s16[11,32,128]{2,1,0:T(8,128)(2,1)S(1)})) conditional(s32[]{:T(128)} %convert_element_type.65, (s32[4,40]{1,0:T(4,128)S(1)}, s32[]{:T(128)}, s32[4,40]{1,0:T(4,128)S(1)}, bf16[12,2,64,128]{3,2,1,0:T(8,128)(2,1)}, ...), branch_computations={%region_16.17_spmd, %region_17.18_spmd} | conditional | flops 246 | bytes 16978228 | solution.py:537
  93.4 2.4 %branch_1_fun.1 = (f32[10,32,128]{2,1,0:T(8,128)S(1)}, s16[11,32,128]{2,1,0:T(8,128)(2,1)S(1)}, s16[11,32,128]{2,1,0:T(8,128)(2,1)S(1)}, s16[11,32,128]{2,1,0:T(8,128)(2,1)S(1)}) custom-call(s32[40]{0:T(128)S(1)} %slice_bitcast_fusion.1.refs_0_, f32[22,32,128]{2,1,0:T(8,128)} %get-tuple-element.62.refs_1_, s16[23,32,128]{2,1,0:T(8,128)(2,1)} %get-tuple-element.63.refs_2_, ...), custom_call_target="tpu_custom_call" | custom-call | flops 1 | bytes 1 | tf_op jit(solution)/shard_map/cond/branch_1_fun/pallas_call | solution.py:215
  95.7 8.9 %collective-permute-start.21 = (s16[11,32,128]{2,1,0:T(8,128)(2,1)S(1)}, s16[11,32,128]{2,1,0:T(8,128)(2,1)S(1)}, u32[]{:S(2)}, u32[]{:S(2)}) collective-permute-start(s16[11,32,128]{2,1,0:T(8,128)(2,1)S(1)} %get-tuple-element.99), channel_id=1, source_target_pairs={{0,8},{4,12},{8,0},{12,4},{16,24},{20,28},{24,16},{28,20},{1,9},{5... | collective-permute-start | bytes 270344 | tf_op jit(solution)/shard_map/ppermute | solution.py:15
  104.7 1.1 collective-permute-start.22
  105.8 1.4 %collective-permute-start.23 = (s16[11,32,128]{2,1,0:T(8,128)(2,1)S(1)}, s16[11,32,128]{2,1,0:T(8,128)(2,1)S(1)}, u32[]{:S(2)}, u32[]{:S(2)}) collective-permute-start(s16[11,32,128]{2,1,0:T(8,128)(2,1)S(1)} %get-tuple-element.101), channel_id=1, source_target_pairs={{0,24},{4,28},{8,16},{12,20},{16,8},{20,12},{24,0},{28,4},{1,25},{... | collective-permute-start | bytes 270344 | tf_op jit(solution)/shard_map/ppermute | solution.py:15
  107.2 0.9 collective-permute-done.21.refs_1_
  108.1 5.3 %collective-permute-done.22.refs_2_ = s16[11,32,128]{2,1,0:T(8,128)(2,1)S(1)} collective-permute-done((s16[11,32,128]{2,1,0:T(8,128)(2,1)S(1)}, s16[11,32,128]{2,1,0:T(8,128)(2,1)S(1)}, u32[]{:S(2)}, u32[]{:S(2)}) %collective-permute-start.22) | collective-permute-done | bytes 90144 | tf_op jit(solution)/shard_map/ppermute | solution.py:15
  113.7 1.6 %collective-permute-start.24 = (s16[11,32,128]{2,1,0:T(8,128)(2,1)S(1)}, s16[11,32,128]{2,1,0:T(8,128)(2,1)S(1)}, u32[]{:S(2)}, u32[]{:S(2)}) collective-permute-start(s16[11,32,128]{2,1,0:T(8,128)(2,1)S(1)} %shard_map.65.refs_0_), channel_id=1, source_target_pairs={{0,8},{4,12},{8,0},{12,4},{16,24},{20,28},{24,16},{28,20},{1,9},{5... | collective-permute-start | bytes 270344 | tf_op jit(solution)/shard_map/ppermute | solution.py:15
  115.3 1.3 collective-permute-start.25
  116.6 1.5 %collective-permute-start.26 = (s16[11,32,128]{2,1,0:T(8,128)(2,1)S(1)}, s16[11,32,128]{2,1,0:T(8,128)(2,1)S(1)}, u32[]{:S(2)}, u32[]{:S(2)}) collective-permute-start(s16[11,32,128]{2,1,0:T(8,128)(2,1)S(1)} %shard_map.65.refs_0_), channel_id=1, source_target_pairs={{0,24},{4,28},{8,16},{12,20},{16,8},{20,12},{24,0},{28,4},{1,25},{... | collective-permute-start | bytes 270344 | tf_op jit(solution)/shard_map/ppermute | solution.py:15
  118.1 0.8 collective-permute-done.24.refs_1_
  118.9 4.8 %collective-permute-done.25.refs_2_ = s16[11,32,128]{2,1,0:T(8,128)(2,1)S(1)} collective-permute-done((s16[11,32,128]{2,1,0:T(8,128)(2,1)S(1)}, s16[11,32,128]{2,1,0:T(8,128)(2,1)S(1)}, u32[]{:S(2)}, u32[]{:S(2)}) %collective-permute-start.25) | collective-permute-done | bytes 90144 | tf_op jit(solution)/shard_map/ppermute | solution.py:15
  123.7 0.9 shard_map.66
  124.6 1.8 %collective-permute-start.28 = (s16[11,32,128]{2,1,0:T(8,128)(2,1)S(1)}, s16[11,32,128]{2,1,0:T(8,128)(2,1)S(1)}, u32[]{:S(2)}, u32[]{:S(2)}) collective-permute-start(s16[11,32,128]{2,1,0:T(8,128)(2,1)S(1)} %get-tuple-element.125), channel_id=1, source_target_pairs={{0,1},{1,0},{2,3},{3,2},{4,5},{5,4},{6,7},{7,6},{8,9},{9,8},{10,11... | collective-permute-start | bytes 270344 | tf_op jit(solution)/shard_map/ppermute | solution.py:15
  126.9 1.4 %collective-permute-start.30 = (s16[11,32,128]{2,1,0:T(8,128)(2,1)S(1)}, s16[11,32,128]{2,1,0:T(8,128)(2,1)S(1)}, u32[]{:S(2)}, u32[]{:S(2)}) collective-permute-start(s16[11,32,128]{2,1,0:T(8,128)(2,1)S(1)} %get-tuple-element.123), channel_id=1, source_target_pairs={{0,3},{1,2},{2,1},{3,0},{4,7},{5,6},{6,5},{7,4},{8,11},{9,10},{10,... | collective-permute-start | bytes 270344 | tf_op jit(solution)/shard_map/ppermute | solution.py:15
  128.4 0.8 collective-permute-done.28
  129.2 1.8 %collective-permute-done.29 = s16[11,32,128]{2,1,0:T(8,128)(2,1)S(1)} collective-permute-done((s16[11,32,128]{2,1,0:T(8,128)(2,1)S(1)}, s16[11,32,128]{2,1,0:T(8,128)(2,1)S(1)}, u32[]{:S(2)}, u32[]{:S(2)}) %collective-permute-start.29) | collective-permute-done | bytes 90144 | tf_op jit(solution)/shard_map/ppermute | solution.py:15
  131.0 1.4 collective-permute-done.30
  132.6 1.6 %collective-permute-done.31.refs_2_ = s16[4,11,32,128]{3,2,1,0:T(8,128)(2,1)S(1)} collective-permute-done((s16[4,11,32,128]{3,2,1,0:T(8,128)(2,1)S(1)}, s16[4,11,32,128]{3,2,1,0:T(8,128)(2,1)S(1)}, u32[]{:S(2)}, u32[]{:S(2)}) %collective-permute-start.31) | collective-permute-done | bytes 360480 | tf_op jit(solution)/shard_map/ppermute | solution.py:15
  134.1 1.9 %shard_map.67 = (f32[2,32,2048]{2,1,0:T(8,128)}, f32[1,40,32,128]{3,2,1,0:T(8,128)}) custom-call(s32[213]{0:T(256)S(1)} %concatenate.35.refs_8_.table, s16[88,32,128]{2,1,0:T(8,128)(2,1)S(1)} %bitcast.38, s16[4,11,32,128]{3,2,1,0:T(8,128)(2,1)S(1)} %pad_add_fusion.3.refs_1_, s16[4,11,32,128]{3,2,1,0:T(8,128)(2,1)S(1)} %collective-permute-done.31.refs_2_), custom_call_target="tpu_custom_call" | custom-call | flops 1 | bytes 1 | tf_op jit(solution)/shard_map/pallas_call | solution.py:387
  (121 shorter events, 8.9 us)
Async XLA Ops:
  0.6 9.8 %copy-start.13 = (s32[80,2]{0,1:T(2,128)S(1)}, s32[80,2]{0,1:T(2,128)}, u32[]{:S(2)}) copy-start(s32[80,2]{0,1:T(2,128)} %param.7) | copy-start | bytes 1924
  0.6 9.8 %copy-start.14 = (s32[80]{0:T(128)S(1)}, s32[80]{0:T(128)}, u32[]{:S(2)}) copy-start(s32[80]{0:T(128)} %param.9) | copy-start | bytes 964
  0.7 11.2 %copy-start.15 = (s32[80,1]{0,1:T(1,128)S(1)}, s32[80,1]{0,1:T(1,128)}, u32[]{:S(2)}) copy-start(s32[80,1]{0,1:T(1,128)} %param.8) | copy-start | bytes 964
  1.7 20.9 %collective-permute-start.4 = (bf16[12,2,64,128]{3,2,1,0:T(8,128)(2,1)S(1)}, bf16[12,2,64,128]{3,2,1,0:T(8,128)(2,1)S(1)}, u32[]{:S(2)}, u32[]{:S(2)}) collective-permute-start(bf16[12,2,64,128]{3,2,1,0:T(8,128)(2,1)S(1)} %constant_dynamic-slice_fusion.9), channel_id=1, source_target_pairs={{0,20},{4,16},{8,28},{12,24},{16,4},{20,0},{24,12},{28,8},{1,21},{... | collective-permute-start | bytes 1179656 | tf_op jit(solution)/shard_map/ppermute | solution.py:15
  7.8 26.3 %collective-permute-start.10 = (bf16[12,2,64,128]{3,2,1,0:T(8,128)(2,1)}, bf16[12,2,64,128]{3,2,1,0:T(8,128)(2,1)}, u32[]{:S(2)}, u32[]{:S(2)}) collective-permute-start(bf16[12,2,64,128]{3,2,1,0:T(8,128)(2,1)} %get-tuple-element.117), channel_id=1, source_target_pairs={{0,12},{4,8},{8,4},{12,0},{16,28},{20,24},{24,20},{28,16},{1,13},{... | collective-permute-start | bytes 1179656 | tf_op jit(solution)/shard_map/ppermute | solution.py:15
  9.7 42.0 %collective-permute-start.11 = (bf16[12,2,64,128]{3,2,1,0:T(8,128)(2,1)}, bf16[12,2,64,128]{3,2,1,0:T(8,128)(2,1)}, u32[]{:S(2)}, u32[]{:S(2)}) collective-permute-start(bf16[12,2,64,128]{3,2,1,0:T(8,128)(2,1)} %get-tuple-element.116), channel_id=1, source_target_pairs={{0,8},{4,12},{8,0},{12,4},{16,24},{20,28},{24,16},{28,20},{1,9},{5... | collective-permute-start | bytes 1179656 | tf_op jit(solution)/shard_map/ppermute | solution.py:15
  10.2 41.5 %collective-permute-start.12 = (bf16[12,2,64,128]{3,2,1,0:T(8,128)(2,1)S(1)}, bf16[12,2,64,128]{3,2,1,0:T(8,128)(2,1)S(1)}, u32[]{:S(2)}, u32[]{:S(2)}) collective-permute-start(bf16[12,2,64,128]{3,2,1,0:T(8,128)(2,1)S(1)} %get-tuple-element.115), channel_id=1, source_target_pairs={{0,4},{4,0},{8,12},{12,8},{16,20},{20,16},{24,28},{28,24},{1,5},{5... | collective-permute-start | bytes 1179656 | tf_op jit(solution)/shard_map/ppermute | solution.py:15
  10.2 41.5 %collective-permute-start.5 = (bf16[12,2,64,128]{3,2,1,0:T(8,128)(2,1)S(1)}, bf16[12,2,64,128]{3,2,1,0:T(8,128)(2,1)S(1)}, u32[]{:S(2)}, u32[]{:S(2)}) collective-permute-start(bf16[12,2,64,128]{3,2,1,0:T(8,128)(2,1)S(1)} %get-tuple-element.118), channel_id=1, source_target_pairs={{0,16},{4,20},{8,24},{12,28},{16,0},{20,4},{24,8},{28,12},{1,17},{... | collective-permute-start | bytes 1179656 | tf_op jit(solution)/shard_map/ppermute | solution.py:15
  22.6 29.1 %copy-start = (bf16[12,2,64,128]{3,2,1,0:T(8,128)(2,1)}, bf16[12,2,64,128]{3,2,1,0:T(8,128)(2,1)S(1)}, u32[]{:S(2)}) copy-start(bf16[12,2,64,128]{3,2,1,0:T(8,128)(2,1)S(1)} %collective-permute-done.4.refs_0_) | copy-start | bytes 1179652
  24.6 27.1 %collective-permute-start.6 = (bf16[12,1,64,128]{3,2,1,0:T(8,128)(2,1)S(1)}, bf16[12,1,64,128]{3,2,1,0:T(8,128)(2,1)S(1)}, u32[]{:S(2)}, u32[]{:S(2)}) collective-permute-start(bf16[12,1,64,128]{3,2,1,0:T(8,128)(2,1)S(1)} %get-tuple-element.121), channel_id=1, source_target_pairs={{0,24},{4,28},{8,16},{12,20},{16,8},{20,12},{24,0},{28,4},{1,25},{... | collective-permute-start | bytes 589832 | tf_op jit(solution)/shard_map/ppermute | solution.py:15
  34.1 17.6 %collective-permute-start.7 = (bf16[12,1,64,128]{3,2,1,0:T(8,128)(2,1)S(1)}, bf16[12,1,64,128]{3,2,1,0:T(8,128)(2,1)S(1)}, u32[]{:S(2)}, u32[]{:S(2)}) collective-permute-start(bf16[12,1,64,128]{3,2,1,0:T(8,128)(2,1)S(1)} %get-tuple-element.120), channel_id=1, source_target_pairs={{0,28},{4,24},{8,20},{12,16},{16,12},{20,8},{24,4},{28,0},{1,29},{... | collective-permute-start | bytes 589832 | tf_op jit(solution)/shard_map/ppermute | solution.py:15
  51.7 0.7 copy-start.3
  51.7 0.9 copy-start.5
  51.7 0.9 copy-start.8
  55.8 9.0 %collective-permute-start.13 = (f32[4,22,32,128]{3,2,1,0:T(8,128)S(1)}, f32[4,22,32,128]{3,2,1,0:T(8,128)S(1)}, u32[]{:S(2)}, u32[]{:S(2)}) collective-permute-start(f32[4,22,32,128]{3,2,1,0:T(8,128)S(1)} %shard_map.59.refs_8_), channel_id=1, source_target_pairs={{0,4},{4,0},{8,12},{12,8},{16,20},{20,16},{24,28},{28,24},{1,5},{5... | collective-permute-start | bytes 4325384 | tf_op jit(solution)/shard_map/ppermute | solution.py:15
  57.1 8.5 %collective-permute-start.9 = (bf16[12,1,64,128]{3,2,1,0:T(8,128)(2,1)S(1)}, bf16[12,1,64,128]{3,2,1,0:T(8,128)(2,1)S(1)}, u32[]{:S(2)}, u32[]{:S(2)}) collective-permute-start(bf16[12,1,64,128]{3,2,1,0:T(8,128)(2,1)S(1)} %constant_dynamic-slice_fusion.4), channel_id=1, source_target_pairs={{0,28},{4,24},{8,20},{12,16},{16,12},{20,8},{24,4},{28,0},{1,29},{... | collective-permute-start | bytes 589832 | tf_op jit(solution)/shard_map/ppermute | solution.py:15
  60.4 10.1 %collective-permute-start.8 = (bf16[12,1,64,128]{3,2,1,0:T(8,128)(2,1)}, bf16[12,1,64,128]{3,2,1,0:T(8,128)(2,1)S(1)}, u32[]{:S(2)}, u32[]{:S(2)}) collective-permute-start(bf16[12,1,64,128]{3,2,1,0:T(8,128)(2,1)} %get-tuple-element.119), channel_id=1, source_target_pairs={{0,24},{4,28},{8,16},{12,20},{16,8},{20,12},{24,0},{28,4},{1,25},{... | collective-permute-start | bytes 589832 | tf_op jit(solution)/shard_map/ppermute | solution.py:15
  64.8 5.7 %copy-start.1 = (bf16[12,2,64,128]{3,2,1,0:T(8,128)(2,1)S(1)}, bf16[12,2,64,128]{3,2,1,0:T(8,128)(2,1)}, u32[]{:S(2)}) copy-start(bf16[12,2,64,128]{3,2,1,0:T(8,128)(2,1)} %copy-done) | copy-start | bytes 1179652
  64.8 5.7 %copy-start.4 = (bf16[12,2,64,128]{3,2,1,0:T(8,128)(2,1)S(1)}, bf16[12,2,64,128]{3,2,1,0:T(8,128)(2,1)}, u32[]{:S(2)}) copy-start(bf16[12,2,64,128]{3,2,1,0:T(8,128)(2,1)} %copy-done.3) | copy-start | bytes 1179652
  64.8 5.7 %copy-start.6 = (bf16[12,2,64,128]{3,2,1,0:T(8,128)(2,1)S(1)}, bf16[12,2,64,128]{3,2,1,0:T(8,128)(2,1)}, u32[]{:S(2)}) copy-start(bf16[12,2,64,128]{3,2,1,0:T(8,128)(2,1)} %copy-done.5) | copy-start | bytes 1179652
  64.8 5.6 %copy-start.9 = (bf16[12,1,64,128]{3,2,1,0:T(8,128)(2,1)S(1)}, bf16[12,1,64,128]{3,2,1,0:T(8,128)(2,1)}, u32[]{:S(2)}) copy-start(bf16[12,1,64,128]{3,2,1,0:T(8,128)(2,1)} %copy-done.8) | copy-start | bytes 589828
  65.5 10.1 %copy-start.12 = (f32[22,32,128]{2,1,0:T(8,128)}, f32[22,32,128]{2,1,0:T(8,128)S(1)}, u32[]{:S(2)}) copy-start(f32[22,32,128]{2,1,0:T(8,128)S(1)} %get-tuple-element.90.refs_10_) | copy-start | bytes 1081348
  65.6 10.1 %copy-start.10 = (bf16[12,1,64,128]{3,2,1,0:T(8,128)(2,1)}, bf16[12,1,64,128]{3,2,1,0:T(8,128)(2,1)S(1)}, u32[]{:S(2)}) copy-start(bf16[12,1,64,128]{3,2,1,0:T(8,128)(2,1)S(1)} %collective-permute-done.9.refs_5_) | copy-start | bytes 589828
  70.4 5.3 %copy-start.11 = (bf16[12,1,64,128]{3,2,1,0:T(8,128)(2,1)}, bf16[12,1,64,128]{3,2,1,0:T(8,128)(2,1)S(1)}, u32[]{:S(2)}) copy-start(bf16[12,1,64,128]{3,2,1,0:T(8,128)(2,1)S(1)} %collective-permute-done.8.refs_4_) | copy-start | bytes 589828
  73.4 7.6 %collective-permute-start.17 = (f32[4,18,32,128]{3,2,1,0:T(8,128)S(1)}, f32[4,18,32,128]{3,2,1,0:T(8,128)S(1)}, u32[]{:S(2)}, u32[]{:S(2)}) collective-permute-start(f32[4,18,32,128]{3,2,1,0:T(8,128)S(1)} %shard_map.62.refs_10_), channel_id=1, source_target_pairs={{0,4},{4,0},{8,12},{12,8},{16,20},{20,16},{24,28},{28,24},{1,5},{5... | collective-permute-start | bytes 3538952 | tf_op jit(solution)/shard_map/ppermute | solution.py:15
  73.5 12.2 %collective-permute-start.14 = (s16[23,32,128]{2,1,0:T(8,128)(2,1)S(1)}, s16[23,32,128]{2,1,0:T(8,128)(2,1)}, u32[]{:S(2)}, u32[]{:S(2)}) collective-permute-start(s16[23,32,128]{2,1,0:T(8,128)(2,1)S(1)} %get-tuple-element.91), channel_id=1, source_target_pairs={{0,1},{1,0},{2,3},{3,2},{4,5},{5,4},{6,7},{7,6},{8,9},{9,8},{10,11... | collective-permute-start | bytes 565256 | tf_op jit(solution)/shard_map/ppermute | solution.py:15
  75.9 11.0 %collective-permute-start.15 = (s16[23,32,128]{2,1,0:T(8,128)(2,1)S(1)}, s16[23,32,128]{2,1,0:T(8,128)(2,1)S(1)}, u32[]{:S(2)}, u32[]{:S(2)}) collective-permute-start(s16[23,32,128]{2,1,0:T(8,128)(2,1)S(1)} %get-tuple-element.92), channel_id=1, source_target_pairs={{0,2},{1,3},{2,0},{3,1},{4,6},{5,7},{6,4},{7,5},{8,10},{9,11},{10,... | collective-permute-start | bytes 565256 | tf_op jit(solution)/shard_map/ppermute | solution.py:15
  77.4 9.5 %collective-permute-start.16 = (s16[23,32,128]{2,1,0:T(8,128)(2,1)S(1)}, s16[23,32,128]{2,1,0:T(8,128)(2,1)S(1)}, u32[]{:S(2)}, u32[]{:S(2)}) collective-permute-start(s16[23,32,128]{2,1,0:T(8,128)(2,1)S(1)} %get-tuple-element.93), channel_id=1, source_target_pairs={{0,3},{1,2},{2,1},{3,0},{4,7},{5,6},{6,5},{7,4},{8,11},{9,10},{10,... | collective-permute-start | bytes 565256 | tf_op jit(solution)/shard_map/ppermute | solution.py:15
  82.2 7.0 %collective-permute-start.18 = (s16[19,32,128]{2,1,0:T(8,128)(2,1)S(1)}, s16[19,32,128]{2,1,0:T(8,128)(2,1)S(1)}, u32[]{:S(2)}, u32[]{:S(2)}) collective-permute-start(s16[19,32,128]{2,1,0:T(8,128)(2,1)S(1)} %get-tuple-element.95), channel_id=1, source_target_pairs={{0,1},{1,0},{2,3},{3,2},{4,5},{5,4},{6,7},{7,6},{8,9},{9,8},{10,11... | collective-permute-start | bytes 466952 | tf_op jit(solution)/shard_map/ppermute | solution.py:15
  84.2 9.2 %collective-permute-start.19 = (s16[19,32,128]{2,1,0:T(8,128)(2,1)S(1)}, s16[19,32,128]{2,1,0:T(8,128)(2,1)S(1)}, u32[]{:S(2)}, u32[]{:S(2)}) collective-permute-start(s16[19,32,128]{2,1,0:T(8,128)(2,1)S(1)} %get-tuple-element.96), channel_id=1, source_target_pairs={{0,2},{1,3},{2,0},{3,1},{4,6},{5,7},{6,4},{7,5},{8,10},{9,11},{10,... | collective-permute-start | bytes 466952 | tf_op jit(solution)/shard_map/ppermute | solution.py:15
  85.7 7.7 %collective-permute-start.20 = (s16[19,32,128]{2,1,0:T(8,128)(2,1)S(1)}, s16[19,32,128]{2,1,0:T(8,128)(2,1)S(1)}, u32[]{:S(2)}, u32[]{:S(2)}) collective-permute-start(s16[19,32,128]{2,1,0:T(8,128)(2,1)S(1)} %get-tuple-element.97), channel_id=1, source_target_pairs={{0,3},{1,2},{2,1},{3,0},{4,7},{5,6},{6,5},{7,4},{8,11},{9,10},{10,... | collective-permute-start | bytes 466952 | tf_op jit(solution)/shard_map/ppermute | solution.py:15
  95.7 12.4 %collective-permute-start.21 = (s16[11,32,128]{2,1,0:T(8,128)(2,1)S(1)}, s16[11,32,128]{2,1,0:T(8,128)(2,1)S(1)}, u32[]{:S(2)}, u32[]{:S(2)}) collective-permute-start(s16[11,32,128]{2,1,0:T(8,128)(2,1)S(1)} %get-tuple-element.99), channel_id=1, source_target_pairs={{0,8},{4,12},{8,0},{12,4},{16,24},{20,28},{24,16},{28,20},{1,9},{5... | collective-permute-start | bytes 270344 | tf_op jit(solution)/shard_map/ppermute | solution.py:15
  104.7 8.8 %collective-permute-start.22 = (s16[11,32,128]{2,1,0:T(8,128)(2,1)S(1)}, s16[11,32,128]{2,1,0:T(8,128)(2,1)S(1)}, u32[]{:S(2)}, u32[]{:S(2)}) collective-permute-start(s16[11,32,128]{2,1,0:T(8,128)(2,1)S(1)} %get-tuple-element.100), channel_id=1, source_target_pairs={{0,16},{4,20},{8,24},{12,28},{16,0},{20,4},{24,8},{28,12},{1,17},{... | collective-permute-start | bytes 270344 | tf_op jit(solution)/shard_map/ppermute | solution.py:15
  105.8 7.6 %collective-permute-start.23 = (s16[11,32,128]{2,1,0:T(8,128)(2,1)S(1)}, s16[11,32,128]{2,1,0:T(8,128)(2,1)S(1)}, u32[]{:S(2)}, u32[]{:S(2)}) collective-permute-start(s16[11,32,128]{2,1,0:T(8,128)(2,1)S(1)} %get-tuple-element.101), channel_id=1, source_target_pairs={{0,24},{4,28},{8,16},{12,20},{16,8},{20,12},{24,0},{28,4},{1,25},{... | collective-permute-start | bytes 270344 | tf_op jit(solution)/shard_map/ppermute | solution.py:15
  113.7 5.2 %collective-permute-start.24 = (s16[11,32,128]{2,1,0:T(8,128)(2,1)S(1)}, s16[11,32,128]{2,1,0:T(8,128)(2,1)S(1)}, u32[]{:S(2)}, u32[]{:S(2)}) collective-permute-start(s16[11,32,128]{2,1,0:T(8,128)(2,1)S(1)} %shard_map.65.refs_0_), channel_id=1, source_target_pairs={{0,8},{4,12},{8,0},{12,4},{16,24},{20,28},{24,16},{28,20},{1,9},{5... | collective-permute-start | bytes 270344 | tf_op jit(solution)/shard_map/ppermute | solution.py:15
  115.3 8.5 %collective-permute-start.25 = (s16[11,32,128]{2,1,0:T(8,128)(2,1)S(1)}, s16[11,32,128]{2,1,0:T(8,128)(2,1)S(1)}, u32[]{:S(2)}, u32[]{:S(2)}) collective-permute-start(s16[11,32,128]{2,1,0:T(8,128)(2,1)S(1)} %shard_map.65.refs_0_), channel_id=1, source_target_pairs={{0,16},{4,20},{8,24},{12,28},{16,0},{20,4},{24,8},{28,12},{1,17},{... | collective-permute-start | bytes 270344 | tf_op jit(solution)/shard_map/ppermute | solution.py:15
  116.6 7.1 %collective-permute-start.26 = (s16[11,32,128]{2,1,0:T(8,128)(2,1)S(1)}, s16[11,32,128]{2,1,0:T(8,128)(2,1)S(1)}, u32[]{:S(2)}, u32[]{:S(2)}) collective-permute-start(s16[11,32,128]{2,1,0:T(8,128)(2,1)S(1)} %shard_map.65.refs_0_), channel_id=1, source_target_pairs={{0,24},{4,28},{8,16},{12,20},{16,8},{20,12},{24,0},{28,4},{1,25},{... | collective-permute-start | bytes 270344 | tf_op jit(solution)/shard_map/ppermute | solution.py:15
  124.6 4.6 %collective-permute-start.28 = (s16[11,32,128]{2,1,0:T(8,128)(2,1)S(1)}, s16[11,32,128]{2,1,0:T(8,128)(2,1)S(1)}, u32[]{:S(2)}, u32[]{:S(2)}) collective-permute-start(s16[11,32,128]{2,1,0:T(8,128)(2,1)S(1)} %get-tuple-element.125), channel_id=1, source_target_pairs={{0,1},{1,0},{2,3},{3,2},{4,5},{5,4},{6,7},{7,6},{8,9},{9,8},{10,11... | collective-permute-start | bytes 270344 | tf_op jit(solution)/shard_map/ppermute | solution.py:15
  126.5 4.5 %collective-permute-start.29 = (s16[11,32,128]{2,1,0:T(8,128)(2,1)S(1)}, s16[11,32,128]{2,1,0:T(8,128)(2,1)S(1)}, u32[]{:S(2)}, u32[]{:S(2)}) collective-permute-start(s16[11,32,128]{2,1,0:T(8,128)(2,1)S(1)} %get-tuple-element.124), channel_id=1, source_target_pairs={{0,2},{1,3},{2,0},{3,1},{4,6},{5,7},{6,4},{7,5},{8,10},{9,11},{10,... | collective-permute-start | bytes 270344 | tf_op jit(solution)/shard_map/ppermute | solution.py:15
  126.9 5.4 %collective-permute-start.30 = (s16[11,32,128]{2,1,0:T(8,128)(2,1)S(1)}, s16[11,32,128]{2,1,0:T(8,128)(2,1)S(1)}, u32[]{:S(2)}, u32[]{:S(2)}) collective-permute-start(s16[11,32,128]{2,1,0:T(8,128)(2,1)S(1)} %get-tuple-element.123), channel_id=1, source_target_pairs={{0,3},{1,2},{2,1},{3,0},{4,7},{5,6},{6,5},{7,4},{8,11},{9,10},{10,... | collective-permute-start | bytes 270344 | tf_op jit(solution)/shard_map/ppermute | solution.py:15
  128.3 4.2 %collective-permute-start.27 = (s16[4,11,32,128]{3,2,1,0:T(8,128)(2,1)S(1)}, s16[4,11,32,128]{3,2,1,0:T(8,128)(2,1)S(1)}, u32[]{:S(2)}, u32[]{:S(2)}) collective-permute-start(s16[4,11,32,128]{3,2,1,0:T(8,128)(2,1)S(1)} %pad_add_fusion.2), channel_id=1, source_target_pairs={{0,4},{4,0},{8,12},{12,8},{16,20},{20,16},{24,28},{28,24},{1,5},{5... | collective-permute-start | bytes 1081352 | tf_op jit(solution)/shard_map/ppermute | solution.py:15
  132.4 1.7 %collective-permute-start.31 = (s16[4,11,32,128]{3,2,1,0:T(8,128)(2,1)S(1)}, s16[4,11,32,128]{3,2,1,0:T(8,128)(2,1)S(1)}, u32[]{:S(2)}, u32[]{:S(2)}) collective-permute-start(s16[4,11,32,128]{3,2,1,0:T(8,128)(2,1)S(1)} %pad_add_fusion.3.refs_1_), channel_id=1, source_target_pairs={{0,4},{4,0},{8,12},{12,8},{16,20},{20,16},{24,28},{28,24},{1,5},{5... | collective-permute-start | bytes 1081352 | tf_op jit(solution)/shard_map/ppermute | solution.py:15

commit v6 on v5

--- a/solution.py
+++ b/solution.py
@@ -507,7 +507,7 @@
     far += [(step, inner, inner + 1) for inner in range(here) for step in last]
     sent, order = {}, []
     for spot, (step, low, high) in enumerate(far):
-        gate = [order[max(0, spot - 4) if spot > 3 else 0]] if spot >= 2 else [first] if spot else []
+        gate = [order[0]] if spot >= 2 else [first] if spot else []
         block = piece(step, low, high, *gate)
         sent[step, low] = swap(block, "pair", pair_size, step)
         order.append(sent[step, low])

time: 137 us -> 136 us (level)
    dynamic_slice x4 -> x3, local copies, waits for them, and re-layouts: 6.55 us -> 5.81 us  [piece(): lax.dynamic_slice(source, start, (depth, high - low, orbitals, width))]
  transfers between devices with their start and end apart: 28 -> 28, of which waited for: 15 -> 16; matrix products, arithmetic and copies ran while one was open for 9% -> 9% of each run, Pallas kernels for 7% -> 7%
where the time goes in v6:
time: 136 us; the launch traced here: 135 us
  waiting for transfers between devices  53.2 us (39%)
  starting transfers between devices  46 us (34%)
  Pallas kernels  20.4 us (15%)
  local copies, waits for them, and re-layouts  9.39 us (7%)
  other arithmetic  4.47 us (3%)
  between operations  1.77 us (1%)
    ppermute x28, waiting for transfers between devices, swap(): return lax.ppermute(value, axis, [(i, i ^ step) for i in range(size)])  53.2 us
    ppermute x28, starting transfers between devices, swap(): return lax.ppermute(value, axis, [(i, i ^ step) for i in range(size)])  46 us
    pallas_call x4, Pallas kernels, contract(): pl.pallas_call(functools.partial(contract_kernel, spots), out_shape=jax.S...  13.3 us
    dynamic_slice x3, local copies, waits for them, and re-layouts, piece(): lax.dynamic_slice(source, start, (depth, high - low, orbitals, width))  5.81 us
  transfers between devices with their start and end apart: 28, of which 16 were waited for; matrix products, arithmetic and copies ran while one was open for 9% of the time, Pallas kernels for 7%

profile of v6, /device:TPU:0, one launch (start us, length us, event | category | flops | bytes accessed | tf_op | source)
XLA Modules:
  0.0 135.3 jit_solution(1420627545874563521)
XLA Ops:
  0.7 1.0 constant_dynamic-slice_fusion.9
  1.7 3.5 %collective-permute-start.4 = (bf16[12,2,64,128]{3,2,1,0:T(8,128)(2,1)S(1)}, bf16[12,2,64,128]{3,2,1,0:T(8,128)(2,1)S(1)}, u32[]{:S(2)}, u32[]{:S(2)}) collective-permute-start(bf16[12,2,64,128]{3,2,1,0:T(8,128)(2,1)S(1)} %constant_dynamic-slice_fusion.9), channel_id=1, source_target_pairs={{0,20},{4,16},{8,28},{12,24},{16,4},{20,0},{24,12},{28,8},{1,21},{... | collective-permute-start | bytes 1179656 | tf_op jit(solution)/shard_map/ppermute | solution.py:15
  5.2 2.6 %constant_dynamic-slice_fusion = (bf16[12,2,64,128]{3,2,1,0:T(8,128)(2,1)S(1)}, bf16[12,2,64,128]{3,2,1,0:T(8,128)(2,1)S(1)}, bf16[12,2,64,128]{3,2,1,0:T(8,128)...) fusion(bf16[96,2,64,128]{3,2,1,0:T(8,128)(2,1)} %param.6, s32[]{:T(128)S(6)} %select_n.217, ...), kind=kLoop, calls=%fused_computation.44 | loop fusion | bytes 3932180 | tf_op jit(solution)/shard_map/dynamic_slice | solution.py:503
  7.8 1.9 %collective-permute-start.10 = (bf16[12,2,64,128]{3,2,1,0:T(8,128)(2,1)}, bf16[12,2,64,128]{3,2,1,0:T(8,128)(2,1)}, u32[]{:S(2)}, u32[]{:S(2)}) collective-permute-start(bf16[12,2,64,128]{3,2,1,0:T(8,128)(2,1)} %get-tuple-element.115), channel_id=1, source_target_pairs={{0,12},{4,8},{8,4},{12,0},{16,28},{20,24},{24,20},{28,16},{1,13},{... | collective-permute-start | bytes 1179656 | tf_op jit(solution)/shard_map/ppermute | solution.py:15
  13.1 0.7 convert_reduce_fusion.3
  16.6 6.0 %collective-permute-done.4.refs_0_ = bf16[12,2,64,128]{3,2,1,0:T(8,128)(2,1)S(1)} collective-permute-done((bf16[12,2,64,128]{3,2,1,0:T(8,128)(2,1)S(1)}, bf16[12,2,64,128]{3,2,1,0:T(8,128)(2,1)S(1)}, u32[]{:S(2)}, u32[]{:S(2)}) %collective-permute-start.4) | collective-permute-done | bytes 393248 | tf_op jit(solution)/shard_map/ppermute | solution.py:15
  22.6 2.2 %constant_dynamic-slice_fusion.4 = (bf16[12,1,64,128]{3,2,1,0:T(8,128)(2,1)}, bf16[12,1,64,128]{3,2,1,0:T(8,128)(2,1)}, bf16[12,1,64,128]{3,2,1,0:T(8,128)(2,1)S(1)}, bf16[12,1,64,128]{3,2,1,0:T(8,128)(2,1)S(1)}) fusion(bf16[96,2,64,128]{3,2,1,0:T(8,128)(2,1)} %param.6, s32[]{:T(128)S(6)} %select_n.213, s32[]{:T(128)S(6)} %select_n.212), kind=kLoop, calls=%fused_computation.48 | loop fusion | bytes 1572872 | tf_op jit(solution)/shard_map/dynamic_slice | solution.py:503
  24.8 4.9 %collective-permute-start.6 = (bf16[12,1,64,128]{3,2,1,0:T(8,128)(2,1)S(1)}, bf16[12,1,64,128]{3,2,1,0:T(8,128)(2,1)S(1)}, u32[]{:S(2)}, u32[]{:S(2)}) collective-permute-start(bf16[12,1,64,128]{3,2,1,0:T(8,128)(2,1)S(1)} %get-tuple-element.120), channel_id=1, source_target_pairs={{0,24},{4,28},{8,16},{12,20},{16,8},{20,12},{24,0},{28,4},{1,25},{... | collective-permute-start | bytes 589832 | tf_op jit(solution)/shard_map/ppermute | solution.py:15
  29.7 4.4 %collective-permute-done.10.refs_4_.refs_6_ = bf16[12,2,64,128]{3,2,1,0:T(8,128)(2,1)} collective-permute-done((bf16[12,2,64,128]{3,2,1,0:T(8,128)(2,1)}, bf16[12,2,64,128]{3,2,1,0:T(8,128)(2,1)}, u32[]{:S(2)}, u32[]{:S(2)}) %collective-permute-start.10) | collective-permute-done | bytes 393248 | tf_op jit(solution)/shard_map/ppermute | solution.py:15
  34.1 3.8 %collective-permute-start.7 = (bf16[12,1,64,128]{3,2,1,0:T(8,128)(2,1)S(1)}, bf16[12,1,64,128]{3,2,1,0:T(8,128)(2,1)S(1)}, u32[]{:S(2)}, u32[]{:S(2)}) collective-permute-start(bf16[12,1,64,128]{3,2,1,0:T(8,128)(2,1)S(1)} %get-tuple-element.119), channel_id=1, source_target_pairs={{0,28},{4,24},{8,20},{12,16},{16,12},{20,8},{24,4},{28,0},{1,29},{... | collective-permute-start | bytes 589832 | tf_op jit(solution)/shard_map/ppermute | solution.py:15
  37.9 0.8 concatenate.35.refs_8_.table
  38.8 12.9 %collective-permute-done.11.refs_5_.refs_7_ = bf16[12,2,64,128]{3,2,1,0:T(8,128)(2,1)} collective-permute-done((bf16[12,2,64,128]{3,2,1,0:T(8,128)(2,1)}, bf16[12,2,64,128]{3,2,1,0:T(8,128)(2,1)}, u32[]{:S(2)}, u32[]{:S(2)}) %collective-permute-start.11) | collective-permute-done | bytes 393248 | tf_op jit(solution)/shard_map/ppermute | solution.py:15
  52.6 3.2 %shard_map.59.refs_8_ = f32[4,22,32,128]{3,2,1,0:T(8,128)S(1)} custom-call(s32[67]{0:T(128)S(1)} %pad_add_fusion.8.table, bf16[12,2,64,128]{3,2,1,0:T(8,128)(2,1)S(1)} %collective-permute-done.4.refs_0_, bf16[12,2,64,128]{3,2,1,0:T(8,128)(2,1)S(1)} %collective-permute-done.5.refs_1_, bf16[12,1,64,128]{3,2,1,0:T(8,128)(2,1)S(1)} %collective-permute-done.6.refs_2_, ...), custom_call_target="tpu_custom_call" | custom-call | flops 1 | bytes 1 | tf_op jit(solution)/shard_map/pallas_call | solution.py:47
  56.1 3.1 %collective-permute-start.8 = (bf16[12,1,64,128]{3,2,1,0:T(8,128)(2,1)}, bf16[12,1,64,128]{3,2,1,0:T(8,128)(2,1)S(1)}, u32[]{:S(2)}, u32[]{:S(2)}) collective-permute-start(bf16[12,1,64,128]{3,2,1,0:T(8,128)(2,1)} %get-tuple-element.118), channel_id=1, source_target_pairs={{0,24},{4,28},{8,16},{12,20},{16,8},{20,12},{24,0},{28,4},{1,25},{... | collective-permute-start | bytes 589832 | tf_op jit(solution)/shard_map/ppermute | solution.py:15
  59.9 3.6 %shard_map.60.kept = f32[4,22,32,128]{3,2,1,0:T(8,128)S(1)} custom-call(s32[67]{0:T(128)S(1)} %pad_add_fusion.7.table, bf16[12,2,64,128]{3,2,1,0:T(8,128)(2,1)} %copy-done, bf16[12,2,64,128]{3,2,1,0:T(8,128)(2,1)} %copy-done.5, bf16[12,1,64,128]{3,2,1,0:T(8,128)(2,1)S(1)} %collective-permute-done.6.refs_2_, bf16[12,1,64,128]{3,2,1,0:T(8,128)(2,1)} %copy-done.8, ...), custom_call_target="tpu_custom_call" | custom-call | flops 1 | bytes 1 | tf_op jit(solution)/shard_map/pallas_call | solution.py:47
  63.5 0.7 shard_map.61
  64.3 1.5 %collective-permute-done.8.refs_4_ = bf16[12,1,64,128]{3,2,1,0:T(8,128)(2,1)S(1)} collective-permute-done((bf16[12,1,64,128]{3,2,1,0:T(8,128)(2,1)}, bf16[12,1,64,128]{3,2,1,0:T(8,128)(2,1)S(1)}, u32[]{:S(2)}, u32[]{:S(2)}) %collective-permute-start.8) | collective-permute-done | bytes 196640 | tf_op jit(solution)/shard_map/ppermute | solution.py:15
  65.8 3.5 %collective-permute-done.9.refs_5_ = bf16[12,1,64,128]{3,2,1,0:T(8,128)(2,1)S(1)} collective-permute-done((bf16[12,1,64,128]{3,2,1,0:T(8,128)(2,1)}, bf16[12,1,64,128]{3,2,1,0:T(8,128)(2,1)S(1)}, u32[]{:S(2)}, u32[]{:S(2)}) %collective-permute-start.9) | collective-permute-done | bytes 196640 | tf_op jit(solution)/shard_map/ppermute | solution.py:15
  69.4 3.0 %shard_map.62.refs_10_ = f32[4,18,32,128]{3,2,1,0:T(8,128)S(1)} custom-call(s32[55]{0:T(128)S(1)} %pad_add_fusion.10.table, bf16[12,2,64,128]{3,2,1,0:T(8,128)(2,1)S(1)} %copy-done.1, bf16[12,2,64,128]{3,2,1,0:T(8,128)(2,1)S(1)} %copy-done.6, bf16[12,1,64,128]{3,2,1,0:T(8,128)(2,1)S(1)} %collective-permute-done.6.refs_2_, ...), custom_call_target="tpu_custom_call" | custom-call | flops 1 | bytes 1 | tf_op jit(solution)/shard_map/pallas_call | solution.py:47
  72.6 2.1 %collective-permute-start.14 = (s16[23,32,128]{2,1,0:T(8,128)(2,1)S(1)}, s16[23,32,128]{2,1,0:T(8,128)(2,1)}, u32[]{:S(2)}, u32[]{:S(2)}) collective-permute-start(s16[23,32,128]{2,1,0:T(8,128)(2,1)S(1)} %get-tuple-element.89), channel_id=1, source_target_pairs={{0,1},{1,0},{2,3},{3,2},{4,5},{5,4},{6,7},{7,6},{8,9},{9,8},{10,11... | collective-permute-start | bytes 565256 | tf_op jit(solution)/shard_map/ppermute | solution.py:15
  74.9 1.5 %collective-permute-start.15 = (s16[23,32,128]{2,1,0:T(8,128)(2,1)S(1)}, s16[23,32,128]{2,1,0:T(8,128)(2,1)S(1)}, u32[]{:S(2)}, u32[]{:S(2)}) collective-permute-start(s16[23,32,128]{2,1,0:T(8,128)(2,1)S(1)} %get-tuple-element.90), channel_id=1, source_target_pairs={{0,2},{1,3},{2,0},{3,1},{4,6},{5,7},{6,4},{7,5},{8,10},{9,11},{10,... | collective-permute-start | bytes 565256 | tf_op jit(solution)/shard_map/ppermute | solution.py:15
  76.5 3.5 %shard_map.63.kept = f32[4,18,32,128]{3,2,1,0:T(8,128)S(1)} custom-call(s32[55]{0:T(128)S(1)} %pad_add_fusion.9.table, bf16[12,2,64,128]{3,2,1,0:T(8,128)(2,1)} %copy-done, bf16[12,2,64,128]{3,2,1,0:T(8,128)(2,1)} %copy-done.5, bf16[12,1,64,128]{3,2,1,0:T(8,128)(2,1)S(1)} %collective-permute-done.6.refs_2_, bf16[12,1,64,128]{3,2,1,0:T(8,128)(2,1)} %copy-done.8, ...), custom_call_target="tpu_custom_call" | custom-call | flops 1 | bytes 1 | tf_op jit(solution)/shard_map/pallas_call | solution.py:47
  80.1 1.2 shard_map.64
  81.3 2.0 %collective-permute-start.18 = (s16[19,32,128]{2,1,0:T(8,128)(2,1)S(1)}, s16[19,32,128]{2,1,0:T(8,128)(2,1)S(1)}, u32[]{:S(2)}, u32[]{:S(2)}) collective-permute-start(s16[19,32,128]{2,1,0:T(8,128)(2,1)S(1)} %get-tuple-element.93), channel_id=1, source_target_pairs={{0,1},{1,0},{2,3},{3,2},{4,5},{5,4},{6,7},{7,6},{8,9},{9,8},{10,11... | collective-permute-start | bytes 466952 | tf_op jit(solution)/shard_map/ppermute | solution.py:15
  83.2 1.5 %collective-permute-start.19 = (s16[19,32,128]{2,1,0:T(8,128)(2,1)S(1)}, s16[19,32,128]{2,1,0:T(8,128)(2,1)S(1)}, u32[]{:S(2)}, u32[]{:S(2)}) collective-permute-start(s16[19,32,128]{2,1,0:T(8,128)(2,1)S(1)} %get-tuple-element.94), channel_id=1, source_target_pairs={{0,2},{1,3},{2,0},{3,1},{4,6},{5,7},{6,4},{7,5},{8,10},{9,11},{10,... | collective-permute-start | bytes 466952 | tf_op jit(solution)/shard_map/ppermute | solution.py:15
  84.8 1.0 collective-permute-done.15
  85.8 2.4 %collective-permute-done.18 = s16[19,32,128]{2,1,0:T(8,128)(2,1)S(1)} collective-permute-done((s16[19,32,128]{2,1,0:T(8,128)(2,1)S(1)}, s16[19,32,128]{2,1,0:T(8,128)(2,1)S(1)}, u32[]{:S(2)}, u32[]{:S(2)}) %collective-permute-start.18) | collective-permute-done | bytes 155680 | tf_op jit(solution)/shard_map/ppermute | solution.py:15
  88.2 4.0 %collective-permute-done.19 = s16[19,32,128]{2,1,0:T(8,128)(2,1)S(1)} collective-permute-done((s16[19,32,128]{2,1,0:T(8,128)(2,1)S(1)}, s16[19,32,128]{2,1,0:T(8,128)(2,1)S(1)}, u32[]{:S(2)}, u32[]{:S(2)}) %collective-permute-start.19) | collective-permute-done | bytes 155680 | tf_op jit(solution)/shard_map/ppermute | solution.py:15
  92.3 2.4 %conditional.1 = ((f32[10,32,128]{2,1,0:T(8,128)S(1)}, s16[11,32,128]{2,1,0:T(8,128)(2,1)S(1)}, s16[11,32,128]{2,1,0:T(8,128)(2,1)S(1)}, s16[11,32,128]{2,1,0:T(8,128)(2,1)S(1)})) conditional(s32[]{:T(128)} %convert_element_type.65, (s32[4,40]{1,0:T(4,128)S(1)}, s32[]{:T(128)}, s32[4,40]{1,0:T(4,128)S(1)}, bf16[12,2,64,128]{3,2,1,0:T(8,128)(2,1)}, ...), branch_computations={%region_16.17_spmd, %region_17.18_spmd} | conditional | flops 246 | bytes 16978228 | solution.py:537
  92.3 2.4 %branch_1_fun.1 = (f32[10,32,128]{2,1,0:T(8,128)S(1)}, s16[11,32,128]{2,1,0:T(8,128)(2,1)S(1)}, s16[11,32,128]{2,1,0:T(8,128)(2,1)S(1)}, s16[11,32,128]{2,1,0:T(8,128)(2,1)S(1)}) custom-call(s32[40]{0:T(128)S(1)} %slice_bitcast_fusion.1.refs_0_, f32[22,32,128]{2,1,0:T(8,128)} %get-tuple-element.62.refs_1_, s16[23,32,128]{2,1,0:T(8,128)(2,1)} %get-tuple-element.63.refs_2_, ...), custom_call_target="tpu_custom_call" | custom-call | flops 1 | bytes 1 | tf_op jit(solution)/shard_map/cond/branch_1_fun/pallas_call | solution.py:215
  94.6 9.3 %collective-permute-start.21 = (s16[11,32,128]{2,1,0:T(8,128)(2,1)S(1)}, s16[11,32,128]{2,1,0:T(8,128)(2,1)S(1)}, u32[]{:S(2)}, u32[]{:S(2)}) collective-permute-start(s16[11,32,128]{2,1,0:T(8,128)(2,1)S(1)} %get-tuple-element.97), channel_id=1, source_target_pairs={{0,8},{4,12},{8,0},{12,4},{16,24},{20,28},{24,16},{28,20},{1,9},{5... | collective-permute-start | bytes 270344 | tf_op jit(solution)/shard_map/ppermute | solution.py:15
  103.9 1.1 collective-permute-start.22
  105.1 1.4 %collective-permute-start.23 = (s16[11,32,128]{2,1,0:T(8,128)(2,1)S(1)}, s16[11,32,128]{2,1,0:T(8,128)(2,1)S(1)}, u32[]{:S(2)}, u32[]{:S(2)}) collective-permute-start(s16[11,32,128]{2,1,0:T(8,128)(2,1)S(1)} %get-tuple-element.99), channel_id=1, source_target_pairs={{0,24},{4,28},{8,16},{12,20},{16,8},{20,12},{24,0},{28,4},{1,25},{... | collective-permute-start | bytes 270344 | tf_op jit(solution)/shard_map/ppermute | solution.py:15
  106.5 0.9 collective-permute-done.21.refs_1_
  107.4 5.4 %collective-permute-done.22.refs_2_ = s16[11,32,128]{2,1,0:T(8,128)(2,1)S(1)} collective-permute-done((s16[11,32,128]{2,1,0:T(8,128)(2,1)S(1)}, s16[11,32,128]{2,1,0:T(8,128)(2,1)S(1)}, u32[]{:S(2)}, u32[]{:S(2)}) %collective-permute-start.22) | collective-permute-done | bytes 90144 | tf_op jit(solution)/shard_map/ppermute | solution.py:15
  113.0 1.6 %collective-permute-start.24 = (s16[11,32,128]{2,1,0:T(8,128)(2,1)S(1)}, s16[11,32,128]{2,1,0:T(8,128)(2,1)S(1)}, u32[]{:S(2)}, u32[]{:S(2)}) collective-permute-start(s16[11,32,128]{2,1,0:T(8,128)(2,1)S(1)} %shard_map.65.refs_0_), channel_id=1, source_target_pairs={{0,8},{4,12},{8,0},{12,4},{16,24},{20,28},{24,16},{28,20},{1,9},{5... | collective-permute-start | bytes 270344 | tf_op jit(solution)/shard_map/ppermute | solution.py:15
  114.5 1.3 collective-permute-start.25
  115.9 1.5 %collective-permute-start.26 = (s16[11,32,128]{2,1,0:T(8,128)(2,1)S(1)}, s16[11,32,128]{2,1,0:T(8,128)(2,1)S(1)}, u32[]{:S(2)}, u32[]{:S(2)}) collective-permute-start(s16[11,32,128]{2,1,0:T(8,128)(2,1)S(1)} %shard_map.65.refs_0_), channel_id=1, source_target_pairs={{0,24},{4,28},{8,16},{12,20},{16,8},{20,12},{24,0},{28,4},{1,25},{... | collective-permute-start | bytes 270344 | tf_op jit(solution)/shard_map/ppermute | solution.py:15
  117.4 0.8 collective-permute-done.24.refs_1_
  118.2 4.8 %collective-permute-done.25.refs_2_ = s16[11,32,128]{2,1,0:T(8,128)(2,1)S(1)} collective-permute-done((s16[11,32,128]{2,1,0:T(8,128)(2,1)S(1)}, s16[11,32,128]{2,1,0:T(8,128)(2,1)S(1)}, u32[]{:S(2)}, u32[]{:S(2)}) %collective-permute-start.25) | collective-permute-done | bytes 90144 | tf_op jit(solution)/shard_map/ppermute | solution.py:15
  123.0 0.9 shard_map.66
  123.9 1.8 %collective-permute-start.28 = (s16[11,32,128]{2,1,0:T(8,128)(2,1)S(1)}, s16[11,32,128]{2,1,0:T(8,128)(2,1)S(1)}, u32[]{:S(2)}, u32[]{:S(2)}) collective-permute-start(s16[11,32,128]{2,1,0:T(8,128)(2,1)S(1)} %get-tuple-element.124), channel_id=1, source_target_pairs={{0,1},{1,0},{2,3},{3,2},{4,5},{5,4},{6,7},{7,6},{8,9},{9,8},{10,11... | collective-permute-start | bytes 270344 | tf_op jit(solution)/shard_map/ppermute | solution.py:15
  126.2 1.4 %collective-permute-start.30 = (s16[11,32,128]{2,1,0:T(8,128)(2,1)S(1)}, s16[11,32,128]{2,1,0:T(8,128)(2,1)S(1)}, u32[]{:S(2)}, u32[]{:S(2)}) collective-permute-start(s16[11,32,128]{2,1,0:T(8,128)(2,1)S(1)} %get-tuple-element.122), channel_id=1, source_target_pairs={{0,3},{1,2},{2,1},{3,0},{4,7},{5,6},{6,5},{7,4},{8,11},{9,10},{10,... | collective-permute-start | bytes 270344 | tf_op jit(solution)/shard_map/ppermute | solution.py:15
  127.8 0.8 collective-permute-done.28
  128.5 1.7 %collective-permute-done.29 = s16[11,32,128]{2,1,0:T(8,128)(2,1)S(1)} collective-permute-done((s16[11,32,128]{2,1,0:T(8,128)(2,1)S(1)}, s16[11,32,128]{2,1,0:T(8,128)(2,1)S(1)}, u32[]{:S(2)}, u32[]{:S(2)}) %collective-permute-start.29) | collective-permute-done | bytes 90144 | tf_op jit(solution)/shard_map/ppermute | solution.py:15
  130.3 1.4 %collective-permute-done.30 = s16[11,32,128]{2,1,0:T(8,128)(2,1)S(1)} collective-permute-done((s16[11,32,128]{2,1,0:T(8,128)(2,1)S(1)}, s16[11,32,128]{2,1,0:T(8,128)(2,1)S(1)}, u32[]{:S(2)}, u32[]{:S(2)}) %collective-permute-start.30) | collective-permute-done | bytes 90144 | tf_op jit(solution)/shard_map/ppermute | solution.py:15
  131.9 1.6 %collective-permute-done.31.refs_2_ = s16[4,11,32,128]{3,2,1,0:T(8,128)(2,1)S(1)} collective-permute-done((s16[4,11,32,128]{3,2,1,0:T(8,128)(2,1)S(1)}, s16[4,11,32,128]{3,2,1,0:T(8,128)(2,1)S(1)}, u32[]{:S(2)}, u32[]{:S(2)}) %collective-permute-start.31) | collective-permute-done | bytes 360480 | tf_op jit(solution)/shard_map/ppermute | solution.py:15
  133.4 1.9 %shard_map.67 = (f32[2,32,2048]{2,1,0:T(8,128)}, f32[1,40,32,128]{3,2,1,0:T(8,128)}) custom-call(s32[213]{0:T(256)S(1)} %concatenate.35.refs_8_.table, s16[88,32,128]{2,1,0:T(8,128)(2,1)S(1)} %bitcast.38, s16[4,11,32,128]{3,2,1,0:T(8,128)(2,1)S(1)} %pad_add_fusion.3.refs_1_, s16[4,11,32,128]{3,2,1,0:T(8,128)(2,1)S(1)} %collective-permute-done.31.refs_2_), custom_call_target="tpu_custom_call" | custom-call | flops 1 | bytes 1 | tf_op jit(solution)/shard_map/pallas_call | solution.py:387
  (120 shorter events, 8.9 us)
Async XLA Ops:
  0.6 9.8 %copy-start.13 = (s32[80,2]{0,1:T(2,128)S(1)}, s32[80,2]{0,1:T(2,128)}, u32[]{:S(2)}) copy-start(s32[80,2]{0,1:T(2,128)} %param.7) | copy-start | bytes 1924
  0.6 9.8 %copy-start.14 = (s32[80]{0:T(128)S(1)}, s32[80]{0:T(128)}, u32[]{:S(2)}) copy-start(s32[80]{0:T(128)} %param.9) | copy-start | bytes 964
  0.7 11.2 %copy-start.15 = (s32[80,1]{0,1:T(1,128)S(1)}, s32[80,1]{0,1:T(1,128)}, u32[]{:S(2)}) copy-start(s32[80,1]{0,1:T(1,128)} %param.8) | copy-start | bytes 964
  1.7 20.9 %collective-permute-start.4 = (bf16[12,2,64,128]{3,2,1,0:T(8,128)(2,1)S(1)}, bf16[12,2,64,128]{3,2,1,0:T(8,128)(2,1)S(1)}, u32[]{:S(2)}, u32[]{:S(2)}) collective-permute-start(bf16[12,2,64,128]{3,2,1,0:T(8,128)(2,1)S(1)} %constant_dynamic-slice_fusion.9), channel_id=1, source_target_pairs={{0,20},{4,16},{8,28},{12,24},{16,4},{20,0},{24,12},{28,8},{1,21},{... | collective-permute-start | bytes 1179656 | tf_op jit(solution)/shard_map/ppermute | solution.py:15
  7.8 26.3 %collective-permute-start.10 = (bf16[12,2,64,128]{3,2,1,0:T(8,128)(2,1)}, bf16[12,2,64,128]{3,2,1,0:T(8,128)(2,1)}, u32[]{:S(2)}, u32[]{:S(2)}) collective-permute-start(bf16[12,2,64,128]{3,2,1,0:T(8,128)(2,1)} %get-tuple-element.115), channel_id=1, source_target_pairs={{0,12},{4,8},{8,4},{12,0},{16,28},{20,24},{24,20},{28,16},{1,13},{... | collective-permute-start | bytes 1179656 | tf_op jit(solution)/shard_map/ppermute | solution.py:15
  9.7 42.0 %collective-permute-start.11 = (bf16[12,2,64,128]{3,2,1,0:T(8,128)(2,1)}, bf16[12,2,64,128]{3,2,1,0:T(8,128)(2,1)}, u32[]{:S(2)}, u32[]{:S(2)}) collective-permute-start(bf16[12,2,64,128]{3,2,1,0:T(8,128)(2,1)} %get-tuple-element.114), channel_id=1, source_target_pairs={{0,8},{4,12},{8,0},{12,4},{16,24},{20,28},{24,16},{28,20},{1,9},{5... | collective-permute-start | bytes 1179656 | tf_op jit(solution)/shard_map/ppermute | solution.py:15
  10.2 41.5 %collective-permute-start.12 = (bf16[12,2,64,128]{3,2,1,0:T(8,128)(2,1)S(1)}, bf16[12,2,64,128]{3,2,1,0:T(8,128)(2,1)S(1)}, u32[]{:S(2)}, u32[]{:S(2)}) collective-permute-start(bf16[12,2,64,128]{3,2,1,0:T(8,128)(2,1)S(1)} %get-tuple-element.113), channel_id=1, source_target_pairs={{0,4},{4,0},{8,12},{12,8},{16,20},{20,16},{24,28},{28,24},{1,5},{5... | collective-permute-start | bytes 1179656 | tf_op jit(solution)/shard_map/ppermute | solution.py:15
  10.2 41.5 %collective-permute-start.5 = (bf16[12,2,64,128]{3,2,1,0:T(8,128)(2,1)S(1)}, bf16[12,2,64,128]{3,2,1,0:T(8,128)(2,1)S(1)}, u32[]{:S(2)}, u32[]{:S(2)}) collective-permute-start(bf16[12,2,64,128]{3,2,1,0:T(8,128)(2,1)S(1)} %get-tuple-element.116), channel_id=1, source_target_pairs={{0,16},{4,20},{8,24},{12,28},{16,0},{20,4},{24,8},{28,12},{1,17},{... | collective-permute-start | bytes 1179656 | tf_op jit(solution)/shard_map/ppermute | solution.py:15
  22.6 29.1 %copy-start = (bf16[12,2,64,128]{3,2,1,0:T(8,128)(2,1)}, bf16[12,2,64,128]{3,2,1,0:T(8,128)(2,1)S(1)}, u32[]{:S(2)}) copy-start(bf16[12,2,64,128]{3,2,1,0:T(8,128)(2,1)S(1)} %collective-permute-done.4.refs_0_) | copy-start | bytes 1179652
  24.8 26.9 %collective-permute-start.6 = (bf16[12,1,64,128]{3,2,1,0:T(8,128)(2,1)S(1)}, bf16[12,1,64,128]{3,2,1,0:T(8,128)(2,1)S(1)}, u32[]{:S(2)}, u32[]{:S(2)}) collective-permute-start(bf16[12,1,64,128]{3,2,1,0:T(8,128)(2,1)S(1)} %get-tuple-element.120), channel_id=1, source_target_pairs={{0,24},{4,28},{8,16},{12,20},{16,8},{20,12},{24,0},{28,4},{1,25},{... | collective-permute-start | bytes 589832 | tf_op jit(solution)/shard_map/ppermute | solution.py:15
  34.1 17.6 %collective-permute-start.7 = (bf16[12,1,64,128]{3,2,1,0:T(8,128)(2,1)S(1)}, bf16[12,1,64,128]{3,2,1,0:T(8,128)(2,1)S(1)}, u32[]{:S(2)}, u32[]{:S(2)}) collective-permute-start(bf16[12,1,64,128]{3,2,1,0:T(8,128)(2,1)S(1)} %get-tuple-element.119), channel_id=1, source_target_pairs={{0,28},{4,24},{8,20},{12,16},{16,12},{20,8},{24,4},{28,0},{1,29},{... | collective-permute-start | bytes 589832 | tf_op jit(solution)/shard_map/ppermute | solution.py:15
  51.7 0.7 copy-start.3
  51.7 0.9 copy-start.5
  51.7 0.9 copy-start.8
  55.8 7.7 %collective-permute-start.13 = (f32[4,22,32,128]{3,2,1,0:T(8,128)S(1)}, f32[4,22,32,128]{3,2,1,0:T(8,128)S(1)}, u32[]{:S(2)}, u32[]{:S(2)}) collective-permute-start(f32[4,22,32,128]{3,2,1,0:T(8,128)S(1)} %shard_map.59.refs_8_), channel_id=1, source_target_pairs={{0,4},{4,0},{8,12},{12,8},{16,20},{20,16},{24,28},{28,24},{1,5},{5... | collective-permute-start | bytes 4325384 | tf_op jit(solution)/shard_map/ppermute | solution.py:15
  56.1 9.7 %collective-permute-start.8 = (bf16[12,1,64,128]{3,2,1,0:T(8,128)(2,1)}, bf16[12,1,64,128]{3,2,1,0:T(8,128)(2,1)S(1)}, u32[]{:S(2)}, u32[]{:S(2)}) collective-permute-start(bf16[12,1,64,128]{3,2,1,0:T(8,128)(2,1)} %get-tuple-element.118), channel_id=1, source_target_pairs={{0,24},{4,28},{8,16},{12,20},{16,8},{20,12},{24,0},{28,4},{1,25},{... | collective-permute-start | bytes 589832 | tf_op jit(solution)/shard_map/ppermute | solution.py:15
  59.2 10.1 %collective-permute-start.9 = (bf16[12,1,64,128]{3,2,1,0:T(8,128)(2,1)}, bf16[12,1,64,128]{3,2,1,0:T(8,128)(2,1)S(1)}, u32[]{:S(2)}, u32[]{:S(2)}) collective-permute-start(bf16[12,1,64,128]{3,2,1,0:T(8,128)(2,1)} %get-tuple-element.117), channel_id=1, source_target_pairs={{0,28},{4,24},{8,20},{12,16},{16,12},{20,8},{24,4},{28,0},{1,29},{... | collective-permute-start | bytes 589832 | tf_op jit(solution)/shard_map/ppermute | solution.py:15
  63.5 5.9 %copy-start.1 = (bf16[12,2,64,128]{3,2,1,0:T(8,128)(2,1)S(1)}, bf16[12,2,64,128]{3,2,1,0:T(8,128)(2,1)}, u32[]{:S(2)}) copy-start(bf16[12,2,64,128]{3,2,1,0:T(8,128)(2,1)} %copy-done) | copy-start | bytes 1179652
  63.5 5.8 %copy-start.4 = (bf16[12,2,64,128]{3,2,1,0:T(8,128)(2,1)S(1)}, bf16[12,2,64,128]{3,2,1,0:T(8,128)(2,1)}, u32[]{:S(2)}) copy-start(bf16[12,2,64,128]{3,2,1,0:T(8,128)(2,1)} %copy-done.3) | copy-start | bytes 1179652
  63.5 5.8 %copy-start.6 = (bf16[12,2,64,128]{3,2,1,0:T(8,128)(2,1)S(1)}, bf16[12,2,64,128]{3,2,1,0:T(8,128)(2,1)}, u32[]{:S(2)}) copy-start(bf16[12,2,64,128]{3,2,1,0:T(8,128)(2,1)} %copy-done.5) | copy-start | bytes 1179652
  63.5 5.8 %copy-start.9 = (bf16[12,1,64,128]{3,2,1,0:T(8,128)(2,1)S(1)}, bf16[12,1,64,128]{3,2,1,0:T(8,128)(2,1)}, u32[]{:S(2)}) copy-start(bf16[12,1,64,128]{3,2,1,0:T(8,128)(2,1)} %copy-done.8) | copy-start | bytes 589828
  64.3 10.5 %copy-start.12 = (f32[22,32,128]{2,1,0:T(8,128)}, f32[22,32,128]{2,1,0:T(8,128)S(1)}, u32[]{:S(2)}) copy-start(f32[22,32,128]{2,1,0:T(8,128)S(1)} %get-tuple-element.88.refs_10_) | copy-start | bytes 1081348
  65.8 8.9 %copy-start.10 = (bf16[12,1,64,128]{3,2,1,0:T(8,128)(2,1)}, bf16[12,1,64,128]{3,2,1,0:T(8,128)(2,1)S(1)}, u32[]{:S(2)}) copy-start(bf16[12,1,64,128]{3,2,1,0:T(8,128)(2,1)S(1)} %collective-permute-done.8.refs_4_) | copy-start | bytes 589828
  69.3 5.4 %copy-start.11 = (bf16[12,1,64,128]{3,2,1,0:T(8,128)(2,1)}, bf16[12,1,64,128]{3,2,1,0:T(8,128)(2,1)S(1)}, u32[]{:S(2)}) copy-start(bf16[12,1,64,128]{3,2,1,0:T(8,128)(2,1)S(1)} %collective-permute-done.9.refs_5_) | copy-start | bytes 589828
  72.3 7.7 %collective-permute-start.17 = (f32[4,18,32,128]{3,2,1,0:T(8,128)S(1)}, f32[4,18,32,128]{3,2,1,0:T(8,128)S(1)}, u32[]{:S(2)}, u32[]{:S(2)}) collective-permute-start(f32[4,18,32,128]{3,2,1,0:T(8,128)S(1)} %shard_map.62.refs_10_), channel_id=1, source_target_pairs={{0,4},{4,0},{8,12},{12,8},{16,20},{20,16},{24,28},{28,24},{1,5},{5... | collective-permute-start | bytes 3538952 | tf_op jit(solution)/shard_map/ppermute | solution.py:15
  72.6 12.1 %collective-permute-start.14 = (s16[23,32,128]{2,1,0:T(8,128)(2,1)S(1)}, s16[23,32,128]{2,1,0:T(8,128)(2,1)}, u32[]{:S(2)}, u32[]{:S(2)}) collective-permute-start(s16[23,32,128]{2,1,0:T(8,128)(2,1)S(1)} %get-tuple-element.89), channel_id=1, source_target_pairs={{0,1},{1,0},{2,3},{3,2},{4,5},{5,4},{6,7},{7,6},{8,9},{9,8},{10,11... | collective-permute-start | bytes 565256 | tf_op jit(solution)/shard_map/ppermute | solution.py:15
  74.9 10.9 %collective-permute-start.15 = (s16[23,32,128]{2,1,0:T(8,128)(2,1)S(1)}, s16[23,32,128]{2,1,0:T(8,128)(2,1)S(1)}, u32[]{:S(2)}, u32[]{:S(2)}) collective-permute-start(s16[23,32,128]{2,1,0:T(8,128)(2,1)S(1)} %get-tuple-element.90), channel_id=1, source_target_pairs={{0,2},{1,3},{2,0},{3,1},{4,6},{5,7},{6,4},{7,5},{8,10},{9,11},{10,... | collective-permute-start | bytes 565256 | tf_op jit(solution)/shard_map/ppermute | solution.py:15
  76.4 9.4 %collective-permute-start.16 = (s16[23,32,128]{2,1,0:T(8,128)(2,1)S(1)}, s16[23,32,128]{2,1,0:T(8,128)(2,1)S(1)}, u32[]{:S(2)}, u32[]{:S(2)}) collective-permute-start(s16[23,32,128]{2,1,0:T(8,128)(2,1)S(1)} %get-tuple-element.91), channel_id=1, source_target_pairs={{0,3},{1,2},{2,1},{3,0},{4,7},{5,6},{6,5},{7,4},{8,11},{9,10},{10,... | collective-permute-start | bytes 565256 | tf_op jit(solution)/shard_map/ppermute | solution.py:15
  81.3 7.0 %collective-permute-start.18 = (s16[19,32,128]{2,1,0:T(8,128)(2,1)S(1)}, s16[19,32,128]{2,1,0:T(8,128)(2,1)S(1)}, u32[]{:S(2)}, u32[]{:S(2)}) collective-permute-start(s16[19,32,128]{2,1,0:T(8,128)(2,1)S(1)} %get-tuple-element.93), channel_id=1, source_target_pairs={{0,1},{1,0},{2,3},{3,2},{4,5},{5,4},{6,7},{7,6},{8,9},{9,8},{10,11... | collective-permute-start | bytes 466952 | tf_op jit(solution)/shard_map/ppermute | solution.py:15
  83.2 9.0 %collective-permute-start.19 = (s16[19,32,128]{2,1,0:T(8,128)(2,1)S(1)}, s16[19,32,128]{2,1,0:T(8,128)(2,1)S(1)}, u32[]{:S(2)}, u32[]{:S(2)}) collective-permute-start(s16[19,32,128]{2,1,0:T(8,128)(2,1)S(1)} %get-tuple-element.94), channel_id=1, source_target_pairs={{0,2},{1,3},{2,0},{3,1},{4,6},{5,7},{6,4},{7,5},{8,10},{9,11},{10,... | collective-permute-start | bytes 466952 | tf_op jit(solution)/shard_map/ppermute | solution.py:15
  84.8 7.5 %collective-permute-start.20 = (s16[19,32,128]{2,1,0:T(8,128)(2,1)S(1)}, s16[19,32,128]{2,1,0:T(8,128)(2,1)S(1)}, u32[]{:S(2)}, u32[]{:S(2)}) collective-permute-start(s16[19,32,128]{2,1,0:T(8,128)(2,1)S(1)} %get-tuple-element.95), channel_id=1, source_target_pairs={{0,3},{1,2},{2,1},{3,0},{4,7},{5,6},{6,5},{7,4},{8,11},{9,10},{10,... | collective-permute-start | bytes 466952 | tf_op jit(solution)/shard_map/ppermute | solution.py:15
  94.6 12.8 %collective-permute-start.21 = (s16[11,32,128]{2,1,0:T(8,128)(2,1)S(1)}, s16[11,32,128]{2,1,0:T(8,128)(2,1)S(1)}, u32[]{:S(2)}, u32[]{:S(2)}) collective-permute-start(s16[11,32,128]{2,1,0:T(8,128)(2,1)S(1)} %get-tuple-element.97), channel_id=1, source_target_pairs={{0,8},{4,12},{8,0},{12,4},{16,24},{20,28},{24,16},{28,20},{1,9},{5... | collective-permute-start | bytes 270344 | tf_op jit(solution)/shard_map/ppermute | solution.py:15
  103.9 8.8 %collective-permute-start.22 = (s16[11,32,128]{2,1,0:T(8,128)(2,1)S(1)}, s16[11,32,128]{2,1,0:T(8,128)(2,1)S(1)}, u32[]{:S(2)}, u32[]{:S(2)}) collective-permute-start(s16[11,32,128]{2,1,0:T(8,128)(2,1)S(1)} %get-tuple-element.98), channel_id=1, source_target_pairs={{0,16},{4,20},{8,24},{12,28},{16,0},{20,4},{24,8},{28,12},{1,17},{... | collective-permute-start | bytes 270344 | tf_op jit(solution)/shard_map/ppermute | solution.py:15
  105.1 7.7 %collective-permute-start.23 = (s16[11,32,128]{2,1,0:T(8,128)(2,1)S(1)}, s16[11,32,128]{2,1,0:T(8,128)(2,1)S(1)}, u32[]{:S(2)}, u32[]{:S(2)}) collective-permute-start(s16[11,32,128]{2,1,0:T(8,128)(2,1)S(1)} %get-tuple-element.99), channel_id=1, source_target_pairs={{0,24},{4,28},{8,16},{12,20},{16,8},{20,12},{24,0},{28,4},{1,25},{... | collective-permute-start | bytes 270344 | tf_op jit(solution)/shard_map/ppermute | solution.py:15
  113.0 5.2 %collective-permute-start.24 = (s16[11,32,128]{2,1,0:T(8,128)(2,1)S(1)}, s16[11,32,128]{2,1,0:T(8,128)(2,1)S(1)}, u32[]{:S(2)}, u32[]{:S(2)}) collective-permute-start(s16[11,32,128]{2,1,0:T(8,128)(2,1)S(1)} %shard_map.65.refs_0_), channel_id=1, source_target_pairs={{0,8},{4,12},{8,0},{12,4},{16,24},{20,28},{24,16},{28,20},{1,9},{5... | collective-permute-start | bytes 270344 | tf_op jit(solution)/shard_map/ppermute | solution.py:15
  114.5 8.5 %collective-permute-start.25 = (s16[11,32,128]{2,1,0:T(8,128)(2,1)S(1)}, s16[11,32,128]{2,1,0:T(8,128)(2,1)S(1)}, u32[]{:S(2)}, u32[]{:S(2)}) collective-permute-start(s16[11,32,128]{2,1,0:T(8,128)(2,1)S(1)} %shard_map.65.refs_0_), channel_id=1, source_target_pairs={{0,16},{4,20},{8,24},{12,28},{16,0},{20,4},{24,8},{28,12},{1,17},{... | collective-permute-start | bytes 270344 | tf_op jit(solution)/shard_map/ppermute | solution.py:15
  115.9 7.1 %collective-permute-start.26 = (s16[11,32,128]{2,1,0:T(8,128)(2,1)S(1)}, s16[11,32,128]{2,1,0:T(8,128)(2,1)S(1)}, u32[]{:S(2)}, u32[]{:S(2)}) collective-permute-start(s16[11,32,128]{2,1,0:T(8,128)(2,1)S(1)} %shard_map.65.refs_0_), channel_id=1, source_target_pairs={{0,24},{4,28},{8,16},{12,20},{16,8},{20,12},{24,0},{28,4},{1,25},{... | collective-permute-start | bytes 270344 | tf_op jit(solution)/shard_map/ppermute | solution.py:15
  123.9 4.6 %collective-permute-start.28 = (s16[11,32,128]{2,1,0:T(8,128)(2,1)S(1)}, s16[11,32,128]{2,1,0:T(8,128)(2,1)S(1)}, u32[]{:S(2)}, u32[]{:S(2)}) collective-permute-start(s16[11,32,128]{2,1,0:T(8,128)(2,1)S(1)} %get-tuple-element.124), channel_id=1, source_target_pairs={{0,1},{1,0},{2,3},{3,2},{4,5},{5,4},{6,7},{7,6},{8,9},{9,8},{10,11... | collective-permute-start | bytes 270344 | tf_op jit(solution)/shard_map/ppermute | solution.py:15
  125.7 4.5 %collective-permute-start.29 = (s16[11,32,128]{2,1,0:T(8,128)(2,1)S(1)}, s16[11,32,128]{2,1,0:T(8,128)(2,1)S(1)}, u32[]{:S(2)}, u32[]{:S(2)}) collective-permute-start(s16[11,32,128]{2,1,0:T(8,128)(2,1)S(1)} %get-tuple-element.123), channel_id=1, source_target_pairs={{0,2},{1,3},{2,0},{3,1},{4,6},{5,7},{6,4},{7,5},{8,10},{9,11},{10,... | collective-permute-start | bytes 270344 | tf_op jit(solution)/shard_map/ppermute | solution.py:15
  126.2 5.4 %collective-permute-start.30 = (s16[11,32,128]{2,1,0:T(8,128)(2,1)S(1)}, s16[11,32,128]{2,1,0:T(8,128)(2,1)S(1)}, u32[]{:S(2)}, u32[]{:S(2)}) collective-permute-start(s16[11,32,128]{2,1,0:T(8,128)(2,1)S(1)} %get-tuple-element.122), channel_id=1, source_target_pairs={{0,3},{1,2},{2,1},{3,0},{4,7},{5,6},{6,5},{7,4},{8,11},{9,10},{10,... | collective-permute-start | bytes 270344 | tf_op jit(solution)/shard_map/ppermute | solution.py:15
  127.7 4.2 %collective-permute-start.27 = (s16[4,11,32,128]{3,2,1,0:T(8,128)(2,1)S(1)}, s16[4,11,32,128]{3,2,1,0:T(8,128)(2,1)S(1)}, u32[]{:S(2)}, u32[]{:S(2)}) collective-permute-start(s16[4,11,32,128]{3,2,1,0:T(8,128)(2,1)S(1)} %pad_add_fusion.2), channel_id=1, source_target_pairs={{0,4},{4,0},{8,12},{12,8},{16,20},{20,16},{24,28},{28,24},{1,5},{5... | collective-permute-start | bytes 1081352 | tf_op jit(solution)/shard_map/ppermute | solution.py:15
  131.7 1.7 %collective-permute-start.31 = (s16[4,11,32,128]{3,2,1,0:T(8,128)(2,1)S(1)}, s16[4,11,32,128]{3,2,1,0:T(8,128)(2,1)S(1)}, u32[]{:S(2)}, u32[]{:S(2)}) collective-permute-start(s16[4,11,32,128]{3,2,1,0:T(8,128)(2,1)S(1)} %pad_add_fusion.3.refs_1_), channel_id=1, source_target_pairs={{0,4},{4,0},{8,12},{12,8},{16,20},{20,16},{24,28},{28,24},{1,5},{5... | collective-permute-start | bytes 1081352 | tf_op jit(solution)/shard_map/ppermute | solution.py:15
